TPU v7x, 256 devices: a whole 4x4x8 slice. The times are simulated.
256 devices in a mesh: row: 16 (over x, y_lo, core), col: 16 (over y_hi, z).
Axes of the slice: x: 4, y: 4 (y_hi: 2, y_lo: 2; y = y_hi * 2 + y_lo), z: 8, core: 2. Of those that a mesh axis runs over, the one named last changes fastest.
Arguments:
- alignment: float32 [128, 768, 64], P('col', 'row'), may hold values from -6 to 6
- pair_rep: float32 [768, 768, 128], P('row', 'col'), may hold values from -6 to 6
- seq_mask: int32 [128], P('col'), may hold values 0 or 1
- res_mask: int32 [768], P('row'), may hold values 0 or 1
- left_weight: float32 [64, 32], replicated, may hold values from -0.75 to 0.75
- right_weight: float32 [64, 32], replicated, may hold values from -0.75 to 0.75
- w_outer: float32 [1024, 128], replicated, may hold values from -4 to 4
- w_logits: float32 [128, 8], replicated, may hold values from -45 to 45
- value_weight: float32 [64, 256], replicated, may hold values from -0.75 to 0.75
- gate_weight: float32 [64, 256], replicated, may hold values from -0.75 to 0.75
- output_weight: float32 [256, 64], replicated, may hold values from -6 to 6
Outputs:
- alignment_out: float32 [128, 768, 64], P('col', 'row')
- pair_out: float32 [768, 768, 128], P('row', 'col')
All inputs are finite; a program needn't handle non-finite values. No bound on the sum of `seq_mask` or of `res_mask` on one device may be relied on, other than what follows from the above.
Results may differ from a plain program's by a relative error of at most 0.0003.
Values sent between devices are 32-bit elements; how exact they have to be, the bound alone decides.
No kernel may reach another device: no remote copies, remote signals or barrier semaphores. Data moves between devices by JAX's collectives and lax.ppermute only.
A program may use at most 128 MiB of HBM per device.

v0:
```python
import functools

import jax
import jax.numpy as jnp
from jax import lax
from jax.experimental import pallas as pl
from jax.experimental.pallas import tpu as pltpu
from jax.sharding import PartitionSpec as P

epsilon = 1e-05
highest = lax.Precision.HIGHEST
f32 = jnp.float32
bf16 = jnp.bfloat16
LANES = 128
Z_CHIPS = 8
ROWS_PER_STEP = 16


def split_two(values):
    high = values.astype(bf16)
    low = (values - high.astype(f32)).astype(bf16)
    return high, low


def mxu(left, right):
    return jnp.dot(left, right, preferred_element_type=f32)


def lane_group(shape, width):
    return lax.broadcasted_iota(jnp.int32, shape, len(shape) - 1) // width


def swap_groups(parts):
    group = lane_group(parts[0].shape, 32)
    upper = group >= 2
    odd = (group % 2) == 1
    first = list(parts)
    for v in (0, 1):
        mixed = pltpu.roll(jnp.where(upper, parts[v], parts[v + 2]), 64, 1)
        first[v] = jnp.where(upper, mixed, parts[v])
        first[v + 2] = jnp.where(upper, parts[v + 2], mixed)
    second = list(first)
    for v in (0, 2):
        second[v] = jnp.where(odd, pltpu.roll(first[v + 1], 32, 1), first[v])
        second[v + 1] = jnp.where(odd, first[v + 1], pltpu.roll(first[v], 96, 1))
    return second


def first_kernel(seq_ref, res_ref, align_ref, weight_ref, left_ref, right_ref, normed_ref, flat_ref, proj):
    seqs, residues, width = align_ref.shape
    values = align_ref[...].reshape(seqs * residues, width)
    center = jnp.mean(values, axis=-1, keepdims=True)
    centred = values - center
    normed = centred * lax.rsqrt(jnp.mean(centred * centred, axis=-1, keepdims=True) + epsilon)
    flat_ref[...] = normed
    for s in range(seqs):
        normed_ref[:, s * width : (s + 1) * width] = normed[s * residues : (s + 1) * residues]
    wide = jnp.dot(normed, weight_ref[...], precision=highest, preferred_element_type=f32)
    proj[0] = wide[:, :LANES]
    proj[1] = wide[:, LANES:]
    lane = lax.broadcasted_iota(jnp.int32, (seqs, LANES), 1)
    sub = lax.broadcasted_iota(jnp.int32, (seqs, LANES), 0)
    seq_live = jnp.zeros((seqs, LANES), f32)
    for s in range(seqs):
        seq_live = jnp.where(sub == s, seq_ref[s].astype(f32), seq_live)
    extra = jnp.where(lane == 64, seq_live, 0.0)
    group = lane // 32
    for quad in range(residues // 4):
        left = jnp.zeros((seqs, LANES), f32)
        right = jnp.zeros((seqs, LANES), f32)
        for g in range(4):
            i = quad * 4 + g
            live = res_ref[i].astype(f32)
            extra = jnp.where(lane == i, live, extra)
            here = group == g
            left = jnp.where(here, proj[0, pl.ds(i, seqs, stride=residues), :] * live, left)
            right = jnp.where(here, proj[1, pl.ds(i, seqs, stride=residues), :] * live, right)
        left_ref[:, quad * LANES : (quad + 1) * LANES] = left * seq_live
        right_ref[:, quad * LANES : (quad + 1) * LANES] = right * seq_live
    right_ref[:, residues * 32 :] = extra


def weights_kernel(outer_ref, value_ref, out_weight_ref, mapped_ref, mixed_ref, out_ref, tall):
    tall[...] = outer_ref[...]
    for b in range(32):
        high, low = split_two(tall[pl.ds(b, 32, stride=32), :])
        mapped_ref[b * 32 : (b + 1) * 32, :LANES] = high
        mapped_ref[b * 32 : (b + 1) * 32, LANES:] = low
    heads = mixed_ref.shape[0]
    values = value_ref[...]
    entry = lax.broadcasted_iota(jnp.int32, (256, LANES), 0)
    group = lane_group((256, LANES), 32)
    within = lax.broadcasted_iota(jnp.int32, (256, LANES), 1) % 32
    for h in range(heads):
        pick = jnp.where(entry == h * 32 + within, 1.0, 0.0)
        tiled = jnp.dot(values, pick, precision=highest, preferred_element_type=f32)
        four = jnp.concatenate([tiled] * 4, axis=0)
        block = jnp.where(entry // 64 == group, four, 0.0)
        high, low = split_two(block)
        mixed_ref[h, :, :LANES] = high
        mixed_ref[h, :, LANES:] = low
    high, low = split_two(out_weight_ref[...])
    out_ref[0] = high
    out_ref[1] = low


def outer_kernel(res_ref, left_ref, right_ref, mapped_ref, pair_ref, head_ref, pair_out_ref, logits_ref, tall, right_two, outer, high_ref, low_ref, seen):
    step = pl.program_id(0)
    cols = 48

    @pl.when(step == 0)
    def _():
        tall[...] = right_ref[:, : cols * 32].T
        for b in range(32):
            high, low = split_two(tall[pl.ds(b, cols, stride=32), :])
            right_two[b * cols : (b + 1) * cols, :LANES] = high
            right_two[b * cols : (b + 1) * cols, LANES:] = low
        extra = right_ref[:, cols * 32 :]
        lane = lax.broadcasted_iota(jnp.int32, (LANES, LANES), 1)
        total = jnp.sum(jnp.where(lane == 64, extra, 0.0))
        live_cols = extra.T[:cols, :1]
        seen[0] = jnp.broadcast_to(live_cols * total, (cols, LANES))
        seen[1] = jnp.broadcast_to((live_cols - 1.0) * 1e9, (cols, LANES))

    left_high, left_low = split_two(left_ref[...])
    both = right_two[...]
    outer[...] = mxu(both, jnp.concatenate([left_high, left_high], axis=0)) + mxu(both[:, :LANES], left_low)
    for quad in range(ROWS_PER_STEP // 4):
        for four in range(8):
            parts = [
                outer[(four * 4 + v) * cols : (four * 4 + v + 1) * cols, quad * LANES : (quad + 1) * LANES]
                for v in range(4)
            ]
            for g, part in enumerate(swap_groups(parts)):
                high, low = split_two(part)
                at = (quad * 4 + g) * cols
                high_ref[at : at + cols, four * LANES : (four + 1) * LANES] = high
                low_ref[at : at + cols, four * LANES : (four + 1) * LANES] = low
    wide = mxu(high_ref[...], mapped_ref[...])
    sums = wide[:, :LANES] + wide[:, LANES:] + mxu(low_ref[...], mapped_ref[:, :LANES])
    head_high, head_low = split_two(head_ref[...])
    head_high = jnp.concatenate([head_high, head_high], axis=0)
    head_low = jnp.concatenate([head_low, head_low], axis=0)
    pairs = []
    for i in range(ROWS_PER_STEP):
        live = res_ref[step * ROWS_PER_STEP + i].astype(f32)
        count = jnp.maximum(seen[0] * live, 1.0)
        pair = pair_ref[i] + sums[i * cols : (i + 1) * cols] / count
        pair_out_ref[i] = pair
        pairs.append(pair)
    pair = jnp.concatenate(pairs, axis=0)
    centred = pair - jnp.mean(pair, axis=-1, keepdims=True)
    normed = centred * lax.rsqrt(jnp.mean(centred * centred, axis=-1, keepdims=True) + epsilon)
    high, low = split_two(normed)
    normed_two = jnp.concatenate([high, low], axis=1)
    logits = mxu(normed_two, head_high) + mxu(normed_two, head_low)
    lane = lax.broadcasted_iota(jnp.int32, (cols, LANES), 1)
    line = jnp.zeros((cols, LANES), f32)
    for i in range(ROWS_PER_STEP):
        line = jnp.where(lane // 8 == i, pltpu.roll(logits[i * cols : (i + 1) * cols], 8 * i, 1) if i else logits[:cols], line)
    logits_ref[...] = line + seen[1]


def middle_kernel(align_normed_ref, normed_ref, gate_ref, turned_high_ref, turned_low_ref, open_ref):
    high, low = split_two(normed_ref[...].T)
    turned_high_ref[...] = high
    turned_low_ref[...] = low
    wide = jnp.dot(align_normed_ref[...], gate_ref[...], precision=highest, preferred_element_type=f32)
    open_ref[...] = jax.nn.sigmoid(wide)


def last_kernel(*refs):
    pieces_in = refs[:Z_CHIPS]
    turned_high_ref, turned_low_ref, mixed_ref, open_ref, out_weight_ref, align_ref, out_ref, held, averaged = refs[Z_CHIPS:]
    heads = mixed_ref.shape[0]
    rows = 48
    me = lax.axis_index("col")
    side, place = me // Z_CHIPS, me % Z_CHIPS
    for k, piece in enumerate(pieces_in):
        at = lax.rem(place + k, Z_CHIPS) * rows
        for other in range(2):
            half = side if other == 0 else 1 - side
            start = pl.multiple_of(half * (Z_CHIPS * rows) + at, 8)
            held[pl.ds(start, rows), :] = piece[other]
    logits = held[...]
    top = jnp.max(logits, axis=0, keepdims=True)
    expo = jnp.exp(logits - top)
    total = jnp.sum(expo, axis=0, keepdims=True)
    high, low = split_two(expo)
    turned_high = turned_high_ref[...]
    summed = mxu(turned_high, high) + mxu(turned_high, low) + mxu(turned_low_ref[...], high)
    turned = (summed / total).T
    for k in range(4):
        averaged[k] = turned[:, k * LANES : (k + 1) * LANES]
    ready = []
    for h in range(heads):
        one = [averaged[k, pl.ds(h, rows, stride=heads), :] for k in range(4)]
        one = jnp.concatenate([jnp.concatenate(one[:2], axis=1), jnp.concatenate(one[2:], axis=1)], axis=0)
        high, low = split_two(one)
        wide = mxu(high, mixed_ref[h])
        ready.append(wide[:, :LANES] + wide[:, LANES:] + mxu(low, mixed_ref[h, :, :LANES]))
    pieces = [[None, None] for _ in range(8)]
    for half in range(2):
        for s, part in enumerate(swap_groups(ready[half * 4 : half * 4 + 4])):
            pieces[s][half] = part[:rows]
            pieces[s + 4][half] = part[rows:]
    merged = jnp.concatenate([jnp.concatenate(p, axis=1) for p in pieces], axis=0)
    high, low = split_two(open_ref[...] * merged)
    result = mxu(high, out_weight_ref[0]) + mxu(high, out_weight_ref[1]) + mxu(low, out_weight_ref[0])
    out_ref[...] = align_ref[...] + result.reshape(out_ref.shape)


def spread(shard, axis):
    devices = lax.axis_size(axis)
    return lax.all_to_all(jnp.broadcast_to(shard[None], (devices, *shard.shape)), axis, 0, 0, tiled=True)


def ring_pieces(shard, axis):
    devices = lax.axis_size(axis)
    ring = Z_CHIPS
    other = lax.ppermute(shard, axis, [(d, (d + ring) % devices) for d in range(devices)])
    ahead = [(d, d // ring * ring + (d + 1) % ring) for d in range(devices)]
    back = [(d, d // ring * ring + (d + ring - 1) % ring) for d in range(devices)]
    pieces = [None] * ring
    pieces[0] = up = down = jnp.stack([shard, other])
    for hop in range(1, ring // 2 + 1):
        up = lax.ppermute(up, axis, ahead)
        pieces[ring - hop] = up
        if hop < ring // 2:
            down = lax.ppermute(down, axis, back)
            pieces[hop] = down
    return pieces


def call(kernel, outs, scratch=(), **more):
    return pl.pallas_call(
        kernel,
        out_shape=outs,
        scratch_shapes=scratch,
        compiler_params=pltpu.CompilerParams(vmem_limit_bytes=48 * 1024 * 1024),
        **more,
    )


def shape(dims, dtype=f32):
    return jax.ShapeDtypeStruct(dims, dtype)


VMEM = pl.BlockSpec(memory_space=pltpu.VMEM)
SMEM = pl.BlockSpec(memory_space=pltpu.SMEM)


def per_device(n_row, n_col, alignment, pair_rep, seq_mask, res_mask, left_weight, right_weight, w_outer, w_logits, value_weight, gate_weight, output_weight):
    seqs, rows, width = alignment.shape
    cols = pair_rep.shape[1]
    pair_width = pair_rep.shape[2]
    four_weights = jnp.concatenate([left_weight] * 4 + [right_weight] * 4, axis=1)
    left, right, normed, normed_flat = call(
        first_kernel,
        (shape((seqs, rows * 32)), shape((seqs, rows * 32 + LANES)), shape((rows, seqs * width)), shape((seqs * rows, width))),
        scratch=[pltpu.VMEM((2, seqs * rows, LANES), f32)],
        in_specs=[SMEM, SMEM, VMEM, VMEM],
    )(seq_mask, res_mask, alignment, four_weights)
    turn = [(r * n_col + c, c * n_col + r) for r in range(n_row) for c in range(n_col)]
    right_here = lax.ppermute(right, ("row", "col"), turn)
    right_all = spread(right_here, "row").reshape(n_row * seqs, -1)
    left_all = spread(left, "col").reshape(n_col * seqs, -1)
    mapped, mixed, out_two = call(
        weights_kernel,
        (shape((1024, 256), bf16), shape((8, 256, 256), bf16), shape((2, 256, 64), bf16)),
        scratch=[pltpu.VMEM((1024, LANES), f32)],
    )(w_outer, value_weight, output_weight)
    head_pad = jnp.pad(w_logits, ((0, 0), (0, LANES - w_logits.shape[1])))
    steps = rows // ROWS_PER_STEP
    pair_out, logits = pl.pallas_call(
        outer_kernel,
        grid=(steps,),
        out_shape=(shape(pair_rep.shape), shape((cols, steps * LANES))),
        in_specs=[
            SMEM,
            pl.BlockSpec((n_col * seqs, ROWS_PER_STEP * 32), lambda t: (0, t)),
            pl.BlockSpec(right_all.shape, lambda t: (0, 0)),
            pl.BlockSpec((1024, 256), lambda t: (0, 0)),
            pl.BlockSpec((ROWS_PER_STEP, cols, pair_width), lambda t: (t, 0, 0)),
            pl.BlockSpec((pair_width, LANES), lambda t: (0, 0)),
        ],
        out_specs=[
            pl.BlockSpec((ROWS_PER_STEP, cols, pair_width), lambda t: (t, 0, 0)),
            pl.BlockSpec((cols, LANES), lambda t: (0, t)),
        ],
        scratch_shapes=[
            pltpu.VMEM((cols * 32, LANES), f32),
            pltpu.VMEM((cols * 32, 256), bf16),
            pltpu.VMEM((cols * 32, ROWS_PER_STEP * 32), f32),
            pltpu.VMEM((ROWS_PER_STEP * cols, 1024), bf16),
            pltpu.VMEM((ROWS_PER_STEP * cols, 1024), bf16),
            pltpu.VMEM((2, cols, LANES), f32),
        ],
        compiler_params=pltpu.CompilerParams(vmem_limit_bytes=48 * 1024 * 1024),
    )(res_mask, left_all, right_all, mapped, pair_rep, head_pad)
    normed_all = lax.all_gather(normed, "row", axis=0, tiled=True)
    turned_high, turned_low, opened = call(
        middle_kernel,
        (shape((seqs * width, n_row * rows), bf16), shape((seqs * width, n_row * rows), bf16), shape((seqs * rows, gate_weight.shape[1]))),
    )(normed_flat, normed_all, gate_weight)
    pieces = ring_pieces(logits, "col")
    alignment_out = call(
        last_kernel,
        shape(alignment.shape),
        scratch=[pltpu.VMEM((n_row * rows, steps * LANES), f32), pltpu.VMEM((4, steps * LANES, LANES), f32)],
    )(*pieces, turned_high, turned_low, mixed, opened, out_two, alignment)
    return alignment_out, pair_out


def solution(mesh):
    in_specs = (
        P("col", "row", None),
        P("row", "col", None),
        P("col"),
        P("row"),
        P(),
        P(),
        P(),
        P(),
        P(),
        P(),
        P(),
    )
    out_specs = (P("col", "row", None), P("row", "col", None))
    body = functools.partial(per_device, mesh.shape["row"], mesh.shape["col"])
    return jax.shard_map(body, mesh=mesh, in_specs=in_specs, out_specs=out_specs, check_vma=False)
```

profile of v0, /device:TPU:2, one launch (start us, length us, event | category | flops | bytes accessed | tf_op | source)
XLA Modules:
  0.0 137.7 jit_solution(8016773713458407206)
XLA Ops:
  7.2 0.8 copy.13
  8.0 0.8 copy.17
  8.8 0.1 concatenate.3.weight_ref
  8.9 0.0 copy-start.4
  8.9 0.9 copy-done.4
  9.8 0.7 copy-done.15
  10.5 0.7 copy-done.17
  11.1 1.8 %shard_map.122 = (f32[8,1536]{1,0:T(8,128)S(1)}, f32[8,1664]{1,0:T(8,128)S(1)}, f32[48,512]{1,0:T(8,128)}, f32[384,64]{1,0:T(8,128)S(1)}) custom-call(s32[8]{0:T(128)S(1)} %copy-done.17, s32[48]{0:T(128)S(1)} %copy-done.15, f32[8,48,64]{2,1,0:T(8,128)S(1)} %copy-done.4, f32[64,256]{1,0:T(8,128)S(1)} %concatenate.3.weight_ref), custom_call_target="tpu_custom_call" | custom-call | tf_op jit(solution)/shard_map/pallas_call | solution.py:258
  13.0 0.7 copy-done.9
  13.7 9.1 %collective-permute-start = (f32[8,1664]{1,0:T(8,128)S(1)}, f32[8,1664]{1,0:T(8,128)S(1)}, u32[]{:S(2)}, u32[]{:S(2)}) collective-permute-start(f32[8,1664]{1,0:T(8,128)S(1)} %get-tuple-element.15), channel_id=1, source_target_pairs={{0,0},{1,16},{2,32},{3,48},{4,64},{5,80},{6,96},{7,112},{8,128},{9... | collective-permute-start | bytes 159752 | tf_op jit(solution)/shard_map/ppermute | solution.py:265
  22.7 2.4 %collective-permute-done = f32[8,1664]{1,0:T(8,128)S(1)} collective-permute-done((f32[8,1664]{1,0:T(8,128)S(1)}, f32[8,1664]{1,0:T(8,128)S(1)}, u32[]{:S(2)}, u32[]{:S(2)}) %collective-permute-start) | collective-permute-done | bytes 53280 | tf_op jit(solution)/shard_map/ppermute | solution.py:265
  25.1 1.0 broadcast_in_dim.5
  26.1 7.6 %all-to-all-start.1 = ((f32[16,8,1664]{2,1,0:T(8,128)}), f32[16,8,1664]{2,1,0:T(8,128)S(1)}, u32[]{:S(2)}, u32[]{:S(2)}) async-start(f32[16,8,1664]{2,1,0:T(8,128)} %broadcast_in_dim.5), calls=%async_computation.1 | async-start | bytes 1703936 | tf_op jit(solution)/shard_map/all_to_all | solution.py:215
  33.7 0.0 all-gather.2.cloned.1.call-start
  33.8 0.7 all-gather.2.cloned.1.call-update
  34.5 11.4 %all-to-all-done.1 = f32[16,8,1664]{2,1,0:T(8,128)S(1)} async-done(((f32[16,8,1664]{2,1,0:T(8,128)}), f32[16,8,1664]{2,1,0:T(8,128)S(1)}, u32[]{:S(2)}, u32[]{:S(2)}) %all-to-all-start.1) | async-done | bytes 852000 | tf_op jit(solution)/shard_map/all_to_all | solution.py:215
  45.8 1.0 broadcast_in_dim.4
  46.8 10.6 %all-to-all-start = ((f32[16,8,1536]{2,1,0:T(8,128)}), f32[16,8,1536]{2,1,0:T(8,128)S(1)}, u32[]{:S(2)}, u32[]{:S(2)}) async-start(f32[16,8,1536]{2,1,0:T(8,128)} %broadcast_in_dim.4), calls=%async_computation | async-start | bytes 1572864 | tf_op jit(solution)/shard_map/all_to_all | solution.py:215
  57.4 0.7 copy.22
  58.1 0.1 copy.21.out_weight_ref
  58.2 0.9 pad.4.head_ref
  59.1 0.0 copy-start.14
  59.1 0.8 copy-done.14
  59.9 1.1 shard_map.123
  61.0 1.0 copy-done.2
  62.0 0.8 copy-done.7
  62.8 0.6 copy-done.11
  63.4 16.7 %all-to-all-done = f32[16,8,1536]{2,1,0:T(8,128)S(1)} async-done(((f32[16,8,1536]{2,1,0:T(8,128)}), f32[16,8,1536]{2,1,0:T(8,128)S(1)}, u32[]{:S(2)}, u32[]{:S(2)}) %all-to-all-start) | async-done | bytes 786464 | tf_op jit(solution)/shard_map/all_to_all | solution.py:215
  80.2 1.0 copy-done.8
  81.2 11.2 %shard_map.124 = (f32[48,48,128]{2,1,0:T(8,128)}, f32[48,384]{1,0:T(8,128)S(1)}) custom-call(s32[48]{0:T(128)S(1)} %copy-done.16, f32[128,1536]{1,0:T(8,128)S(1)} %bitcast.5, f32[128,1664]{1,0:T(8,128)S(1)} %bitcast.4, bf16[1024,256]{1,0:T(8,128)(2,1)S(1)} %copy-done.8, f32[48,48,128]{2,1,0:T(8,128)S(1)} %copy-done.1, f32[128,128]{1,0:T(8,128)S(1)} %pad.4.head_ref), custom_call_target="tpu_custom_call" | custom-call | tf_op jit(solution)/shard_map/pallas_call | solution.py:275
  92.4 0.5 collective-permute-start.1
  93.0 5.3 %collective-permute-done.1 = f32[48,384]{1,0:T(8,128)S(1)} collective-permute-done((f32[48,384]{1,0:T(8,128)S(1)}, f32[48,384]{1,0:T(8,128)S(1)}, u32[]{:S(2)}, u32[]{:S(2)}) %collective-permute-start.1) | collective-permute-done | bytes 73760 | tf_op jit(solution)/shard_map/ppermute | solution.py:221
  98.3 1.6 %collective-permute-start.5 = (f32[2,48,384]{2,1,0:T(8,128)S(1)}, f32[2,48,384]{2,1,0:T(8,128)S(1)}, u32[]{:S(2)}, u32[]{:S(2)}) collective-permute-start(f32[2,48,384]{2,1,0:T(8,128)S(1)} %pad_maximum_fusion.refs_0_), channel_id=1, source_target_pairs={{0,1},{1,2},{2,3},{3,4},{4,5},{5,6},{6,7},{7,0},{8,9},{9,10},{10,1... | collective-permute-start | bytes 442376 | tf_op jit(solution)/shard_map/ppermute | solution.py:227
  99.9 1.7 %collective-permute-start.2 = (f32[2,48,384]{2,1,0:T(8,128)S(1)}, f32[2,48,384]{2,1,0:T(8,128)S(1)}, u32[]{:S(2)}, u32[]{:S(2)}) collective-permute-start(f32[2,48,384]{2,1,0:T(8,128)S(1)} %pad_maximum_fusion.refs_0_), channel_id=1, source_target_pairs={{0,7},{1,0},{2,1},{3,2},{4,3},{5,4},{6,5},{7,6},{8,15},{9,8},{10,9... | collective-permute-start | bytes 442376 | tf_op jit(solution)/shard_map/ppermute | solution.py:230
  101.6 3.8 %collective-permute-done.5.refs_7_ = f32[2,48,384]{2,1,0:T(8,128)S(1)} collective-permute-done((f32[2,48,384]{2,1,0:T(8,128)S(1)}, f32[2,48,384]{2,1,0:T(8,128)S(1)}, u32[]{:S(2)}, u32[]{:S(2)}) %collective-permute-start.5) | collective-permute-done | bytes 147488 | tf_op jit(solution)/shard_map/ppermute | solution.py:227
  105.4 0.9 collective-permute-start.6
  106.3 2.6 %collective-permute-start.3 = (f32[2,48,384]{2,1,0:T(8,128)S(1)}, f32[2,48,384]{2,1,0:T(8,128)S(1)}, u32[]{:S(2)}, u32[]{:S(2)}) collective-permute-start(f32[2,48,384]{2,1,0:T(8,128)S(1)} %collective-permute-done.2.refs_1_), channel_id=1, source_target_pairs={{0,7},{1,0},{2,1},{3,2},{4,3},{5,4},{6,5},{7,6},{8,15},{9,8},{10,9... | collective-permute-start | bytes 442376 | tf_op jit(solution)/shard_map/ppermute | solution.py:230
  109.0 4.2 %collective-permute-done.6.refs_6_ = f32[2,48,384]{2,1,0:T(8,128)S(1)} collective-permute-done((f32[2,48,384]{2,1,0:T(8,128)S(1)}, f32[2,48,384]{2,1,0:T(8,128)S(1)}, u32[]{:S(2)}, u32[]{:S(2)}) %collective-permute-start.6) | collective-permute-done | bytes 147488 | tf_op jit(solution)/shard_map/ppermute | solution.py:227
  113.1 0.0 collective-permute-start.7
  113.1 3.2 %collective-permute-start.4 = (f32[2,48,384]{2,1,0:T(8,128)S(1)}, f32[2,48,384]{2,1,0:T(8,128)S(1)}, u32[]{:S(2)}, u32[]{:S(2)}) collective-permute-start(f32[2,48,384]{2,1,0:T(8,128)S(1)} %collective-permute-done.3.refs_2_), channel_id=1, source_target_pairs={{0,7},{1,0},{2,1},{3,2},{4,3},{5,4},{6,5},{7,6},{8,15},{9,8},{10,9... | collective-permute-start | bytes 442376 | tf_op jit(solution)/shard_map/ppermute | solution.py:230
  116.4 3.6 %collective-permute-done.7.refs_5_ = f32[2,48,384]{2,1,0:T(8,128)S(1)} collective-permute-done((f32[2,48,384]{2,1,0:T(8,128)S(1)}, f32[2,48,384]{2,1,0:T(8,128)S(1)}, u32[]{:S(2)}, u32[]{:S(2)}) %collective-permute-start.7) | collective-permute-done | bytes 147488 | tf_op jit(solution)/shard_map/ppermute | solution.py:227
  120.0 0.0 collective-permute-start.8
  120.0 1.4 %copy-done = f32[768,512]{1,0:T(8,128)S(1)} copy-done((f32[768,512]{1,0:T(8,128)S(1)}, f32[768,512]{1,0:T(8,128)}, u32[]{:S(2)}) %copy-start) | copy-done | bytes 1572888
  121.4 0.5 shard_map.125
  121.9 0.0 collective-permute-done.4.refs_3_
  121.9 4.4 %collective-permute-done.8.refs_4_ = f32[2,48,384]{2,1,0:T(8,128)S(1)} collective-permute-done((f32[2,48,384]{2,1,0:T(8,128)S(1)}, f32[2,48,384]{2,1,0:T(8,128)S(1)}, u32[]{:S(2)}, u32[]{:S(2)}) %collective-permute-start.8) | collective-permute-done | bytes 147488 | tf_op jit(solution)/shard_map/ppermute | solution.py:227
  126.3 1.2 copy-done.3
  127.5 3.3 %shard_map.126 = f32[8,48,64]{2,1,0:T(8,128)} custom-call(f32[2,48,384]{2,1,0:T(8,128)S(1)} %pad_maximum_fusion.refs_0_, f32[2,48,384]{2,1,0:T(8,128)S(1)} %collective-permute-done.2.refs_1_, f32[2,48,384]{2,1,0:T(8,128)S(1)} %collective-permute-done.3.refs_2_, f32[2,48,384]{2,1,0:T(8,128)S(1)} %collective-permute-done.4.refs_3_, ...), custom_call_target="tpu_custom_call" | custom-call | tf_op jit(solution)/shard_map/pallas_call | solution.py:307
  (31 shorter events, 0.1 us)
Async XLA Ops:
  8.9 0.9 copy-start.4
  9.8 0.7 copy-start.15
  10.5 0.7 copy-start.17
  13.0 0.7 copy-start.9
  13.7 11.5 %collective-permute-start = (f32[8,1664]{1,0:T(8,128)S(1)}, f32[8,1664]{1,0:T(8,128)S(1)}, u32[]{:S(2)}, u32[]{:S(2)}) collective-permute-start(f32[8,1664]{1,0:T(8,128)S(1)} %get-tuple-element.15), channel_id=1, source_target_pairs={{0,0},{1,16},{2,32},{3,48},{4,64},{5,80},{6,96},{7,112},{8,128},{9... | collective-permute-start | bytes 159752 | tf_op jit(solution)/shard_map/ppermute | solution.py:265
  26.1 19.8 %all-to-all-start.1 = ((f32[16,8,1664]{2,1,0:T(8,128)}), f32[16,8,1664]{2,1,0:T(8,128)S(1)}, u32[]{:S(2)}, u32[]{:S(2)}) async-start(f32[16,8,1664]{2,1,0:T(8,128)} %broadcast_in_dim.5), calls=%async_computation.1 | async-start | bytes 1703936 | tf_op jit(solution)/shard_map/all_to_all | solution.py:215
  33.7 86.2 %all-gather.2.cloned.1.call-start = ((), (), s32[]{:S(2)}) async-start(), calls=%async_computation.2 | async-start | bytes 1671168 | tf_op jit(solution)/shard_map/all_gather | solution.py:301
  45.8 11.6 %copy-start.19 = (f32[128,8]{0,1:T(8,128)S(1)}, f32[128,8]{0,1:T(8,128)}, u32[]{:S(2)}) copy-start(f32[128,8]{0,1:T(8,128)} %param.18) | copy-start | bytes 12292
  45.8 12.3 %copy-start.18 = (f32[256,64]{0,1:T(8,128)S(1)}, f32[256,64]{0,1:T(8,128)}, u32[]{:S(2)}) copy-start(f32[256,64]{0,1:T(8,128)} %param.21) | copy-start | bytes 196612
  46.8 12.3 %copy-start.6 = (f32[1024,128]{1,0:T(8,128)S(1)}, f32[1024,128]{1,0:T(8,128)}, u32[]{:S(2)}) copy-start(f32[1024,128]{1,0:T(8,128)} %outer_ref.1) | copy-start | bytes 1572868
  46.8 33.4 %copy-start.1 = (f32[48,48,128]{2,1,0:T(8,128)S(1)}, f32[48,48,128]{2,1,0:T(8,128)}, u32[]{:S(2)}) copy-start(f32[48,48,128]{2,1,0:T(8,128)} %pair_ref.1) | copy-start | bytes 3538948
  46.8 33.4 %copy-start.16 = (s32[48]{0:T(128)S(1)}, s32[48]{0:T(128)}, u32[]{:S(2)}) copy-start(s32[48]{0:T(128)} %res_ref.3) | copy-start | bytes 580
  46.8 33.4 %all-to-all-start = ((f32[16,8,1536]{2,1,0:T(8,128)}), f32[16,8,1536]{2,1,0:T(8,128)S(1)}, u32[]{:S(2)}, u32[]{:S(2)}) async-start(f32[16,8,1536]{2,1,0:T(8,128)} %broadcast_in_dim.4), calls=%async_computation | async-start | bytes 1572864 | tf_op jit(solution)/shard_map/all_to_all | solution.py:215
  59.1 0.8 copy-start.14
  61.0 1.0 copy-start.2
  62.0 0.8 copy-start.7
  62.8 0.6 copy-start.11
  80.2 1.0 copy-start.8
  81.2 38.7 %copy-start.10 = (f32[384,64]{1,0:T(8,128)S(1)}, f32[384,64]{1,0:T(8,128)}, u32[]{:S(2)}) copy-start(f32[384,64]{1,0:T(8,128)} %copy-done.9) | copy-start | bytes 294916
  81.2 38.8 %copy-start.13 = (f32[64,256]{1,0:T(8,128)S(1)}, f32[64,256]{1,0:T(8,128)}, u32[]{:S(2)}) copy-start(f32[64,256]{1,0:T(8,128)} %gate_ref.1) | copy-start | bytes 196612
  81.2 45.1 %copy-start.12 = (bf16[2,256,64]{2,1,0:T(8,128)(2,1)S(1)}, bf16[2,256,64]{2,1,0:T(8,128)(2,1)}, u32[]{:S(2)}) copy-start(bf16[2,256,64]{2,1,0:T(8,128)(2,1)} %copy-done.11) | copy-start | bytes 196612
  92.4 33.9 %copy-start.5 = (f32[8,48,64]{2,1,0:T(8,128)S(1)}, f32[8,48,64]{2,1,0:T(8,128)}, u32[]{:S(2)}) copy-start(f32[8,48,64]{2,1,0:T(8,128)} %refs_13_.1) | copy-start | bytes 294916
  92.4 5.9 %collective-permute-start.1 = (f32[48,384]{1,0:T(8,128)S(1)}, f32[48,384]{1,0:T(8,128)S(1)}, u32[]{:S(2)}, u32[]{:S(2)}) collective-permute-start(f32[48,384]{1,0:T(8,128)S(1)} %get-tuple-element.17), channel_id=1, source_target_pairs={{0,8},{1,9},{2,10},{3,11},{4,12},{5,13},{6,14},{7,15},{8,0},{9,1},... | collective-permute-start | bytes 221192 | tf_op jit(solution)/shard_map/ppermute | solution.py:221
  98.3 7.1 %collective-permute-start.5 = (f32[2,48,384]{2,1,0:T(8,128)S(1)}, f32[2,48,384]{2,1,0:T(8,128)S(1)}, u32[]{:S(2)}, u32[]{:S(2)}) collective-permute-start(f32[2,48,384]{2,1,0:T(8,128)S(1)} %pad_maximum_fusion.refs_0_), channel_id=1, source_target_pairs={{0,1},{1,2},{2,3},{3,4},{4,5},{5,6},{6,7},{7,0},{8,9},{9,10},{10,1... | collective-permute-start | bytes 442376 | tf_op jit(solution)/shard_map/ppermute | solution.py:227
  99.9 6.4 %collective-permute-start.2 = (f32[2,48,384]{2,1,0:T(8,128)S(1)}, f32[2,48,384]{2,1,0:T(8,128)S(1)}, u32[]{:S(2)}, u32[]{:S(2)}) collective-permute-start(f32[2,48,384]{2,1,0:T(8,128)S(1)} %pad_maximum_fusion.refs_0_), channel_id=1, source_target_pairs={{0,7},{1,0},{2,1},{3,2},{4,3},{5,4},{6,5},{7,6},{8,15},{9,8},{10,9... | collective-permute-start | bytes 442376 | tf_op jit(solution)/shard_map/ppermute | solution.py:230
  105.4 7.7 %collective-permute-start.6 = (f32[2,48,384]{2,1,0:T(8,128)S(1)}, f32[2,48,384]{2,1,0:T(8,128)S(1)}, u32[]{:S(2)}, u32[]{:S(2)}) collective-permute-start(f32[2,48,384]{2,1,0:T(8,128)S(1)} %collective-permute-done.5.refs_7_), channel_id=1, source_target_pairs={{0,1},{1,2},{2,3},{3,4},{4,5},{5,6},{6,7},{7,0},{8,9},{9,10},{10,1... | collective-permute-start | bytes 442376 | tf_op jit(solution)/shard_map/ppermute | solution.py:227
  106.3 6.8 %collective-permute-start.3 = (f32[2,48,384]{2,1,0:T(8,128)S(1)}, f32[2,48,384]{2,1,0:T(8,128)S(1)}, u32[]{:S(2)}, u32[]{:S(2)}) collective-permute-start(f32[2,48,384]{2,1,0:T(8,128)S(1)} %collective-permute-done.2.refs_1_), channel_id=1, source_target_pairs={{0,7},{1,0},{2,1},{3,2},{4,3},{5,4},{6,5},{7,6},{8,15},{9,8},{10,9... | collective-permute-start | bytes 442376 | tf_op jit(solution)/shard_map/ppermute | solution.py:230
  113.1 6.8 %collective-permute-start.7 = (f32[2,48,384]{2,1,0:T(8,128)S(1)}, f32[2,48,384]{2,1,0:T(8,128)S(1)}, u32[]{:S(2)}, u32[]{:S(2)}) collective-permute-start(f32[2,48,384]{2,1,0:T(8,128)S(1)} %collective-permute-done.6.refs_6_), channel_id=1, source_target_pairs={{0,1},{1,2},{2,3},{3,4},{4,5},{5,6},{6,7},{7,0},{8,9},{9,10},{10,1... | collective-permute-start | bytes 442376 | tf_op jit(solution)/shard_map/ppermute | solution.py:227
  113.1 8.8 %collective-permute-start.4 = (f32[2,48,384]{2,1,0:T(8,128)S(1)}, f32[2,48,384]{2,1,0:T(8,128)S(1)}, u32[]{:S(2)}, u32[]{:S(2)}) collective-permute-start(f32[2,48,384]{2,1,0:T(8,128)S(1)} %collective-permute-done.3.refs_2_), channel_id=1, source_target_pairs={{0,7},{1,0},{2,1},{3,2},{4,3},{5,4},{6,5},{7,6},{8,15},{9,8},{10,9... | collective-permute-start | bytes 442376 | tf_op jit(solution)/shard_map/ppermute | solution.py:230
  120.0 6.4 %collective-permute-start.8 = (f32[2,48,384]{2,1,0:T(8,128)S(1)}, f32[2,48,384]{2,1,0:T(8,128)S(1)}, u32[]{:S(2)}, u32[]{:S(2)}) collective-permute-start(f32[2,48,384]{2,1,0:T(8,128)S(1)} %collective-permute-done.7.refs_5_), channel_id=1, source_target_pairs={{0,1},{1,2},{2,3},{3,4},{4,5},{5,6},{6,7},{7,0},{8,9},{9,10},{10,1... | collective-permute-start | bytes 442376 | tf_op jit(solution)/shard_map/ppermute | solution.py:227
  120.0 1.4 %copy-start = (f32[768,512]{1,0:T(8,128)S(1)}, f32[768,512]{1,0:T(8,128)}, u32[]{:S(2)}) copy-start(f32[768,512]{1,0:T(8,128)} %all-gather.2.cloned.1.call-done.normed_ref) | copy-start | bytes 4718596
  126.3 1.2 copy-start.3
Sparse Core Ops, SparseCore 0:
  36.4 39.4 all-gather.1
where the time goes:
time: 139 us; the launch traced here: 138 us
  waiting for transfers between devices  52.4 us (38%)
  starting transfers between devices  38 us (27%)
  Pallas kernels  18 us (13%)
  local copies, waits for them, and re-layouts  15.1 us (11%)
  between operations  14.2 us (10%)
    all_to_all x2, waiting for transfers between devices, spread(): lax.all_to_all(jnp.broadcast_to(shard[None], (devices, *shard.shape)), ax...  28.1 us
    all_to_all x2, starting transfers between devices, spread(): lax.all_to_all(jnp.broadcast_to(shard[None], (devices, *shard.shape)), ax...  18.2 us
    ppermute x4, waiting for transfers between devices, ring_pieces(): up = lax.ppermute(up, axis, ahead)  15.9 us
    unnamed x44, local copies, waits for them, and re-layouts  12.3 us
    pallas_call x1, Pallas kernels, per_device(): pl.pallas_call(outer_kernel, grid=(steps,), out_shape=(shape(pair_rep.sha...  11.2 us
    ppermute x1, starting transfers between devices, per_device(): right_here = lax.ppermute(right, ('row', 'col'), turn)  9.06 us
    ppermute x3, starting transfers between devices, ring_pieces(): down = lax.ppermute(down, axis, back)  7.59 us
    ppermute x1, waiting for transfers between devices, ring_pieces(): lax.ppermute(shard, axis, [(d, (d + ring) % devices) for d in range(devic...  5.31 us
  transfers between devices with their start and end apart: 12, of which 8 were waited for; matrix products, arithmetic and copies ran while one was open for 2% of the time, Pallas kernels for 9%

commit v1 on v0

--- a/solution.py
+++ b/solution.py
@@ -46,7 +46,18 @@
     return second
 
 
-def first_kernel(seq_ref, res_ref, align_ref, weight_ref, left_ref, right_ref, normed_ref, flat_ref, proj):
+def first_kernel(seq_in, res_in, align_in, left_in, right_in, left_ref, right_ref, normed_ref, flat_ref, seq_ref, res_ref, align_ref, weight_ref, proj, sems):
+    copies = [
+        pltpu.make_async_copy(align_in, align_ref, sems.at[0]),
+        pltpu.make_async_copy(left_in, weight_ref.at[0], sems.at[1]),
+        pltpu.make_async_copy(right_in, weight_ref.at[1], sems.at[2]),
+        pltpu.make_async_copy(seq_in, seq_ref, sems.at[3]),
+        pltpu.make_async_copy(res_in, res_ref, sems.at[4]),
+    ]
+    for copy in copies:
+        copy.start()
+    for copy in copies:
+        copy.wait()
     seqs, residues, width = align_ref.shape
     values = align_ref[...].reshape(seqs * residues, width)
     center = jnp.mean(values, axis=-1, keepdims=True)
@@ -55,7 +66,8 @@
     flat_ref[...] = normed
     for s in range(seqs):
         normed_ref[:, s * width : (s + 1) * width] = normed[s * residues : (s + 1) * residues]
-    wide = jnp.dot(normed, weight_ref[...], precision=highest, preferred_element_type=f32)
+    weight = jnp.concatenate([weight_ref[0]] * 4 + [weight_ref[1]] * 4, axis=0)
+    wide = lax.dot_general(normed, weight, (((1,), (1,)), ((), ())), precision=highest, preferred_element_type=f32)
     proj[0] = wide[:, :LANES]
     proj[1] = wide[:, LANES:]
     lane = lax.broadcasted_iota(jnp.int32, (seqs, LANES), 1)
@@ -99,17 +111,34 @@
         high, low = split_two(block)
         mixed_ref[h, :, :LANES] = high
         mixed_ref[h, :, LANES:] = low
-    high, low = split_two(out_weight_ref[...])
+    high, low = split_two(out_weight_ref[...].T)
     out_ref[0] = high
     out_ref[1] = low
 
 
-def outer_kernel(res_ref, left_ref, right_ref, mapped_ref, pair_ref, head_ref, pair_out_ref, logits_ref, tall, right_two, outer, high_ref, low_ref, seen):
+def outer_kernel(*refs):
+    res_ref = refs[0]
+    left_pieces = refs[1 : 1 + Z_CHIPS]
+    right_pieces = refs[1 + Z_CHIPS : 9 + Z_CHIPS]
+    mapped_ref, pair_ref, head_ref, pair_out_ref, logits_ref = refs[9 + Z_CHIPS : 14 + Z_CHIPS]
+    left_all, right_ref, tall, right_two, outer, high_ref, low_ref, seen, heads_two = refs[14 + Z_CHIPS :]
     step = pl.program_id(0)
     cols = 48
 
     @pl.when(step == 0)
     def _():
+        me = lax.axis_index("col")
+        side, place = me // Z_CHIPS, lax.rem(me, Z_CHIPS)
+        for k, piece in enumerate(left_pieces):
+            at = lax.rem(place + k, Z_CHIPS)
+            left_all[pl.ds(pl.multiple_of((side * Z_CHIPS + at) * 8, 8), 8), :] = piece[0]
+            left_all[pl.ds(pl.multiple_of(((1 - side) * Z_CHIPS + at) * 8, 8), 8), :] = piece[1]
+        row = lax.axis_index("row")
+        x, y, core = row // 4, lax.rem(row // 2, 2), lax.rem(row, 2)
+        for k, piece in enumerate(right_pieces):
+            at = lax.rem(x + k % 4, 4) * 4 + (core if k < 4 else 1 - core)
+            right_ref[pl.ds(pl.multiple_of((at + y * 2) * 8, 8), 8), :] = piece[0]
+            right_ref[pl.ds(pl.multiple_of((at + (1 - y) * 2) * 8, 8), 8), :] = piece[1]
         tall[...] = right_ref[:, : cols * 32].T
         for b in range(32):
             high, low = split_two(tall[pl.ds(b, cols, stride=32), :])
@@ -121,8 +150,14 @@
         live_cols = extra.T[:cols, :1]
         seen[0] = jnp.broadcast_to(live_cols * total, (cols, LANES))
         seen[1] = jnp.broadcast_to((live_cols - 1.0) * 1e9, (cols, LANES))
-
-    left_high, left_low = split_two(left_ref[...])
+        head = jnp.concatenate([head_ref[...], jnp.zeros((LANES - head_ref.shape[0], LANES), f32)], axis=0).T
+        head_high, head_low = split_two(head)
+        heads_two[0, :LANES] = head_high
+        heads_two[0, LANES:] = head_high
+        heads_two[1, :LANES] = head_low
+        heads_two[1, LANES:] = head_low
+
+    left_high, left_low = split_two(left_all[:, pl.ds(pl.multiple_of(step * (ROWS_PER_STEP * 32), LANES), ROWS_PER_STEP * 32)])
     both = right_two[...]
     outer[...] = mxu(both, jnp.concatenate([left_high, left_high], axis=0)) + mxu(both[:, :LANES], left_low)
     for quad in range(ROWS_PER_STEP // 4):
@@ -138,9 +173,6 @@
                 low_ref[at : at + cols, four * LANES : (four + 1) * LANES] = low
     wide = mxu(high_ref[...], mapped_ref[...])
     sums = wide[:, :LANES] + wide[:, LANES:] + mxu(low_ref[...], mapped_ref[:, :LANES])
-    head_high, head_low = split_two(head_ref[...])
-    head_high = jnp.concatenate([head_high, head_high], axis=0)
-    head_low = jnp.concatenate([head_low, head_low], axis=0)
     pairs = []
     for i in range(ROWS_PER_STEP):
         live = res_ref[step * ROWS_PER_STEP + i].astype(f32)
@@ -153,7 +185,7 @@
     normed = centred * lax.rsqrt(jnp.mean(centred * centred, axis=-1, keepdims=True) + epsilon)
     high, low = split_two(normed)
     normed_two = jnp.concatenate([high, low], axis=1)
-    logits = mxu(normed_two, head_high) + mxu(normed_two, head_low)
+    logits = mxu(normed_two, heads_two[0]) + mxu(normed_two, heads_two[1])
     lane = lax.broadcasted_iota(jnp.int32, (cols, LANES), 1)
     line = jnp.zeros((cols, LANES), f32)
     for i in range(ROWS_PER_STEP):
@@ -161,8 +193,17 @@
     logits_ref[...] = line + seen[1]
 
 
-def middle_kernel(align_normed_ref, normed_ref, gate_ref, turned_high_ref, turned_low_ref, open_ref):
-    high, low = split_two(normed_ref[...].T)
+def middle_kernel(align_normed_ref, gate_ref, *refs):
+    pieces = refs[:8]
+    turned_high_ref, turned_low_ref, open_ref, held = refs[8:]
+    residues = pieces[0].shape[1]
+    row = lax.axis_index("row")
+    x, y, core = row // 4, lax.rem(row // 2, 2), lax.rem(row, 2)
+    for k, piece in enumerate(pieces):
+        at = lax.rem(x + k % 4, 4) * 4 + (core if k < 4 else 1 - core)
+        held[pl.ds(pl.multiple_of((at + y * 2) * residues, 8), residues), :] = piece[0]
+        held[pl.ds(pl.multiple_of((at + (1 - y) * 2) * residues, 8), residues), :] = piece[1]
+    high, low = split_two(held[...].T)
     turned_high_ref[...] = high
     turned_low_ref[...] = low
     wide = jnp.dot(align_normed_ref[...], gate_ref[...], precision=highest, preferred_element_type=f32)
@@ -175,7 +216,7 @@
     heads = mixed_ref.shape[0]
     rows = 48
     me = lax.axis_index("col")
-    side, place = me // Z_CHIPS, me % Z_CHIPS
+    side, place = me // Z_CHIPS, lax.rem(me, Z_CHIPS)
     for k, piece in enumerate(pieces_in):
         at = lax.rem(place + k, Z_CHIPS) * rows
         for other in range(2):
@@ -210,9 +251,13 @@
     out_ref[...] = align_ref[...] + result.reshape(out_ref.shape)
 
 
-def spread(shard, axis):
+def row_pieces(shard, axis):
     devices = lax.axis_size(axis)
-    return lax.all_to_all(jnp.broadcast_to(shard[None], (devices, *shard.shape)), axis, 0, 0, tiled=True)
+    both = jnp.stack([shard, lax.ppermute(shard, axis, [(d, d ^ 2) for d in range(devices)])])
+    pieces = [both] + [
+        lax.ppermute(both, axis, [(d, (d + devices - 4 * k) % devices) for d in range(devices)]) for k in (1, 2, 3)
+    ]
+    return pieces + [lax.ppermute(piece, axis, [(d, d ^ 1) for d in range(devices)]) for piece in pieces]
 
 
 def ring_pieces(shard, axis):
@@ -232,12 +277,12 @@
     return pieces
 
 
-def call(kernel, outs, scratch=(), **more):
+def call(kernel, outs, limit, scratch=(), **more):
     return pl.pallas_call(
         kernel,
         out_shape=outs,
-        scratch_shapes=scratch,
-        compiler_params=pltpu.CompilerParams(vmem_limit_bytes=48 * 1024 * 1024),
+        scratch_shapes=list(scratch),
+        compiler_params=pltpu.CompilerParams(vmem_limit_bytes=limit * 1024 * 1024),
         **more,
     )
 
@@ -247,6 +292,7 @@
 
 
 VMEM = pl.BlockSpec(memory_space=pltpu.VMEM)
+HBM = pl.BlockSpec(memory_space=pltpu.HBM)
 SMEM = pl.BlockSpec(memory_space=pltpu.SMEM)
 
 
@@ -254,59 +300,74 @@
     seqs, rows, width = alignment.shape
     cols = pair_rep.shape[1]
     pair_width = pair_rep.shape[2]
-    four_weights = jnp.concatenate([left_weight] * 4 + [right_weight] * 4, axis=1)
     left, right, normed, normed_flat = call(
         first_kernel,
         (shape((seqs, rows * 32)), shape((seqs, rows * 32 + LANES)), shape((rows, seqs * width)), shape((seqs * rows, width))),
-        scratch=[pltpu.VMEM((2, seqs * rows, LANES), f32)],
-        in_specs=[SMEM, SMEM, VMEM, VMEM],
-    )(seq_mask, res_mask, alignment, four_weights)
+        8,
+        scratch=[
+            pltpu.SMEM(seq_mask.shape, jnp.int32),
+            pltpu.SMEM(res_mask.shape, jnp.int32),
+            pltpu.VMEM(alignment.shape, f32),
+            pltpu.VMEM((2, 32, width), f32),
+            pltpu.VMEM((2, seqs * rows, LANES), f32),
+            pltpu.SemaphoreType.DMA((5,)),
+        ],
+        in_specs=[HBM] * 5,
+    )(seq_mask, res_mask, alignment, left_weight.T, right_weight.T)
     turn = [(r * n_col + c, c * n_col + r) for r in range(n_row) for c in range(n_col)]
     right_here = lax.ppermute(right, ("row", "col"), turn)
-    right_all = spread(right_here, "row").reshape(n_row * seqs, -1)
-    left_all = spread(left, "col").reshape(n_col * seqs, -1)
+    left_pieces = ring_pieces(left, "col")
+    right_pieces = row_pieces(right_here, "row")
     mapped, mixed, out_two = call(
         weights_kernel,
         (shape((1024, 256), bf16), shape((8, 256, 256), bf16), shape((2, 256, 64), bf16)),
+        12,
         scratch=[pltpu.VMEM((1024, LANES), f32)],
-    )(w_outer, value_weight, output_weight)
-    head_pad = jnp.pad(w_logits, ((0, 0), (0, LANES - w_logits.shape[1])))
+    )(w_outer, value_weight, output_weight.T)
     steps = rows // ROWS_PER_STEP
+    whole = lambda dims: pl.BlockSpec(dims, lambda t: (0,) * len(dims))
     pair_out, logits = pl.pallas_call(
         outer_kernel,
         grid=(steps,),
         out_shape=(shape(pair_rep.shape), shape((cols, steps * LANES))),
-        in_specs=[
-            SMEM,
-            pl.BlockSpec((n_col * seqs, ROWS_PER_STEP * 32), lambda t: (0, t)),
-            pl.BlockSpec(right_all.shape, lambda t: (0, 0)),
-            pl.BlockSpec((1024, 256), lambda t: (0, 0)),
+        in_specs=[SMEM]
+        + [whole(left_pieces[0].shape)] * 8
+        + [whole(right_pieces[0].shape)] * 8
+        + [
+            whole((1024, 256)),
             pl.BlockSpec((ROWS_PER_STEP, cols, pair_width), lambda t: (t, 0, 0)),
-            pl.BlockSpec((pair_width, LANES), lambda t: (0, 0)),
+            whole((8, LANES)),
         ],
         out_specs=[
             pl.BlockSpec((ROWS_PER_STEP, cols, pair_width), lambda t: (t, 0, 0)),
             pl.BlockSpec((cols, LANES), lambda t: (0, t)),
         ],
         scratch_shapes=[
+            pltpu.VMEM((n_col * seqs, rows * 32), f32),
+            pltpu.VMEM((n_row * seqs, rows * 32 + LANES), f32),
             pltpu.VMEM((cols * 32, LANES), f32),
             pltpu.VMEM((cols * 32, 256), bf16),
             pltpu.VMEM((cols * 32, ROWS_PER_STEP * 32), f32),
             pltpu.VMEM((ROWS_PER_STEP * cols, 1024), bf16),
             pltpu.VMEM((ROWS_PER_STEP * cols, 1024), bf16),
             pltpu.VMEM((2, cols, LANES), f32),
+            pltpu.VMEM((2, 256, LANES), bf16),
         ],
-        compiler_params=pltpu.CompilerParams(vmem_limit_bytes=48 * 1024 * 1024),
-    )(res_mask, left_all, right_all, mapped, pair_rep, head_pad)
-    normed_all = lax.all_gather(normed, "row", axis=0, tiled=True)
+        compiler_params=pltpu.CompilerParams(vmem_limit_bytes=32 * 1024 * 1024),
+        cost_estimate=pl.CostEstimate(flops=10**10, bytes_accessed=10**7, transcendentals=0),
+    )(res_mask, *left_pieces, *right_pieces, mapped, pair_rep, w_logits.T)
+    normed_pieces = row_pieces(normed, "row")
     turned_high, turned_low, opened = call(
         middle_kernel,
         (shape((seqs * width, n_row * rows), bf16), shape((seqs * width, n_row * rows), bf16), shape((seqs * rows, gate_weight.shape[1]))),
-    )(normed_flat, normed_all, gate_weight)
+        12,
+        scratch=[pltpu.VMEM((n_row * rows, seqs * width), f32)],
+    )(normed_flat, gate_weight, *normed_pieces)
     pieces = ring_pieces(logits, "col")
     alignment_out = call(
         last_kernel,
         shape(alignment.shape),
+        24,
         scratch=[pltpu.VMEM((n_row * rows, steps * LANES), f32), pltpu.VMEM((4, steps * LANES, LANES), f32)],
     )(*pieces, turned_high, turned_low, mixed, opened, out_two, alignment)
     return alignment_out, pair_out

time: 139 us -> 99.2 us (0.71)
  waiting for transfers between devices: 52.4 us -> 26.6 us
  between operations: 14.2 us -> 0.84 us
  local copies, waits for them, and re-layouts: 15.1 us -> 7.67 us
  starting transfers between devices: 38 us -> 45.1 us
    all_to_all x2 -> x0, waiting for transfers between devices: 28.1 us -> none  [spread(): lax.all_to_all(jnp.broadcast_to(shard[None], (devices, *shard.shape)), ax...]
    all_to_all x2 -> x0, starting transfers between devices: 18.2 us -> none  [spread(): lax.all_to_all(jnp.broadcast_to(shard[None], (devices, *shard.shape)), ax...]
    ppermute x3 -> x6, starting transfers between devices: 7.59 us -> 19.4 us  [ring_pieces(): down = lax.ppermute(down, axis, back)]
    ppermute x0 -> x16, starting transfers between devices: none -> 10.6 us  [the longest x6 9.23 us: row_pieces(): lax.ppermute(both, axis, [(d, (d + devices - 4 * k) % devices) for d in r...]
    ppermute x1 -> x2, starting transfers between devices: 0.54 us -> 5.35 us  [ring_pieces(): lax.ppermute(shard, axis, [(d, (d + ring) % devices) for d in range(devic...]
    unnamed x44 -> x26, local copies, waits for them, and re-layouts: 12.3 us -> 7.67 us
    ppermute x3 -> x6, waiting for transfers between devices: 0.01 us -> 3.64 us  [ring_pieces(): down = lax.ppermute(down, axis, back)]
    ppermute x1, waiting for transfers between devices: 2.4 us -> 0.01 us  [per_device(): right_here = lax.ppermute(right, ('row', 'col'), turn)]
  transfers between devices with their start and end apart: 12 -> 33, of which waited for: 8 -> 12; matrix products, arithmetic and copies ran while one was open for 2% -> 0% of each run, Pallas kernels for 9% -> 13%
where the time goes in v1:
time: 99.2 us; the launch traced here: 98.2 us
  starting transfers between devices  45.1 us (45%)
  waiting for transfers between devices  26.6 us (27%)
  Pallas kernels  18 us (18%)
  local copies, waits for them, and re-layouts  7.67 us (8%)
    ppermute x6, starting transfers between devices, ring_pieces(): down = lax.ppermute(down, axis, back)  19.4 us
    ppermute x8, waiting for transfers between devices, ring_pieces(): up = lax.ppermute(up, axis, ahead)  14.7 us
    pallas_call x1, Pallas kernels, per_device(): pl.pallas_call(outer_kernel, grid=(steps,), out_shape=(shape(pair_rep.sha...  11.3 us
    ppermute x6, starting transfers between devices, row_pieces(): lax.ppermute(both, axis, [(d, (d + devices - 4 * k) % devices) for d in r...  9.23 us
    ppermute x1, starting transfers between devices, per_device(): right_here = lax.ppermute(right, ('row', 'col'), turn)  9.07 us
    unnamed x26, local copies, waits for them, and re-layouts  7.67 us
    ppermute x2, waiting for transfers between devices, ring_pieces(): lax.ppermute(shard, axis, [(d, (d + ring) % devices) for d in range(devic...  6.39 us
    ppermute x2, starting transfers between devices, ring_pieces(): lax.ppermute(shard, axis, [(d, (d + ring) % devices) for d in range(devic...  5.35 us
  transfers between devices with their start and end apart: 33, of which 12 were waited for; matrix products, arithmetic and copies ran while one was open for 0% of the time, Pallas kernels for 13%

profile of v1, /device:TPU:2, one launch (start us, length us, event | category | flops | bytes accessed | tf_op | source)
XLA Modules:
  0.0 98.2 jit_solution(13130258539084779954)
XLA Ops:
  0.7 0.9 copy-done
  1.6 0.7 copy-done.6
  2.3 0.7 copy-done.7
  3.0 0.7 copy-done.8
  3.7 0.7 copy-done.9
  4.3 1.6 %shard_map.122 = (f32[8,1536]{1,0:T(8,128)S(1)}, f32[8,1664]{1,0:T(8,128)S(1)}, f32[48,512]{1,0:T(8,128)S(1)}, f32[384,64]{1,0:T(8,128)S(1)}) custom-call(s32[8]{0:T(128)S(1)} %copy-done.8, s32[48]{0:T(128)S(1)} %copy-done.9, f32[8,48,64]{2,1,0:T(8,128)S(1)} %copy-done, f32[32,64]{1,0:T(8,128)S(1)} %bitcast.16, f32[32,64]{1,0:T(8,128)S(1)} %bitcast.17), custom_call_target="tpu_custom_call" | custom-call | tf_op jit(solution)/shard_map/pallas_call | solution.py:303
  5.9 9.1 %collective-permute-start.8 = (f32[8,1664]{1,0:T(8,128)S(1)}, f32[8,1664]{1,0:T(8,128)S(1)}, u32[]{:S(2)}, u32[]{:S(2)}) collective-permute-start(f32[8,1664]{1,0:T(8,128)S(1)} %get-tuple-element.15), channel_id=1, source_target_pairs={{0,0},{1,16},{2,32},{3,48},{4,64},{5,80},{6,96},{7,112},{8,128},{9... | collective-permute-start | bytes 159752 | tf_op jit(solution)/shard_map/ppermute | solution.py:318
  15.0 4.0 %collective-permute-start = (f32[8,1536]{1,0:T(8,128)S(1)}, f32[8,1536]{1,0:T(8,128)S(1)}, u32[]{:S(2)}, u32[]{:S(2)}) collective-permute-start(f32[8,1536]{1,0:T(8,128)S(1)} %get-tuple-element.14), channel_id=1, source_target_pairs={{0,8},{1,9},{2,10},{3,11},{4,12},{5,13},{6,14},{7,15},{8,0},{9,1},... | collective-permute-start | bytes 147464 | tf_op jit(solution)/shard_map/ppermute | solution.py:266
  19.1 2.0 %collective-permute-done = f32[8,1536]{1,0:T(8,128)S(1)} collective-permute-done((f32[8,1536]{1,0:T(8,128)S(1)}, f32[8,1536]{1,0:T(8,128)S(1)}, u32[]{:S(2)}, u32[]{:S(2)}) %collective-permute-start) | collective-permute-done | bytes 49184 | tf_op jit(solution)/shard_map/ppermute | solution.py:266
  21.1 0.5 collective-permute-start.4
  21.6 2.8 %collective-permute-start.1 = (f32[2,8,1536]{2,1,0:T(8,128)S(1)}, f32[2,8,1536]{2,1,0:T(8,128)S(1)}, u32[]{:S(2)}, u32[]{:S(2)}) collective-permute-start(f32[2,8,1536]{2,1,0:T(8,128)S(1)} %pad_maximum_fusion.3.refs_1_), channel_id=1, source_target_pairs={{0,7},{1,0},{2,1},{3,2},{4,3},{5,4},{6,5},{7,6},{8,15},{9,8},{10,9... | collective-permute-start | bytes 294920 | tf_op jit(solution)/shard_map/ppermute | solution.py:275
  24.4 0.1 collective-permute-start.13
  24.5 2.5 %collective-permute-done.4.refs_8_ = f32[2,8,1536]{2,1,0:T(8,128)S(1)} collective-permute-done((f32[2,8,1536]{2,1,0:T(8,128)S(1)}, f32[2,8,1536]{2,1,0:T(8,128)S(1)}, u32[]{:S(2)}, u32[]{:S(2)}) %collective-permute-start.4) | collective-permute-done | bytes 98336 | tf_op jit(solution)/shard_map/ppermute | solution.py:272
  27.0 2.9 %collective-permute-start.12 = (f32[2,8,1664]{2,1,0:T(8,128)S(1)}, f32[2,8,1664]{2,1,0:T(8,128)S(1)}, u32[]{:S(2)}, u32[]{:S(2)}) collective-permute-start(f32[2,8,1664]{2,1,0:T(8,128)S(1)} %pad_maximum_fusion.2.refs_9_), channel_id=1, source_target_pairs={{0,64},{16,80},{32,96},{48,112},{64,128},{80,144},{96,160},{112,17... | collective-permute-start | bytes 319496 | tf_op jit(solution)/shard_map/ppermute | solution.py:258
  29.9 1.4 %collective-permute-start.11 = (f32[2,8,1664]{2,1,0:T(8,128)S(1)}, f32[2,8,1664]{2,1,0:T(8,128)S(1)}, u32[]{:S(2)}, u32[]{:S(2)}) collective-permute-start(f32[2,8,1664]{2,1,0:T(8,128)S(1)} %pad_maximum_fusion.2.refs_9_), channel_id=1, source_target_pairs={{0,128},{16,144},{32,160},{48,176},{64,192},{80,208},{96,224},{112... | collective-permute-start | bytes 319496 | tf_op jit(solution)/shard_map/ppermute | solution.py:258
  31.3 2.6 %collective-permute-start.10 = (f32[2,8,1664]{2,1,0:T(8,128)S(1)}, f32[2,8,1664]{2,1,0:T(8,128)S(1)}, u32[]{:S(2)}, u32[]{:S(2)}) collective-permute-start(f32[2,8,1664]{2,1,0:T(8,128)S(1)} %pad_maximum_fusion.2.refs_9_), channel_id=1, source_target_pairs={{0,192},{16,208},{32,224},{48,240},{64,0},{80,16},{96,32},{112,48}... | collective-permute-start | bytes 319496 | tf_op jit(solution)/shard_map/ppermute | solution.py:258
  34.0 3.2 %collective-permute-start.2 = (f32[2,8,1536]{2,1,0:T(8,128)S(1)}, f32[2,8,1536]{2,1,0:T(8,128)S(1)}, u32[]{:S(2)}, u32[]{:S(2)}) collective-permute-start(f32[2,8,1536]{2,1,0:T(8,128)S(1)} %collective-permute-done.1.refs_2_), channel_id=1, source_target_pairs={{0,7},{1,0},{2,1},{3,2},{4,3},{5,4},{6,5},{7,6},{8,15},{9,8},{10,9... | collective-permute-start | bytes 294920 | tf_op jit(solution)/shard_map/ppermute | solution.py:275
  37.2 0.1 collective-permute-start.16
  37.3 0.5 collective-permute-start.15
  37.8 0.1 collective-permute-start.14
  37.9 1.5 %collective-permute-done.2.refs_3_ = f32[2,8,1536]{2,1,0:T(8,128)S(1)} collective-permute-done((f32[2,8,1536]{2,1,0:T(8,128)S(1)}, f32[2,8,1536]{2,1,0:T(8,128)S(1)}, u32[]{:S(2)}, u32[]{:S(2)}) %collective-permute-start.2) | collective-permute-done | bytes 98336 | tf_op jit(solution)/shard_map/ppermute | solution.py:275
  39.4 3.6 %collective-permute-start.3 = (f32[2,8,1536]{2,1,0:T(8,128)S(1)}, f32[2,8,1536]{2,1,0:T(8,128)S(1)}, u32[]{:S(2)}, u32[]{:S(2)}) collective-permute-start(f32[2,8,1536]{2,1,0:T(8,128)S(1)} %collective-permute-done.2.refs_3_), channel_id=1, source_target_pairs={{0,7},{1,0},{2,1},{3,2},{4,3},{5,4},{6,5},{7,6},{8,15},{9,8},{10,9... | collective-permute-start | bytes 294920 | tf_op jit(solution)/shard_map/ppermute | solution.py:275
  43.0 1.0 %copy-done.2 = f32[1024,128]{1,0:T(8,128)S(1)} copy-done((f32[1024,128]{1,0:T(8,128)S(1)}, f32[1024,128]{1,0:T(8,128)}, u32[]{:S(2)}) %copy-start.2) | copy-done | bytes 524312
  44.1 0.8 copy-done.3
  44.9 0.8 copy-done.4
  45.7 1.1 %shard_map.123 = (bf16[1024,256]{1,0:T(8,128)(2,1)S(1)}, bf16[8,256,256]{2,1,0:T(8,128)(2,1)S(1)}, bf16[2,256,64]{2,1,0:T(8,128)(2,1)S(1)}) custom-call(f32[1024,128]{1,0:T(8,128)S(1)} %copy-done.2, f32[64,256]{1,0:T(8,128)S(1)} %copy-done.3, f32[64,256]{1,0:T(8,128)S(1)} %bitcast.14), custom_call_target="tpu_custom_call" | custom-call | tf_op jit(solution)/shard_map/pallas_call | solution.py:321
  46.8 0.1 collective-permute-start.25
  47.0 1.9 %collective-permute-done.7.refs_5_ = f32[2,8,1536]{2,1,0:T(8,128)S(1)} collective-permute-done((f32[2,8,1536]{2,1,0:T(8,128)S(1)}, f32[2,8,1536]{2,1,0:T(8,128)S(1)}, u32[]{:S(2)}, u32[]{:S(2)}) %collective-permute-start.7) | collective-permute-done | bytes 98336 | tf_op jit(solution)/shard_map/ppermute | solution.py:272
  48.9 1.3 %copy-done.11 = f32[48,48,128]{2,1,0:T(8,128)S(1)} copy-done((f32[48,48,128]{2,1,0:T(8,128)S(1)}, f32[48,48,128]{2,1,0:T(8,128)}, u32[]{:S(2)}) %copy-start.11) | copy-done | bytes 1179672
  50.1 11.3 %shard_map.124 = (f32[48,48,128]{2,1,0:T(8,128)}, f32[48,384]{1,0:T(8,128)S(1)}) custom-call(s32[48]{0:T(128)S(1)} %copy-done.10, f32[2,8,1536]{2,1,0:T(8,128)S(1)} %pad_maximum_fusion.3.refs_1_, f32[2,8,1536]{2,1,0:T(8,128)S(1)} %collective-permute-done.1.refs_2_, f32[2,8,1536]{2,1,0:T(8,128)S(1)} %collective-permute-done.2.refs_3_, ...), custom_call_target="tpu_custom_call" | custom-call | flops 10000000000 | bytes 10000000 | tf_op jit(solution)/shard_map/pallas_call | solution.py:329
  61.5 1.3 %collective-permute-start.17 = (f32[48,384]{1,0:T(8,128)S(1)}, f32[48,384]{1,0:T(8,128)S(1)}, u32[]{:S(2)}, u32[]{:S(2)}) collective-permute-start(f32[48,384]{1,0:T(8,128)S(1)} %get-tuple-element.17), channel_id=1, source_target_pairs={{0,8},{1,9},{2,10},{3,11},{4,12},{5,13},{6,14},{7,15},{8,0},{9,1},... | collective-permute-start | bytes 221192 | tf_op jit(solution)/shard_map/ppermute | solution.py:266
  62.8 0.1 collective-permute-start.29
  62.9 4.4 %collective-permute-done.17 = f32[48,384]{1,0:T(8,128)S(1)} collective-permute-done((f32[48,384]{1,0:T(8,128)S(1)}, f32[48,384]{1,0:T(8,128)S(1)}, u32[]{:S(2)}, u32[]{:S(2)}) %collective-permute-start.17) | collective-permute-done | bytes 73760 | tf_op jit(solution)/shard_map/ppermute | solution.py:266
  67.3 0.1 collective-permute-start.21
  67.4 3.2 %collective-permute-start.18 = (f32[2,48,384]{2,1,0:T(8,128)S(1)}, f32[2,48,384]{2,1,0:T(8,128)S(1)}, u32[]{:S(2)}, u32[]{:S(2)}) collective-permute-start(f32[2,48,384]{2,1,0:T(8,128)S(1)} %pad_maximum_fusion.1.refs_0_), channel_id=1, source_target_pairs={{0,7},{1,0},{2,1},{3,2},{4,3},{5,4},{6,5},{7,6},{8,15},{9,8},{10,9... | collective-permute-start | bytes 442376 | tf_op jit(solution)/shard_map/ppermute | solution.py:275
  70.7 4.4 %collective-permute-done.21.refs_7_ = f32[2,48,384]{2,1,0:T(8,128)S(1)} collective-permute-done((f32[2,48,384]{2,1,0:T(8,128)S(1)}, f32[2,48,384]{2,1,0:T(8,128)S(1)}, u32[]{:S(2)}, u32[]{:S(2)}) %collective-permute-start.21) | collective-permute-done | bytes 147488 | tf_op jit(solution)/shard_map/ppermute | solution.py:272
  75.0 2.3 %collective-permute-start.27 = (f32[2,48,512]{2,1,0:T(8,128)S(1)}, f32[2,48,512]{2,1,0:T(8,128)S(1)}, u32[]{:S(2)}, u32[]{:S(2)}) collective-permute-start(f32[2,48,512]{2,1,0:T(8,128)S(1)} %pad_maximum_fusion.refs_0_), channel_id=1, source_target_pairs={{0,128},{16,144},{32,160},{48,176},{64,192},{80,208},{96,224},{112... | collective-permute-start | bytes 589832 | tf_op jit(solution)/shard_map/ppermute | solution.py:258
  77.3 3.3 %collective-permute-start.19 = (f32[2,48,384]{2,1,0:T(8,128)S(1)}, f32[2,48,384]{2,1,0:T(8,128)S(1)}, u32[]{:S(2)}, u32[]{:S(2)}) collective-permute-start(f32[2,48,384]{2,1,0:T(8,128)S(1)} %collective-permute-done.18.refs_1_), channel_id=1, source_target_pairs={{0,7},{1,0},{2,1},{3,2},{4,3},{5,4},{6,5},{7,6},{8,15},{9,8},{10,9... | collective-permute-start | bytes 442376 | tf_op jit(solution)/shard_map/ppermute | solution.py:275
  80.6 1.5 %collective-permute-done.22.refs_6_ = f32[2,48,384]{2,1,0:T(8,128)S(1)} collective-permute-done((f32[2,48,384]{2,1,0:T(8,128)S(1)}, f32[2,48,384]{2,1,0:T(8,128)S(1)}, u32[]{:S(2)}, u32[]{:S(2)}) %collective-permute-start.22) | collective-permute-done | bytes 147488 | tf_op jit(solution)/shard_map/ppermute | solution.py:272
  82.2 0.1 collective-permute-done.27.refs_2_
  82.3 0.4 collective-permute-start.31
  82.7 1.6 %collective-permute-done.26.refs_1_ = f32[2,48,512]{2,1,0:T(8,128)S(1)} collective-permute-done((f32[2,48,512]{2,1,0:T(8,128)S(1)}, f32[2,48,512]{2,1,0:T(8,128)S(1)}, u32[]{:S(2)}, u32[]{:S(2)}) %collective-permute-start.26) | collective-permute-done | bytes 196640 | tf_op jit(solution)/shard_map/ppermute | solution.py:258
  84.3 3.2 %collective-permute-start.20 = (f32[2,48,384]{2,1,0:T(8,128)S(1)}, f32[2,48,384]{2,1,0:T(8,128)S(1)}, u32[]{:S(2)}, u32[]{:S(2)}) collective-permute-start(f32[2,48,384]{2,1,0:T(8,128)S(1)} %collective-permute-done.19.refs_2_), channel_id=1, source_target_pairs={{0,7},{1,0},{2,1},{3,2},{4,3},{5,4},{6,5},{7,6},{8,15},{9,8},{10,9... | collective-permute-start | bytes 442376 | tf_op jit(solution)/shard_map/ppermute | solution.py:275
  87.5 0.9 collective-permute-done.23.refs_5_
  88.5 0.7 shard_map.125
  89.2 2.1 %collective-permute-done.20.refs_3_ = f32[2,48,384]{2,1,0:T(8,128)S(1)} collective-permute-done((f32[2,48,384]{2,1,0:T(8,128)S(1)}, f32[2,48,384]{2,1,0:T(8,128)S(1)}, u32[]{:S(2)}, u32[]{:S(2)}) %collective-permute-start.20) | collective-permute-done | bytes 147488 | tf_op jit(solution)/shard_map/ppermute | solution.py:275
  91.3 3.5 %collective-permute-done.24.refs_4_ = f32[2,48,384]{2,1,0:T(8,128)S(1)} collective-permute-done((f32[2,48,384]{2,1,0:T(8,128)S(1)}, f32[2,48,384]{2,1,0:T(8,128)S(1)}, u32[]{:S(2)}, u32[]{:S(2)}) %collective-permute-start.24) | collective-permute-done | bytes 147488 | tf_op jit(solution)/shard_map/ppermute | solution.py:272
  94.8 3.3 %shard_map.126 = f32[8,48,64]{2,1,0:T(8,128)} custom-call(f32[2,48,384]{2,1,0:T(8,128)S(1)} %pad_maximum_fusion.1.refs_0_, f32[2,48,384]{2,1,0:T(8,128)S(1)} %collective-permute-done.18.refs_1_, f32[2,48,384]{2,1,0:T(8,128)S(1)} %collective-permute-done.19.refs_2_, f32[2,48,384]{2,1,0:T(8,128)S(1)} %collective-permute-done.20.refs_3_, ...), custom_call_target="tpu_custom_call" | custom-call | tf_op jit(solution)/shard_map/pallas_call | solution.py:367
  (53 shorter events, 0.2 us)
Async XLA Ops:
  0.6 48.2 %copy-start.10 = (s32[48]{0:T(128)S(1)}, s32[48]{0:T(128)}, u32[]{:S(2)}) copy-start(s32[48]{0:T(128)} %refs_0_.1) | copy-start | bytes 580
  0.6 0.9 copy-start
  1.6 0.7 copy-start.6
  2.3 0.7 copy-start.7
  3.0 0.7 copy-start.8
  3.7 0.7 copy-start.9
  4.3 44.5 %copy-start.12 = (f32[128,8]{0,1:T(8,128)S(1)}, f32[128,8]{0,1:T(8,128)}, u32[]{:S(2)}) copy-start(f32[128,8]{0,1:T(8,128)} %param.18) | copy-start | bytes 12292
  5.9 13.1 %collective-permute-start.8 = (f32[8,1664]{1,0:T(8,128)S(1)}, f32[8,1664]{1,0:T(8,128)S(1)}, u32[]{:S(2)}, u32[]{:S(2)}) collective-permute-start(f32[8,1664]{1,0:T(8,128)S(1)} %get-tuple-element.15), channel_id=1, source_target_pairs={{0,0},{1,16},{2,32},{3,48},{4,64},{5,80},{6,96},{7,112},{8,128},{9... | collective-permute-start | bytes 159752 | tf_op jit(solution)/shard_map/ppermute | solution.py:318
  15.0 6.1 %collective-permute-start = (f32[8,1536]{1,0:T(8,128)S(1)}, f32[8,1536]{1,0:T(8,128)S(1)}, u32[]{:S(2)}, u32[]{:S(2)}) collective-permute-start(f32[8,1536]{1,0:T(8,128)S(1)} %get-tuple-element.14), channel_id=1, source_target_pairs={{0,8},{1,9},{2,10},{3,11},{4,12},{5,13},{6,14},{7,15},{8,0},{9,1},... | collective-permute-start | bytes 147464 | tf_op jit(solution)/shard_map/ppermute | solution.py:266
  19.0 5.4 %collective-permute-start.9 = (f32[8,1664]{1,0:T(8,128)S(1)}, f32[8,1664]{1,0:T(8,128)S(1)}, u32[]{:S(2)}, u32[]{:S(2)}) collective-permute-start(f32[8,1664]{1,0:T(8,128)S(1)} %collective-permute-done.8), channel_id=1, source_target_pairs={{0,32},{16,48},{32,0},{48,16},{64,96},{80,112},{96,64},{112,80},{1... | collective-permute-start | bytes 159752 | tf_op jit(solution)/shard_map/ppermute | solution.py:256
  21.1 5.9 %collective-permute-start.4 = (f32[2,8,1536]{2,1,0:T(8,128)S(1)}, f32[2,8,1536]{2,1,0:T(8,128)S(1)}, u32[]{:S(2)}, u32[]{:S(2)}) collective-permute-start(f32[2,8,1536]{2,1,0:T(8,128)S(1)} %pad_maximum_fusion.3.refs_1_), channel_id=1, source_target_pairs={{0,1},{1,2},{2,3},{3,4},{4,5},{5,6},{6,7},{7,0},{8,9},{9,10},{10,1... | collective-permute-start | bytes 294920 | tf_op jit(solution)/shard_map/ppermute | solution.py:272
  21.6 9.7 %collective-permute-start.1 = (f32[2,8,1536]{2,1,0:T(8,128)S(1)}, f32[2,8,1536]{2,1,0:T(8,128)S(1)}, u32[]{:S(2)}, u32[]{:S(2)}) collective-permute-start(f32[2,8,1536]{2,1,0:T(8,128)S(1)} %pad_maximum_fusion.3.refs_1_), channel_id=1, source_target_pairs={{0,7},{1,0},{2,1},{3,2},{4,3},{5,4},{6,5},{7,6},{8,15},{9,8},{10,9... | collective-permute-start | bytes 294920 | tf_op jit(solution)/shard_map/ppermute | solution.py:275
  24.4 9.5 %collective-permute-start.13 = (f32[2,8,1664]{2,1,0:T(8,128)S(1)}, f32[2,8,1664]{2,1,0:T(8,128)S(1)}, u32[]{:S(2)}, u32[]{:S(2)}) collective-permute-start(f32[2,8,1664]{2,1,0:T(8,128)S(1)} %pad_maximum_fusion.2.refs_9_), channel_id=1, source_target_pairs={{0,16},{16,0},{32,48},{48,32},{64,80},{80,64},{96,112},{112,96},{1... | collective-permute-start | bytes 319496 | tf_op jit(solution)/shard_map/ppermute | solution.py:260
  27.0 10.2 %collective-permute-start.5 = (f32[2,8,1536]{2,1,0:T(8,128)S(1)}, f32[2,8,1536]{2,1,0:T(8,128)S(1)}, u32[]{:S(2)}, u32[]{:S(2)}) collective-permute-start(f32[2,8,1536]{2,1,0:T(8,128)S(1)} %collective-permute-done.4.refs_8_), channel_id=1, source_target_pairs={{0,1},{1,2},{2,3},{3,4},{4,5},{5,6},{6,7},{7,0},{8,9},{9,10},{10,1... | collective-permute-start | bytes 294920 | tf_op jit(solution)/shard_map/ppermute | solution.py:272
  27.0 10.2 %collective-permute-start.12 = (f32[2,8,1664]{2,1,0:T(8,128)S(1)}, f32[2,8,1664]{2,1,0:T(8,128)S(1)}, u32[]{:S(2)}, u32[]{:S(2)}) collective-permute-start(f32[2,8,1664]{2,1,0:T(8,128)S(1)} %pad_maximum_fusion.2.refs_9_), channel_id=1, source_target_pairs={{0,64},{16,80},{32,96},{48,112},{64,128},{80,144},{96,160},{112,17... | collective-permute-start | bytes 319496 | tf_op jit(solution)/shard_map/ppermute | solution.py:258
  29.9 7.4 %collective-permute-start.11 = (f32[2,8,1664]{2,1,0:T(8,128)S(1)}, f32[2,8,1664]{2,1,0:T(8,128)S(1)}, u32[]{:S(2)}, u32[]{:S(2)}) collective-permute-start(f32[2,8,1664]{2,1,0:T(8,128)S(1)} %pad_maximum_fusion.2.refs_9_), channel_id=1, source_target_pairs={{0,128},{16,144},{32,160},{48,176},{64,192},{80,208},{96,224},{112... | collective-permute-start | bytes 319496 | tf_op jit(solution)/shard_map/ppermute | solution.py:258
  31.3 6.5 %collective-permute-start.10 = (f32[2,8,1664]{2,1,0:T(8,128)S(1)}, f32[2,8,1664]{2,1,0:T(8,128)S(1)}, u32[]{:S(2)}, u32[]{:S(2)}) collective-permute-start(f32[2,8,1664]{2,1,0:T(8,128)S(1)} %pad_maximum_fusion.2.refs_9_), channel_id=1, source_target_pairs={{0,192},{16,208},{32,224},{48,240},{64,0},{80,16},{96,32},{112,48}... | collective-permute-start | bytes 319496 | tf_op jit(solution)/shard_map/ppermute | solution.py:258
  34.0 5.4 %collective-permute-start.2 = (f32[2,8,1536]{2,1,0:T(8,128)S(1)}, f32[2,8,1536]{2,1,0:T(8,128)S(1)}, u32[]{:S(2)}, u32[]{:S(2)}) collective-permute-start(f32[2,8,1536]{2,1,0:T(8,128)S(1)} %collective-permute-done.1.refs_2_), channel_id=1, source_target_pairs={{0,7},{1,0},{2,1},{3,2},{4,3},{5,4},{6,5},{7,6},{8,15},{9,8},{10,9... | collective-permute-start | bytes 294920 | tf_op jit(solution)/shard_map/ppermute | solution.py:275
  37.2 5.8 %collective-permute-start.6 = (f32[2,8,1536]{2,1,0:T(8,128)S(1)}, f32[2,8,1536]{2,1,0:T(8,128)S(1)}, u32[]{:S(2)}, u32[]{:S(2)}) collective-permute-start(f32[2,8,1536]{2,1,0:T(8,128)S(1)} %collective-permute-done.5.refs_7_), channel_id=1, source_target_pairs={{0,1},{1,2},{2,3},{3,4},{4,5},{5,6},{6,7},{7,0},{8,9},{9,10},{10,1... | collective-permute-start | bytes 294920 | tf_op jit(solution)/shard_map/ppermute | solution.py:272
  37.2 9.6 %collective-permute-start.16 = (f32[2,8,1664]{2,1,0:T(8,128)S(1)}, f32[2,8,1664]{2,1,0:T(8,128)S(1)}, u32[]{:S(2)}, u32[]{:S(2)}) collective-permute-start(f32[2,8,1664]{2,1,0:T(8,128)S(1)} %collective-permute-done.12.refs_12_), channel_id=1, source_target_pairs={{0,16},{16,0},{32,48},{48,32},{64,80},{80,64},{96,112},{112,96},{1... | collective-permute-start | bytes 319496 | tf_op jit(solution)/shard_map/ppermute | solution.py:260
  37.3 9.6 %collective-permute-start.15 = (f32[2,8,1664]{2,1,0:T(8,128)S(1)}, f32[2,8,1664]{2,1,0:T(8,128)S(1)}, u32[]{:S(2)}, u32[]{:S(2)}) collective-permute-start(f32[2,8,1664]{2,1,0:T(8,128)S(1)} %collective-permute-done.11.refs_11_), channel_id=1, source_target_pairs={{0,16},{16,0},{32,48},{48,32},{64,80},{80,64},{96,112},{112,96},{1... | collective-permute-start | bytes 319496 | tf_op jit(solution)/shard_map/ppermute | solution.py:260
  37.8 9.1 %collective-permute-start.14 = (f32[2,8,1664]{2,1,0:T(8,128)S(1)}, f32[2,8,1664]{2,1,0:T(8,128)S(1)}, u32[]{:S(2)}, u32[]{:S(2)}) collective-permute-start(f32[2,8,1664]{2,1,0:T(8,128)S(1)} %collective-permute-done.10.refs_10_), channel_id=1, source_target_pairs={{0,16},{16,0},{32,48},{48,32},{64,80},{80,64},{96,112},{112,96},{1... | collective-permute-start | bytes 319496 | tf_op jit(solution)/shard_map/ppermute | solution.py:260
  39.4 7.6 %collective-permute-start.3 = (f32[2,8,1536]{2,1,0:T(8,128)S(1)}, f32[2,8,1536]{2,1,0:T(8,128)S(1)}, u32[]{:S(2)}, u32[]{:S(2)}) collective-permute-start(f32[2,8,1536]{2,1,0:T(8,128)S(1)} %collective-permute-done.2.refs_3_), channel_id=1, source_target_pairs={{0,7},{1,0},{2,1},{3,2},{4,3},{5,4},{6,5},{7,6},{8,15},{9,8},{10,9... | collective-permute-start | bytes 294920 | tf_op jit(solution)/shard_map/ppermute | solution.py:275
  43.0 5.8 %collective-permute-start.7 = (f32[2,8,1536]{2,1,0:T(8,128)S(1)}, f32[2,8,1536]{2,1,0:T(8,128)S(1)}, u32[]{:S(2)}, u32[]{:S(2)}) collective-permute-start(f32[2,8,1536]{2,1,0:T(8,128)S(1)} %collective-permute-done.6.refs_6_), channel_id=1, source_target_pairs={{0,1},{1,2},{2,3},{3,4},{4,5},{5,6},{6,7},{7,0},{8,9},{9,10},{10,1... | collective-permute-start | bytes 294920 | tf_op jit(solution)/shard_map/ppermute | solution.py:272
  43.0 1.0 %copy-start.2 = (f32[1024,128]{1,0:T(8,128)S(1)}, f32[1024,128]{1,0:T(8,128)}, u32[]{:S(2)}) copy-start(f32[1024,128]{1,0:T(8,128)} %outer_ref.1) | copy-start | bytes 1572868
  44.1 0.8 copy-start.3
  44.9 0.8 copy-start.4
  46.8 16.0 %collective-permute-start.25 = (f32[48,512]{1,0:T(8,128)S(1)}, f32[48,512]{1,0:T(8,128)S(1)}, u32[]{:S(2)}, u32[]{:S(2)}) collective-permute-start(f32[48,512]{1,0:T(8,128)S(1)} %get-tuple-element.19), channel_id=1, source_target_pairs={{0,32},{16,48},{32,0},{48,16},{64,96},{80,112},{96,64},{112,80},{1... | collective-permute-start | bytes 294920 | tf_op jit(solution)/shard_map/ppermute | solution.py:256
  48.8 1.3 %copy-start.11 = (f32[48,48,128]{2,1,0:T(8,128)S(1)}, f32[48,48,128]{2,1,0:T(8,128)}, u32[]{:S(2)}) copy-start(f32[48,48,128]{2,1,0:T(8,128)} %refs_18_.1) | copy-start | bytes 3538948
  50.1 38.4 %copy-start.5 = (f32[64,256]{1,0:T(8,128)S(1)}, f32[64,256]{1,0:T(8,128)}, u32[]{:S(2)}) copy-start(f32[64,256]{1,0:T(8,128)} %gate_ref.1) | copy-start | bytes 196612
  61.5 5.9 %collective-permute-start.17 = (f32[48,384]{1,0:T(8,128)S(1)}, f32[48,384]{1,0:T(8,128)S(1)}, u32[]{:S(2)}, u32[]{:S(2)}) collective-permute-start(f32[48,384]{1,0:T(8,128)S(1)} %get-tuple-element.17), channel_id=1, source_target_pairs={{0,8},{1,9},{2,10},{3,11},{4,12},{5,13},{6,14},{7,15},{8,0},{9,1},... | collective-permute-start | bytes 221192 | tf_op jit(solution)/shard_map/ppermute | solution.py:266
  62.8 32.0 %copy-start.1 = (f32[8,48,64]{2,1,0:T(8,128)S(1)}, f32[8,48,64]{2,1,0:T(8,128)}, u32[]{:S(2)}) copy-start(f32[8,48,64]{2,1,0:T(8,128)} %refs_13_.1) | copy-start | bytes 294916
  62.8 14.5 %collective-permute-start.29 = (f32[2,48,512]{2,1,0:T(8,128)S(1)}, f32[2,48,512]{2,1,0:T(8,128)S(1)}, u32[]{:S(2)}, u32[]{:S(2)}) collective-permute-start(f32[2,48,512]{2,1,0:T(8,128)S(1)} %pad_maximum_fusion.refs_0_), channel_id=1, source_target_pairs={{0,16},{16,0},{32,48},{48,32},{64,80},{80,64},{96,112},{112,96},{1... | collective-permute-start | bytes 589832 | tf_op jit(solution)/shard_map/ppermute | solution.py:260
  67.3 7.7 %collective-permute-start.21 = (f32[2,48,384]{2,1,0:T(8,128)S(1)}, f32[2,48,384]{2,1,0:T(8,128)S(1)}, u32[]{:S(2)}, u32[]{:S(2)}) collective-permute-start(f32[2,48,384]{2,1,0:T(8,128)S(1)} %pad_maximum_fusion.1.refs_0_), channel_id=1, source_target_pairs={{0,1},{1,2},{2,3},{3,4},{4,5},{5,6},{6,7},{7,0},{8,9},{9,10},{10,1... | collective-permute-start | bytes 442376 | tf_op jit(solution)/shard_map/ppermute | solution.py:272
  67.4 9.9 %collective-permute-start.18 = (f32[2,48,384]{2,1,0:T(8,128)S(1)}, f32[2,48,384]{2,1,0:T(8,128)S(1)}, u32[]{:S(2)}, u32[]{:S(2)}) collective-permute-start(f32[2,48,384]{2,1,0:T(8,128)S(1)} %pad_maximum_fusion.1.refs_0_), channel_id=1, source_target_pairs={{0,7},{1,0},{2,1},{3,2},{4,3},{5,4},{6,5},{7,6},{8,15},{9,8},{10,9... | collective-permute-start | bytes 442376 | tf_op jit(solution)/shard_map/ppermute | solution.py:275
  75.0 7.1 %collective-permute-start.22 = (f32[2,48,384]{2,1,0:T(8,128)S(1)}, f32[2,48,384]{2,1,0:T(8,128)S(1)}, u32[]{:S(2)}, u32[]{:S(2)}) collective-permute-start(f32[2,48,384]{2,1,0:T(8,128)S(1)} %collective-permute-done.21.refs_7_), channel_id=1, source_target_pairs={{0,1},{1,2},{2,3},{3,4},{4,5},{5,6},{6,7},{7,0},{8,9},{9,10},{10,1... | collective-permute-start | bytes 442376 | tf_op jit(solution)/shard_map/ppermute | solution.py:272
  75.0 7.1 %collective-permute-start.28 = (f32[2,48,512]{2,1,0:T(8,128)S(1)}, f32[2,48,512]{2,1,0:T(8,128)S(1)}, u32[]{:S(2)}, u32[]{:S(2)}) collective-permute-start(f32[2,48,512]{2,1,0:T(8,128)S(1)} %pad_maximum_fusion.refs_0_), channel_id=1, source_target_pairs={{0,64},{16,80},{32,96},{48,112},{64,128},{80,144},{96,160},{112,17... | collective-permute-start | bytes 589832 | tf_op jit(solution)/shard_map/ppermute | solution.py:258
  75.0 7.3 %collective-permute-start.27 = (f32[2,48,512]{2,1,0:T(8,128)S(1)}, f32[2,48,512]{2,1,0:T(8,128)S(1)}, u32[]{:S(2)}, u32[]{:S(2)}) collective-permute-start(f32[2,48,512]{2,1,0:T(8,128)S(1)} %pad_maximum_fusion.refs_0_), channel_id=1, source_target_pairs={{0,128},{16,144},{32,160},{48,176},{64,192},{80,208},{96,224},{112... | collective-permute-start | bytes 589832 | tf_op jit(solution)/shard_map/ppermute | solution.py:258
  77.3 7.0 %collective-permute-start.26 = (f32[2,48,512]{2,1,0:T(8,128)S(1)}, f32[2,48,512]{2,1,0:T(8,128)S(1)}, u32[]{:S(2)}, u32[]{:S(2)}) collective-permute-start(f32[2,48,512]{2,1,0:T(8,128)S(1)} %pad_maximum_fusion.refs_0_), channel_id=1, source_target_pairs={{0,192},{16,208},{32,224},{48,240},{64,0},{80,16},{96,32},{112,48}... | collective-permute-start | bytes 589832 | tf_op jit(solution)/shard_map/ppermute | solution.py:258
  77.3 7.0 %collective-permute-start.19 = (f32[2,48,384]{2,1,0:T(8,128)S(1)}, f32[2,48,384]{2,1,0:T(8,128)S(1)}, u32[]{:S(2)}, u32[]{:S(2)}) collective-permute-start(f32[2,48,384]{2,1,0:T(8,128)S(1)} %collective-permute-done.18.refs_1_), channel_id=1, source_target_pairs={{0,7},{1,0},{2,1},{3,2},{4,3},{5,4},{6,5},{7,6},{8,15},{9,8},{10,9... | collective-permute-start | bytes 442376 | tf_op jit(solution)/shard_map/ppermute | solution.py:275
  82.1 6.4 %collective-permute-start.23 = (f32[2,48,384]{2,1,0:T(8,128)S(1)}, f32[2,48,384]{2,1,0:T(8,128)S(1)}, u32[]{:S(2)}, u32[]{:S(2)}) collective-permute-start(f32[2,48,384]{2,1,0:T(8,128)S(1)} %collective-permute-done.22.refs_6_), channel_id=1, source_target_pairs={{0,1},{1,2},{2,3},{3,4},{4,5},{5,6},{6,7},{7,0},{8,9},{9,10},{10,1... | collective-permute-start | bytes 442376 | tf_op jit(solution)/shard_map/ppermute | solution.py:272
  82.1 6.4 %collective-permute-start.32 = (f32[2,48,512]{2,1,0:T(8,128)S(1)}, f32[2,48,512]{2,1,0:T(8,128)S(1)}, u32[]{:S(2)}, u32[]{:S(2)}) collective-permute-start(f32[2,48,512]{2,1,0:T(8,128)S(1)} %collective-permute-done.28.refs_3_), channel_id=1, source_target_pairs={{0,16},{16,0},{32,48},{48,32},{64,80},{80,64},{96,112},{112,96},{1... | collective-permute-start | bytes 589832 | tf_op jit(solution)/shard_map/ppermute | solution.py:260
  82.3 6.2 %collective-permute-start.31 = (f32[2,48,512]{2,1,0:T(8,128)S(1)}, f32[2,48,512]{2,1,0:T(8,128)S(1)}, u32[]{:S(2)}, u32[]{:S(2)}) collective-permute-start(f32[2,48,512]{2,1,0:T(8,128)S(1)} %collective-permute-done.27.refs_2_), channel_id=1, source_target_pairs={{0,16},{16,0},{32,48},{48,32},{64,80},{80,64},{96,112},{112,96},{1... | collective-permute-start | bytes 589832 | tf_op jit(solution)/shard_map/ppermute | solution.py:260
  84.3 4.2 %collective-permute-start.30 = (f32[2,48,512]{2,1,0:T(8,128)S(1)}, f32[2,48,512]{2,1,0:T(8,128)S(1)}, u32[]{:S(2)}, u32[]{:S(2)}) collective-permute-start(f32[2,48,512]{2,1,0:T(8,128)S(1)} %collective-permute-done.26.refs_1_), channel_id=1, source_target_pairs={{0,16},{16,0},{32,48},{48,32},{64,80},{80,64},{96,112},{112,96},{1... | collective-permute-start | bytes 589832 | tf_op jit(solution)/shard_map/ppermute | solution.py:260
  84.3 7.0 %collective-permute-start.20 = (f32[2,48,384]{2,1,0:T(8,128)S(1)}, f32[2,48,384]{2,1,0:T(8,128)S(1)}, u32[]{:S(2)}, u32[]{:S(2)}) collective-permute-start(f32[2,48,384]{2,1,0:T(8,128)S(1)} %collective-permute-done.19.refs_2_), channel_id=1, source_target_pairs={{0,7},{1,0},{2,1},{3,2},{4,3},{5,4},{6,5},{7,6},{8,15},{9,8},{10,9... | collective-permute-start | bytes 442376 | tf_op jit(solution)/shard_map/ppermute | solution.py:275
  88.5 6.4 %collective-permute-start.24 = (f32[2,48,384]{2,1,0:T(8,128)S(1)}, f32[2,48,384]{2,1,0:T(8,128)S(1)}, u32[]{:S(2)}, u32[]{:S(2)}) collective-permute-start(f32[2,48,384]{2,1,0:T(8,128)S(1)} %collective-permute-done.23.refs_5_), channel_id=1, source_target_pairs={{0,1},{1,2},{2,3},{3,4},{4,5},{5,6},{6,7},{7,0},{8,9},{9,10},{10,1... | collective-permute-start | bytes 442376 | tf_op jit(solution)/shard_map/ppermute | solution.py:272

commit v2 on v1

--- a/solution.py
+++ b/solution.py
@@ -46,18 +46,25 @@
     return second
 
 
-def first_kernel(seq_in, res_in, align_in, left_in, right_in, left_ref, right_ref, normed_ref, flat_ref, seq_ref, res_ref, align_ref, weight_ref, proj, sems):
-    copies = [
-        pltpu.make_async_copy(align_in, align_ref, sems.at[0]),
-        pltpu.make_async_copy(left_in, weight_ref.at[0], sems.at[1]),
-        pltpu.make_async_copy(right_in, weight_ref.at[1], sems.at[2]),
-        pltpu.make_async_copy(seq_in, seq_ref, sems.at[3]),
-        pltpu.make_async_copy(res_in, res_ref, sems.at[4]),
-    ]
+def copied(pairs, sems):
+    copies = [pltpu.make_async_copy(source, target, sems.at[k]) for k, (source, target) in enumerate(pairs)]
     for copy in copies:
         copy.start()
     for copy in copies:
         copy.wait()
+
+
+def first_kernel(seq_in, res_in, align_in, left_in, right_in, left_ref, right_ref, normed_ref, flat_ref, seq_ref, res_ref, align_ref, weight_ref, proj, sems):
+    copied(
+        [
+            (align_in, align_ref),
+            (left_in, weight_ref.at[0]),
+            (right_in, weight_ref.at[1]),
+            (seq_in, seq_ref),
+            (res_in, res_ref),
+        ],
+        sems,
+    )
     seqs, residues, width = align_ref.shape
     values = align_ref[...].reshape(seqs * residues, width)
     center = jnp.mean(values, axis=-1, keepdims=True)
@@ -92,8 +99,8 @@
     right_ref[:, residues * 32 :] = extra
 
 
-def weights_kernel(outer_ref, value_ref, out_weight_ref, mapped_ref, mixed_ref, out_ref, tall):
-    tall[...] = outer_ref[...]
+def weights_kernel(outer_in, value_in, out_weight_in, mapped_ref, mixed_ref, out_ref, tall, value_ref, out_weight_ref, sems):
+    copied([(outer_in, tall), (value_in, value_ref), (out_weight_in, out_weight_ref)], sems)
     for b in range(32):
         high, low = split_two(tall[pl.ds(b, 32, stride=32), :])
         mapped_ref[b * 32 : (b + 1) * 32, :LANES] = high
@@ -116,12 +123,50 @@
     out_ref[1] = low
 
 
+def outer_rows(left, first_row, res_ref, right_two, mapped_ref, pair_ref, heads_two, seen, pair_out_ref, logits_ref, outer, high_ref, low_ref):
+    cols = 48
+    left_high, left_low = split_two(left)
+    both = right_two[...]
+    outer[...] = mxu(both, jnp.concatenate([left_high, left_high], axis=0)) + mxu(both[:, :LANES], left_low)
+    for quad in range(ROWS_PER_STEP // 4):
+        for four in range(8):
+            parts = [
+                outer[(four * 4 + v) * cols : (four * 4 + v + 1) * cols, quad * LANES : (quad + 1) * LANES]
+                for v in range(4)
+            ]
+            for g, part in enumerate(swap_groups(parts)):
+                high, low = split_two(part)
+                at = (quad * 4 + g) * cols
+                high_ref[at : at + cols, four * LANES : (four + 1) * LANES] = high
+                low_ref[at : at + cols, four * LANES : (four + 1) * LANES] = low
+    wide = mxu(high_ref[...], mapped_ref[...])
+    sums = wide[:, :LANES] + wide[:, LANES:] + mxu(low_ref[...], mapped_ref[:, :LANES])
+    pairs = []
+    for i in range(ROWS_PER_STEP):
+        live = res_ref[first_row + i].astype(f32)
+        count = jnp.maximum(seen[0] * live, 1.0)
+        pair = pair_ref[i] + sums[i * cols : (i + 1) * cols] / count
+        pair_out_ref[i] = pair
+        pairs.append(pair)
+    pair = jnp.concatenate(pairs, axis=0)
+    centred = pair - jnp.mean(pair, axis=-1, keepdims=True)
+    normed = centred * lax.rsqrt(jnp.mean(centred * centred, axis=-1, keepdims=True) + epsilon)
+    high, low = split_two(normed)
+    normed_two = jnp.concatenate([high, low], axis=1)
+    logits = mxu(normed_two, heads_two[0]) + mxu(normed_two, heads_two[1])
+    lane = lax.broadcasted_iota(jnp.int32, (cols, LANES), 1)
+    line = jnp.zeros((cols, LANES), f32)
+    for i in range(ROWS_PER_STEP):
+        line = jnp.where(lane // 8 == i, pltpu.roll(logits[i * cols : (i + 1) * cols], 8 * i, 1) if i else logits[:cols], line)
+    logits_ref[...] = line + seen[1]
+
+
 def outer_kernel(*refs):
     res_ref = refs[0]
     left_pieces = refs[1 : 1 + Z_CHIPS]
     right_pieces = refs[1 + Z_CHIPS : 9 + Z_CHIPS]
-    mapped_ref, pair_ref, head_ref, pair_out_ref, logits_ref = refs[9 + Z_CHIPS : 14 + Z_CHIPS]
-    left_all, right_ref, tall, right_two, outer, high_ref, low_ref, seen, heads_two = refs[14 + Z_CHIPS :]
+    mapped_ref, head_ref, pair_ref, pair_out_ref, logits_ref, right_two, seen, heads_two = refs[9 + Z_CHIPS : 17 + Z_CHIPS]
+    left_all, right_ref, tall, outer, high_ref, low_ref = refs[17 + Z_CHIPS :]
     step = pl.program_id(0)
     cols = 48
 
@@ -157,40 +202,8 @@
         heads_two[1, :LANES] = head_low
         heads_two[1, LANES:] = head_low
 
-    left_high, left_low = split_two(left_all[:, pl.ds(pl.multiple_of(step * (ROWS_PER_STEP * 32), LANES), ROWS_PER_STEP * 32)])
-    both = right_two[...]
-    outer[...] = mxu(both, jnp.concatenate([left_high, left_high], axis=0)) + mxu(both[:, :LANES], left_low)
-    for quad in range(ROWS_PER_STEP // 4):
-        for four in range(8):
-            parts = [
-                outer[(four * 4 + v) * cols : (four * 4 + v + 1) * cols, quad * LANES : (quad + 1) * LANES]
-                for v in range(4)
-            ]
-            for g, part in enumerate(swap_groups(parts)):
-                high, low = split_two(part)
-                at = (quad * 4 + g) * cols
-                high_ref[at : at + cols, four * LANES : (four + 1) * LANES] = high
-                low_ref[at : at + cols, four * LANES : (four + 1) * LANES] = low
-    wide = mxu(high_ref[...], mapped_ref[...])
-    sums = wide[:, :LANES] + wide[:, LANES:] + mxu(low_ref[...], mapped_ref[:, :LANES])
-    pairs = []
-    for i in range(ROWS_PER_STEP):
-        live = res_ref[step * ROWS_PER_STEP + i].astype(f32)
-        count = jnp.maximum(seen[0] * live, 1.0)
-        pair = pair_ref[i] + sums[i * cols : (i + 1) * cols] / count
-        pair_out_ref[i] = pair
-        pairs.append(pair)
-    pair = jnp.concatenate(pairs, axis=0)
-    centred = pair - jnp.mean(pair, axis=-1, keepdims=True)
-    normed = centred * lax.rsqrt(jnp.mean(centred * centred, axis=-1, keepdims=True) + epsilon)
-    high, low = split_two(normed)
-    normed_two = jnp.concatenate([high, low], axis=1)
-    logits = mxu(normed_two, heads_two[0]) + mxu(normed_two, heads_two[1])
-    lane = lax.broadcasted_iota(jnp.int32, (cols, LANES), 1)
-    line = jnp.zeros((cols, LANES), f32)
-    for i in range(ROWS_PER_STEP):
-        line = jnp.where(lane // 8 == i, pltpu.roll(logits[i * cols : (i + 1) * cols], 8 * i, 1) if i else logits[:cols], line)
-    logits_ref[...] = line + seen[1]
+    left = left_all[:, pl.ds(pl.multiple_of(step * (ROWS_PER_STEP * 32), LANES), ROWS_PER_STEP * 32)]
+    outer_rows(left, step * ROWS_PER_STEP, res_ref, right_two, mapped_ref, pair_ref, heads_two, seen, pair_out_ref, logits_ref, outer, high_ref, low_ref)
 
 
 def middle_kernel(align_normed_ref, gate_ref, *refs):
@@ -260,21 +273,30 @@
     return pieces + [lax.ppermute(piece, axis, [(d, d ^ 1) for d in range(devices)]) for piece in pieces]
 
 
-def ring_pieces(shard, axis):
+def ring_pieces(shard, axis, *first):
     devices = lax.axis_size(axis)
     ring = Z_CHIPS
     other = lax.ppermute(shard, axis, [(d, (d + ring) % devices) for d in range(devices)])
-    ahead = [(d, d // ring * ring + (d + 1) % ring) for d in range(devices)]
-    back = [(d, d // ring * ring + (d + ring - 1) % ring) for d in range(devices)]
-    pieces = [None] * ring
-    pieces[0] = up = down = jnp.stack([shard, other])
-    for hop in range(1, ring // 2 + 1):
-        up = lax.ppermute(up, axis, ahead)
-        pieces[ring - hop] = up
-        if hop < ring // 2:
-            down = lax.ppermute(down, axis, back)
-            pieces[hop] = down
-    return pieces
+    both = after(jnp.stack([shard, other]), *first)
+
+    def further(piece, k):
+        return lax.ppermute(piece, axis, [(d, d // ring * ring + (d + ring - k) % ring) for d in range(devices)])
+
+    pieces = {0: both}
+    for k in (1, 7, 2, 6):
+        pieces[k] = further(both, k)
+    pieces[3] = further(pieces[2], 1)
+    pieces[5] = further(pieces[6], 7)
+    pieces[4] = further(pieces[2], 2)
+    return [pieces[k] for k in range(ring)]
+
+
+def in_hbm(array):
+    return pltpu.with_memory_space_constraint(array, pltpu.HBM)
+
+
+def after(value, *others):
+    return lax.optimization_barrier((value, *others))[0]
 
 
 def call(kernel, outs, limit, scratch=(), **more):
@@ -313,49 +335,55 @@
             pltpu.SemaphoreType.DMA((5,)),
         ],
         in_specs=[HBM] * 5,
-    )(seq_mask, res_mask, alignment, left_weight.T, right_weight.T)
+    )(*[in_hbm(a) for a in (seq_mask, res_mask, alignment, left_weight.T, right_weight.T)])
     turn = [(r * n_col + c, c * n_col + r) for r in range(n_row) for c in range(n_col)]
     right_here = lax.ppermute(right, ("row", "col"), turn)
-    left_pieces = ring_pieces(left, "col")
-    right_pieces = row_pieces(right_here, "row")
     mapped, mixed, out_two = call(
         weights_kernel,
         (shape((1024, 256), bf16), shape((8, 256, 256), bf16), shape((2, 256, 64), bf16)),
         12,
-        scratch=[pltpu.VMEM((1024, LANES), f32)],
-    )(w_outer, value_weight, output_weight.T)
+        scratch=[
+            pltpu.VMEM((1024, LANES), f32),
+            pltpu.VMEM(value_weight.shape, f32),
+            pltpu.VMEM((64, 256), f32),
+            pltpu.SemaphoreType.DMA((3,)),
+        ],
+        in_specs=[HBM] * 3,
+    )(*[in_hbm(a) for a in (w_outer, value_weight, output_weight.T)])
+    left_pieces = ring_pieces(left, "col", mapped)
+    right_pieces = row_pieces(right_here, "row")
     steps = rows // ROWS_PER_STEP
-    whole = lambda dims: pl.BlockSpec(dims, lambda t: (0,) * len(dims))
+    pair_rep = in_hbm(pair_rep)
+    pair_block = (ROWS_PER_STEP, cols, pair_width)
+    work = [
+        pltpu.VMEM((cols * 32, ROWS_PER_STEP * 32), f32),
+        pltpu.VMEM((ROWS_PER_STEP * cols, 1024), bf16),
+        pltpu.VMEM((ROWS_PER_STEP * cols, 1024), bf16),
+    ]
     pair_out, logits = pl.pallas_call(
         outer_kernel,
         grid=(steps,),
-        out_shape=(shape(pair_rep.shape), shape((cols, steps * LANES))),
-        in_specs=[SMEM]
-        + [whole(left_pieces[0].shape)] * 8
-        + [whole(right_pieces[0].shape)] * 8
-        + [
-            whole((1024, 256)),
-            pl.BlockSpec((ROWS_PER_STEP, cols, pair_width), lambda t: (t, 0, 0)),
-            whole((8, LANES)),
-        ],
+        out_shape=(
+            shape(pair_rep.shape),
+            shape((cols, steps * LANES)),
+        ),
+        in_specs=[SMEM] + [VMEM] * 18 + [pl.BlockSpec(pair_block, lambda t: (t, 0, 0))],
         out_specs=[
-            pl.BlockSpec((ROWS_PER_STEP, cols, pair_width), lambda t: (t, 0, 0)),
+            pl.BlockSpec(pair_block, lambda t: (t, 0, 0)),
             pl.BlockSpec((cols, LANES), lambda t: (0, t)),
         ],
         scratch_shapes=[
+            pltpu.VMEM((cols * 32, 256), bf16),
+            pltpu.VMEM((2, cols, LANES), f32),
+            pltpu.VMEM((2, 256, LANES), bf16),
             pltpu.VMEM((n_col * seqs, rows * 32), f32),
             pltpu.VMEM((n_row * seqs, rows * 32 + LANES), f32),
             pltpu.VMEM((cols * 32, LANES), f32),
-            pltpu.VMEM((cols * 32, 256), bf16),
-            pltpu.VMEM((cols * 32, ROWS_PER_STEP * 32), f32),
-            pltpu.VMEM((ROWS_PER_STEP * cols, 1024), bf16),
-            pltpu.VMEM((ROWS_PER_STEP * cols, 1024), bf16),
-            pltpu.VMEM((2, cols, LANES), f32),
-            pltpu.VMEM((2, 256, LANES), bf16),
-        ],
+        ]
+        + work,
         compiler_params=pltpu.CompilerParams(vmem_limit_bytes=32 * 1024 * 1024),
         cost_estimate=pl.CostEstimate(flops=10**10, bytes_accessed=10**7, transcendentals=0),
-    )(res_mask, *left_pieces, *right_pieces, mapped, pair_rep, w_logits.T)
+    )(res_mask, *left_pieces, *right_pieces, mapped, w_logits.T, pair_rep)
     normed_pieces = row_pieces(normed, "row")
     turned_high, turned_low, opened = call(
         middle_kernel,

time: 99.2 us -> 89.2 us (0.90)
  waiting for transfers between devices: 26.6 us -> 17 us
  local copies, waits for them, and re-layouts: 7.67 us -> 0.02 us
  starting transfers between devices: 45.1 us -> 51.3 us
  Pallas kernels: 18 us -> 19.7 us
    unnamed x26 -> x8, local copies, waits for them, and re-layouts: 7.67 us -> 0.02 us
    ppermute x14, waiting for transfers between devices: 18.3 us -> 14.2 us  [further(): lax.ppermute(piece, axis, [(d, d // ring * ring + (d + ring - k) % ring)...]
    ppermute x2, waiting for transfers between devices: 6.39 us -> 2.77 us  [ring_pieces(): lax.ppermute(shard, axis, [(d, (d + ring) % devices) for d in range(devic...]
    ppermute x14, starting transfers between devices: 20 us -> 23.1 us  [further(): lax.ppermute(piece, axis, [(d, d // ring * ring + (d + ring - k) % ring)...]
    ppermute x2, starting transfers between devices: 0.17 us -> 2.11 us  [row_pieces(): lax.ppermute(shard, axis, [(d, d ^ 2) for d in range(devices)])]
    ppermute x6, waiting for transfers between devices: 1.79 us -> 0.02 us  [row_pieces(): lax.ppermute(both, axis, [(d, (d + devices - 4 * k) % devices) for d in r...]
    ppermute x2, starting transfers between devices: 5.35 us -> 6.48 us  [ring_pieces(): lax.ppermute(shard, axis, [(d, (d + ring) % devices) for d in range(devic...]
    pallas_call x1, Pallas kernels: 1.07 us -> 2.12 us  [per_device(): call(weights_kernel, (shape((1024, 256), bf16), shape((8, 256, 256), bf16...]
  transfers between devices with their start and end apart: 33 -> 33, of which waited for: 12 -> 9; matrix products, arithmetic and copies ran while one was open for 0% -> 0% of each run, Pallas kernels for 13% -> 16%
where the time goes in v2:
time: 89.2 us; the launch traced here: 88.8 us
  starting transfers between devices  51.3 us (58%)
  Pallas kernels  19.7 us (22%)
  waiting for transfers between devices  17 us (19%)
    ppermute x14, starting transfers between devices, further(): lax.ppermute(piece, axis, [(d, d // ring * ring + (d + ring - k) % ring)...  23.1 us
    ppermute x14, waiting for transfers between devices, further(): lax.ppermute(piece, axis, [(d, d // ring * ring + (d + ring - k) % ring)...  14.2 us
    pallas_call x1, Pallas kernels, per_device(): pl.pallas_call(outer_kernel, grid=(steps,), out_shape=(shape(pair_rep.sha...  11.8 us
    ppermute x6, starting transfers between devices, row_pieces(): lax.ppermute(both, axis, [(d, (d + devices - 4 * k) % devices) for d in r...  9.3 us
    ppermute x1, starting transfers between devices, per_device(): right_here = lax.ppermute(right, ('row', 'col'), turn)  9.07 us
    ppermute x2, starting transfers between devices, ring_pieces(): lax.ppermute(shard, axis, [(d, (d + ring) % devices) for d in range(devic...  6.48 us
    pallas_call x1, Pallas kernels, per_device(): call(last_kernel, shape(alignment.shape), 24, scratch=[pltpu.VMEM((n_row...  3.34 us
    ppermute x2, waiting for transfers between devices, ring_pieces(): lax.ppermute(shard, axis, [(d, (d + ring) % devices) for d in range(devic...  2.77 us
  transfers between devices with their start and end apart: 33, of which 9 were waited for; matrix products, arithmetic and copies ran while one was open for 0% of the time, Pallas kernels for 16%

profile of v2, /device:TPU:2, one launch (start us, length us, event | category | flops | bytes accessed | tf_op | source)
XLA Modules:
  0.0 88.8 jit_solution(7304923788019852453)
XLA Ops:
  0.7 1.7 %shard_map.122 = (f32[8,1536]{1,0:T(8,128)S(1)}, f32[8,1664]{1,0:T(8,128)S(1)}, f32[48,512]{1,0:T(8,128)S(1)}, f32[384,64]{1,0:T(8,128)S(1)}) custom-call(s32[8]{0:T(128)} %seq_in.1, s32[48]{0:T(128)} %refs_0_.1, f32[8,48,64]{2,1,0:T(8,128)} %refs_13_.1, f32[32,64]{1,0:T(8,128)} %bitcast.22, f32[32,64]{1,0:T(8,128)} %bitcast.23), custom_call_target="tpu_custom_call" | custom-call | tf_op jit(solution)/shard_map/pallas_call | solution.py:325
  2.4 9.1 %collective-permute-start.8 = (f32[8,1664]{1,0:T(8,128)S(1)}, f32[8,1664]{1,0:T(8,128)S(1)}, u32[]{:S(2)}, u32[]{:S(2)}) collective-permute-start(f32[8,1664]{1,0:T(8,128)S(1)} %get-tuple-element.18), channel_id=1, source_target_pairs={{0,0},{1,16},{2,32},{3,48},{4,64},{5,80},{6,96},{7,112},{8,128},{9... | collective-permute-start | bytes 159752 | tf_op jit(solution)/shard_map/ppermute | solution.py:340
  11.5 4.0 %collective-permute-start = (f32[8,1536]{1,0:T(8,128)S(1)}, f32[8,1536]{1,0:T(8,128)S(1)}, u32[]{:S(2)}, u32[]{:S(2)}) collective-permute-start(f32[8,1536]{1,0:T(8,128)S(1)} %get-tuple-element.15), channel_id=1, source_target_pairs={{0,8},{1,9},{2,10},{3,11},{4,12},{5,13},{6,14},{7,15},{8,0},{9,1},... | collective-permute-start | bytes 147464 | tf_op jit(solution)/shard_map/ppermute | solution.py:279
  15.5 2.1 %shard_map.123 = (bf16[1024,256]{1,0:T(8,128)(2,1)S(1)}, bf16[8,256,256]{2,1,0:T(8,128)(2,1)S(1)}, bf16[2,256,64]{2,1,0:T(8,128)(2,1)S(1)}) custom-call(f32[1024,128]{1,0:T(8,128)} %outer_in.1, f32[64,256]{1,0:T(8,128)} %value_in.1, f32[64,256]{1,0:T(8,128)} %bitcast.18), custom_call_target="tpu_custom_call" | custom-call | tf_op jit(solution)/shard_map/pallas_call | solution.py:341
  17.6 2.1 %collective-permute-start.9 = (f32[8,1664]{1,0:T(8,128)S(1)}, f32[8,1664]{1,0:T(8,128)S(1)}, u32[]{:S(2)}, u32[]{:S(2)}) collective-permute-start(f32[8,1664]{1,0:T(8,128)S(1)} %collective-permute-done.8), channel_id=1, source_target_pairs={{0,32},{16,48},{32,0},{48,16},{64,96},{80,112},{96,64},{112,80},{1... | collective-permute-start | bytes 159752 | tf_op jit(solution)/shard_map/ppermute | solution.py:269
  19.8 0.1 collective-permute-start.7
  19.8 1.1 %collective-permute-start.5 = (f32[2,8,1536]{2,1,0:T(8,128)S(1)}, f32[2,8,1536]{2,1,0:T(8,128)S(1)}, u32[]{:S(2)}, u32[]{:S(2)}) collective-permute-start(f32[2,8,1536]{2,1,0:T(8,128)S(1)} %pad_maximum_fusion.3.refs_1_), channel_id=1, source_target_pairs={{0,2},{1,3},{2,4},{3,5},{4,6},{5,7},{6,0},{7,1},{8,10},{9,11},{10,... | collective-permute-start | bytes 294920 | tf_op jit(solution)/shard_map/ppermute | solution.py:283
  21.0 3.1 %collective-permute-start.2 = (f32[2,8,1536]{2,1,0:T(8,128)S(1)}, f32[2,8,1536]{2,1,0:T(8,128)S(1)}, u32[]{:S(2)}, u32[]{:S(2)}) collective-permute-start(f32[2,8,1536]{2,1,0:T(8,128)S(1)} %pad_maximum_fusion.3.refs_1_), channel_id=1, source_target_pairs={{0,6},{1,7},{2,0},{3,1},{4,2},{5,3},{6,4},{7,5},{8,14},{9,15},{10,... | collective-permute-start | bytes 294920 | tf_op jit(solution)/shard_map/ppermute | solution.py:283
  24.1 1.9 %collective-permute-start.1 = (f32[2,8,1536]{2,1,0:T(8,128)S(1)}, f32[2,8,1536]{2,1,0:T(8,128)S(1)}, u32[]{:S(2)}, u32[]{:S(2)}) collective-permute-start(f32[2,8,1536]{2,1,0:T(8,128)S(1)} %pad_maximum_fusion.3.refs_1_), channel_id=1, source_target_pairs={{0,7},{1,0},{2,1},{3,2},{4,3},{5,4},{6,5},{7,6},{8,15},{9,8},{10,9... | collective-permute-start | bytes 294920 | tf_op jit(solution)/shard_map/ppermute | solution.py:283
  26.0 0.1 collective-permute-start.13
  26.1 1.9 %collective-permute-done.7.refs_8_ = f32[2,8,1536]{2,1,0:T(8,128)S(1)} collective-permute-done((f32[2,8,1536]{2,1,0:T(8,128)S(1)}, f32[2,8,1536]{2,1,0:T(8,128)S(1)}, u32[]{:S(2)}, u32[]{:S(2)}) %collective-permute-start.7) | collective-permute-done | bytes 98336 | tf_op jit(solution)/shard_map/ppermute | solution.py:283
  28.0 0.0 collective-permute-done.5.refs_7_
  28.0 2.3 %collective-permute-start.11 = (f32[2,8,1664]{2,1,0:T(8,128)S(1)}, f32[2,8,1664]{2,1,0:T(8,128)S(1)}, u32[]{:S(2)}, u32[]{:S(2)}) collective-permute-start(f32[2,8,1664]{2,1,0:T(8,128)S(1)} %pad_maximum_fusion.2.refs_9_), channel_id=1, source_target_pairs={{0,128},{16,144},{32,160},{48,176},{64,192},{80,208},{96,224},{112... | collective-permute-start | bytes 319496 | tf_op jit(solution)/shard_map/ppermute | solution.py:271
  30.3 0.0 collective-permute-done.2.refs_3_
  30.3 2.6 %collective-permute-start.10 = (f32[2,8,1664]{2,1,0:T(8,128)S(1)}, f32[2,8,1664]{2,1,0:T(8,128)S(1)}, u32[]{:S(2)}, u32[]{:S(2)}) collective-permute-start(f32[2,8,1664]{2,1,0:T(8,128)S(1)} %pad_maximum_fusion.2.refs_9_), channel_id=1, source_target_pairs={{0,192},{16,208},{32,224},{48,240},{64,0},{80,16},{96,32},{112,48}... | collective-permute-start | bytes 319496 | tf_op jit(solution)/shard_map/ppermute | solution.py:271
  32.9 0.0 collective-permute-done.1.refs_2_
  32.9 0.0 collective-permute-start.6
  32.9 0.0 collective-permute-done.13.refs_13_
  32.9 3.0 %collective-permute-start.4 = (f32[2,8,1536]{2,1,0:T(8,128)S(1)}, f32[2,8,1536]{2,1,0:T(8,128)S(1)}, u32[]{:S(2)}, u32[]{:S(2)}) collective-permute-start(f32[2,8,1536]{2,1,0:T(8,128)S(1)} %collective-permute-done.2.refs_3_), channel_id=1, source_target_pairs={{0,6},{1,7},{2,0},{3,1},{4,2},{5,3},{6,4},{7,5},{8,14},{9,15},{10,... | collective-permute-start | bytes 294920 | tf_op jit(solution)/shard_map/ppermute | solution.py:283
  36.0 1.0 %collective-permute-start.3 = (f32[2,8,1536]{2,1,0:T(8,128)S(1)}, f32[2,8,1536]{2,1,0:T(8,128)S(1)}, u32[]{:S(2)}, u32[]{:S(2)}) collective-permute-start(f32[2,8,1536]{2,1,0:T(8,128)S(1)} %collective-permute-done.2.refs_3_), channel_id=1, source_target_pairs={{0,7},{1,0},{2,1},{3,2},{4,3},{5,4},{6,5},{7,6},{8,15},{9,8},{10,9... | collective-permute-start | bytes 294920 | tf_op jit(solution)/shard_map/ppermute | solution.py:283
  37.0 0.5 collective-permute-start.15
  37.5 1.2 %collective-permute-done.6.refs_6_ = f32[2,8,1536]{2,1,0:T(8,128)S(1)} collective-permute-done((f32[2,8,1536]{2,1,0:T(8,128)S(1)}, f32[2,8,1536]{2,1,0:T(8,128)S(1)}, u32[]{:S(2)}, u32[]{:S(2)}) %collective-permute-start.6) | collective-permute-done | bytes 98336 | tf_op jit(solution)/shard_map/ppermute | solution.py:283
  38.7 0.0 collective-permute-start.14
  38.8 1.5 %collective-permute-done.4.refs_5_ = f32[2,8,1536]{2,1,0:T(8,128)S(1)} collective-permute-done((f32[2,8,1536]{2,1,0:T(8,128)S(1)}, f32[2,8,1536]{2,1,0:T(8,128)S(1)}, u32[]{:S(2)}, u32[]{:S(2)}) %collective-permute-start.4) | collective-permute-done | bytes 98336 | tf_op jit(solution)/shard_map/ppermute | solution.py:283
  40.3 0.0 collective-permute-start.29
  40.3 1.1 %collective-permute-done.3.refs_4_ = f32[2,8,1536]{2,1,0:T(8,128)S(1)} collective-permute-done((f32[2,8,1536]{2,1,0:T(8,128)S(1)}, f32[2,8,1536]{2,1,0:T(8,128)S(1)}, u32[]{:S(2)}, u32[]{:S(2)}) %collective-permute-start.3) | collective-permute-done | bytes 98336 | tf_op jit(solution)/shard_map/ppermute | solution.py:283
  41.4 0.6 collective-permute-start.28
  42.0 2.8 %collective-permute-start.27 = (f32[2,48,512]{2,1,0:T(8,128)S(1)}, f32[2,48,512]{2,1,0:T(8,128)S(1)}, u32[]{:S(2)}, u32[]{:S(2)}) collective-permute-start(f32[2,48,512]{2,1,0:T(8,128)S(1)} %pad_maximum_fusion.refs_0_), channel_id=1, source_target_pairs={{0,128},{16,144},{32,160},{48,176},{64,192},{80,208},{96,224},{112... | collective-permute-start | bytes 589832 | tf_op jit(solution)/shard_map/ppermute | solution.py:271
  44.8 0.9 %collective-permute-start.26 = (f32[2,48,512]{2,1,0:T(8,128)S(1)}, f32[2,48,512]{2,1,0:T(8,128)S(1)}, u32[]{:S(2)}, u32[]{:S(2)}) collective-permute-start(f32[2,48,512]{2,1,0:T(8,128)S(1)} %pad_maximum_fusion.refs_0_), channel_id=1, source_target_pairs={{0,192},{16,208},{32,224},{48,240},{64,0},{80,16},{96,32},{112,48}... | collective-permute-start | bytes 589832 | tf_op jit(solution)/shard_map/ppermute | solution.py:271
  45.8 0.0 copy-start.1
  45.8 11.8 %shard_map.124 = (f32[48,48,128]{2,1,0:T(8,128)}, f32[48,384]{1,0:T(8,128)S(1)}) custom-call(s32[48]{0:T(128)S(1)} %copy-done.2, f32[2,8,1536]{2,1,0:T(8,128)S(1)} %pad_maximum_fusion.3.refs_1_, f32[2,8,1536]{2,1,0:T(8,128)S(1)} %collective-permute-done.1.refs_2_, f32[2,8,1536]{2,1,0:T(8,128)S(1)} %collective-permute-done.2.refs_3_, ...), custom_call_target="tpu_custom_call" | custom-call | flops 10000000000 | bytes 10000000 | tf_op jit(solution)/shard_map/pallas_call | solution.py:363
  57.6 2.5 %collective-permute-start.17 = (f32[48,384]{1,0:T(8,128)S(1)}, f32[48,384]{1,0:T(8,128)S(1)}, u32[]{:S(2)}, u32[]{:S(2)}) collective-permute-start(f32[48,384]{1,0:T(8,128)S(1)} %get-tuple-element.19), channel_id=1, source_target_pairs={{0,8},{1,9},{2,10},{3,11},{4,12},{5,13},{6,14},{7,15},{8,0},{9,1},... | collective-permute-start | bytes 221192 | tf_op jit(solution)/shard_map/ppermute | solution.py:279
  60.1 0.5 collective-permute-start.31
  60.6 0.1 collective-permute-start.30
  60.7 2.8 %collective-permute-done.17 = f32[48,384]{1,0:T(8,128)S(1)} collective-permute-done((f32[48,384]{1,0:T(8,128)S(1)}, f32[48,384]{1,0:T(8,128)S(1)}, u32[]{:S(2)}, u32[]{:S(2)}) %collective-permute-start.17) | collective-permute-done | bytes 73760 | tf_op jit(solution)/shard_map/ppermute | solution.py:279
  63.5 2.4 %collective-permute-start.22 = (f32[2,48,384]{2,1,0:T(8,128)S(1)}, f32[2,48,384]{2,1,0:T(8,128)S(1)}, u32[]{:S(2)}, u32[]{:S(2)}) collective-permute-start(f32[2,48,384]{2,1,0:T(8,128)S(1)} %pad_maximum_fusion.1.refs_0_), channel_id=1, source_target_pairs={{0,2},{1,3},{2,4},{3,5},{4,6},{5,7},{6,0},{7,1},{8,10},{9,11},{10,... | collective-permute-start | bytes 442376 | tf_op jit(solution)/shard_map/ppermute | solution.py:283
  65.8 1.8 %collective-permute-start.19 = (f32[2,48,384]{2,1,0:T(8,128)S(1)}, f32[2,48,384]{2,1,0:T(8,128)S(1)}, u32[]{:S(2)}, u32[]{:S(2)}) collective-permute-start(f32[2,48,384]{2,1,0:T(8,128)S(1)} %pad_maximum_fusion.1.refs_0_), channel_id=1, source_target_pairs={{0,6},{1,7},{2,0},{3,1},{4,2},{5,3},{6,4},{7,5},{8,14},{9,15},{10,... | collective-permute-start | bytes 442376 | tf_op jit(solution)/shard_map/ppermute | solution.py:283
  67.7 0.0 collective-permute-start.24
  67.7 3.2 %collective-permute-start.18 = (f32[2,48,384]{2,1,0:T(8,128)S(1)}, f32[2,48,384]{2,1,0:T(8,128)S(1)}, u32[]{:S(2)}, u32[]{:S(2)}) collective-permute-start(f32[2,48,384]{2,1,0:T(8,128)S(1)} %pad_maximum_fusion.1.refs_0_), channel_id=1, source_target_pairs={{0,7},{1,0},{2,1},{3,2},{4,3},{5,4},{6,5},{7,6},{8,15},{9,8},{10,9... | collective-permute-start | bytes 442376 | tf_op jit(solution)/shard_map/ppermute | solution.py:283
  70.9 2.0 %collective-permute-done.22.refs_6_ = f32[2,48,384]{2,1,0:T(8,128)S(1)} collective-permute-done((f32[2,48,384]{2,1,0:T(8,128)S(1)}, f32[2,48,384]{2,1,0:T(8,128)S(1)}, u32[]{:S(2)}, u32[]{:S(2)}) %collective-permute-start.22) | collective-permute-done | bytes 147488 | tf_op jit(solution)/shard_map/ppermute | solution.py:283
  72.9 1.5 %collective-permute-start.23 = (f32[2,48,384]{2,1,0:T(8,128)S(1)}, f32[2,48,384]{2,1,0:T(8,128)S(1)}, u32[]{:S(2)}, u32[]{:S(2)}) collective-permute-start(f32[2,48,384]{2,1,0:T(8,128)S(1)} %collective-permute-done.22.refs_6_), channel_id=1, source_target_pairs={{0,1},{1,2},{2,3},{3,4},{4,5},{5,6},{6,7},{7,0},{8,9},{9,10},{10,1... | collective-permute-start | bytes 442376 | tf_op jit(solution)/shard_map/ppermute | solution.py:283
  74.5 2.8 %collective-permute-start.21 = (f32[2,48,384]{2,1,0:T(8,128)S(1)}, f32[2,48,384]{2,1,0:T(8,128)S(1)}, u32[]{:S(2)}, u32[]{:S(2)}) collective-permute-start(f32[2,48,384]{2,1,0:T(8,128)S(1)} %collective-permute-done.19.refs_2_), channel_id=1, source_target_pairs={{0,6},{1,7},{2,0},{3,1},{4,2},{5,3},{6,4},{7,5},{8,14},{9,15},{10,... | collective-permute-start | bytes 442376 | tf_op jit(solution)/shard_map/ppermute | solution.py:283
  77.3 1.0 %collective-permute-start.20 = (f32[2,48,384]{2,1,0:T(8,128)S(1)}, f32[2,48,384]{2,1,0:T(8,128)S(1)}, u32[]{:S(2)}, u32[]{:S(2)}) collective-permute-start(f32[2,48,384]{2,1,0:T(8,128)S(1)} %collective-permute-done.19.refs_2_), channel_id=1, source_target_pairs={{0,7},{1,0},{2,1},{3,2},{4,3},{5,4},{6,5},{7,6},{8,15},{9,8},{10,9... | collective-permute-start | bytes 442376 | tf_op jit(solution)/shard_map/ppermute | solution.py:283
  78.3 0.6 shard_map.125
  78.9 0.6 collective-permute-done.18.refs_1_
  79.5 4.6 %collective-permute-done.21.refs_4_ = f32[2,48,384]{2,1,0:T(8,128)S(1)} collective-permute-done((f32[2,48,384]{2,1,0:T(8,128)S(1)}, f32[2,48,384]{2,1,0:T(8,128)S(1)}, u32[]{:S(2)}, u32[]{:S(2)}) %collective-permute-start.21) | collective-permute-done | bytes 147488 | tf_op jit(solution)/shard_map/ppermute | solution.py:283
  84.1 1.3 %collective-permute-done.20.refs_3_ = f32[2,48,384]{2,1,0:T(8,128)S(1)} collective-permute-done((f32[2,48,384]{2,1,0:T(8,128)S(1)}, f32[2,48,384]{2,1,0:T(8,128)S(1)}, u32[]{:S(2)}, u32[]{:S(2)}) %collective-permute-start.20) | collective-permute-done | bytes 147488 | tf_op jit(solution)/shard_map/ppermute | solution.py:283
  85.5 3.3 %shard_map.126 = f32[8,48,64]{2,1,0:T(8,128)} custom-call(f32[2,48,384]{2,1,0:T(8,128)S(1)} %pad_maximum_fusion.1.refs_0_, f32[2,48,384]{2,1,0:T(8,128)S(1)} %collective-permute-done.18.refs_1_, f32[2,48,384]{2,1,0:T(8,128)S(1)} %collective-permute-done.19.refs_2_, f32[2,48,384]{2,1,0:T(8,128)S(1)} %collective-permute-done.20.refs_3_, ...), custom_call_target="tpu_custom_call" | custom-call | tf_op jit(solution)/shard_map/pallas_call | solution.py:395
  (35 shorter events, 0.1 us)
Async XLA Ops:
  0.6 45.1 %copy-start.2 = (s32[48]{0:T(128)S(1)}, s32[48]{0:T(128)}, u32[]{:S(2)}) copy-start(s32[48]{0:T(128)} %refs_0_.1) | copy-start | bytes 580
  0.6 45.1 %copy-start.3 = (f32[128,8]{0,1:T(8,128)S(1)}, f32[128,8]{0,1:T(8,128)}, u32[]{:S(2)}) copy-start(f32[128,8]{0,1:T(8,128)} %param.18) | copy-start | bytes 12292
  2.4 15.2 %collective-permute-start.8 = (f32[8,1664]{1,0:T(8,128)S(1)}, f32[8,1664]{1,0:T(8,128)S(1)}, u32[]{:S(2)}, u32[]{:S(2)}) collective-permute-start(f32[8,1664]{1,0:T(8,128)S(1)} %get-tuple-element.18), channel_id=1, source_target_pairs={{0,0},{1,16},{2,32},{3,48},{4,64},{5,80},{6,96},{7,112},{8,128},{9... | collective-permute-start | bytes 159752 | tf_op jit(solution)/shard_map/ppermute | solution.py:340
  11.5 8.3 %collective-permute-start = (f32[8,1536]{1,0:T(8,128)S(1)}, f32[8,1536]{1,0:T(8,128)S(1)}, u32[]{:S(2)}, u32[]{:S(2)}) collective-permute-start(f32[8,1536]{1,0:T(8,128)S(1)} %get-tuple-element.15), channel_id=1, source_target_pairs={{0,8},{1,9},{2,10},{3,11},{4,12},{5,13},{6,14},{7,15},{8,0},{9,1},... | collective-permute-start | bytes 147464 | tf_op jit(solution)/shard_map/ppermute | solution.py:279
  15.5 10.5 %collective-permute-start.25 = (f32[48,512]{1,0:T(8,128)S(1)}, f32[48,512]{1,0:T(8,128)S(1)}, u32[]{:S(2)}, u32[]{:S(2)}) collective-permute-start(f32[48,512]{1,0:T(8,128)S(1)} %get-tuple-element.21), channel_id=1, source_target_pairs={{0,32},{16,48},{32,0},{48,16},{64,96},{80,112},{96,64},{112,80},{1... | collective-permute-start | bytes 294920 | tf_op jit(solution)/shard_map/ppermute | solution.py:269
  17.6 6.4 %collective-permute-start.9 = (f32[8,1664]{1,0:T(8,128)S(1)}, f32[8,1664]{1,0:T(8,128)S(1)}, u32[]{:S(2)}, u32[]{:S(2)}) collective-permute-start(f32[8,1664]{1,0:T(8,128)S(1)} %collective-permute-done.8), channel_id=1, source_target_pairs={{0,32},{16,48},{32,0},{48,16},{64,96},{80,112},{96,64},{112,80},{1... | collective-permute-start | bytes 159752 | tf_op jit(solution)/shard_map/ppermute | solution.py:269
  19.8 8.2 %collective-permute-start.7 = (f32[2,8,1536]{2,1,0:T(8,128)S(1)}, f32[2,8,1536]{2,1,0:T(8,128)S(1)}, u32[]{:S(2)}, u32[]{:S(2)}) collective-permute-start(f32[2,8,1536]{2,1,0:T(8,128)S(1)} %pad_maximum_fusion.3.refs_1_), channel_id=1, source_target_pairs={{0,1},{1,2},{2,3},{3,4},{4,5},{5,6},{6,7},{7,0},{8,9},{9,10},{10,1... | collective-permute-start | bytes 294920 | tf_op jit(solution)/shard_map/ppermute | solution.py:283
  19.8 8.1 %collective-permute-start.5 = (f32[2,8,1536]{2,1,0:T(8,128)S(1)}, f32[2,8,1536]{2,1,0:T(8,128)S(1)}, u32[]{:S(2)}, u32[]{:S(2)}) collective-permute-start(f32[2,8,1536]{2,1,0:T(8,128)S(1)} %pad_maximum_fusion.3.refs_1_), channel_id=1, source_target_pairs={{0,2},{1,3},{2,4},{3,5},{4,6},{5,7},{6,0},{7,1},{8,10},{9,11},{10,... | collective-permute-start | bytes 294920 | tf_op jit(solution)/shard_map/ppermute | solution.py:283
  21.0 9.3 %collective-permute-start.2 = (f32[2,8,1536]{2,1,0:T(8,128)S(1)}, f32[2,8,1536]{2,1,0:T(8,128)S(1)}, u32[]{:S(2)}, u32[]{:S(2)}) collective-permute-start(f32[2,8,1536]{2,1,0:T(8,128)S(1)} %pad_maximum_fusion.3.refs_1_), channel_id=1, source_target_pairs={{0,6},{1,7},{2,0},{3,1},{4,2},{5,3},{6,4},{7,5},{8,14},{9,15},{10,... | collective-permute-start | bytes 294920 | tf_op jit(solution)/shard_map/ppermute | solution.py:283
  24.1 8.9 %collective-permute-start.1 = (f32[2,8,1536]{2,1,0:T(8,128)S(1)}, f32[2,8,1536]{2,1,0:T(8,128)S(1)}, u32[]{:S(2)}, u32[]{:S(2)}) collective-permute-start(f32[2,8,1536]{2,1,0:T(8,128)S(1)} %pad_maximum_fusion.3.refs_1_), channel_id=1, source_target_pairs={{0,7},{1,0},{2,1},{3,2},{4,3},{5,4},{6,5},{7,6},{8,15},{9,8},{10,9... | collective-permute-start | bytes 294920 | tf_op jit(solution)/shard_map/ppermute | solution.py:283
  26.0 6.9 %collective-permute-start.13 = (f32[2,8,1664]{2,1,0:T(8,128)S(1)}, f32[2,8,1664]{2,1,0:T(8,128)S(1)}, u32[]{:S(2)}, u32[]{:S(2)}) collective-permute-start(f32[2,8,1664]{2,1,0:T(8,128)S(1)} %pad_maximum_fusion.2.refs_9_), channel_id=1, source_target_pairs={{0,16},{16,0},{32,48},{48,32},{64,80},{80,64},{96,112},{112,96},{1... | collective-permute-start | bytes 319496 | tf_op jit(solution)/shard_map/ppermute | solution.py:273
  28.0 8.0 %collective-permute-start.12 = (f32[2,8,1664]{2,1,0:T(8,128)S(1)}, f32[2,8,1664]{2,1,0:T(8,128)S(1)}, u32[]{:S(2)}, u32[]{:S(2)}) collective-permute-start(f32[2,8,1664]{2,1,0:T(8,128)S(1)} %pad_maximum_fusion.2.refs_9_), channel_id=1, source_target_pairs={{0,64},{16,80},{32,96},{48,112},{64,128},{80,144},{96,160},{112,17... | collective-permute-start | bytes 319496 | tf_op jit(solution)/shard_map/ppermute | solution.py:271
  28.0 9.0 %collective-permute-start.11 = (f32[2,8,1664]{2,1,0:T(8,128)S(1)}, f32[2,8,1664]{2,1,0:T(8,128)S(1)}, u32[]{:S(2)}, u32[]{:S(2)}) collective-permute-start(f32[2,8,1664]{2,1,0:T(8,128)S(1)} %pad_maximum_fusion.2.refs_9_), channel_id=1, source_target_pairs={{0,128},{16,144},{32,160},{48,176},{64,192},{80,208},{96,224},{112... | collective-permute-start | bytes 319496 | tf_op jit(solution)/shard_map/ppermute | solution.py:271
  30.3 6.7 %collective-permute-start.10 = (f32[2,8,1664]{2,1,0:T(8,128)S(1)}, f32[2,8,1664]{2,1,0:T(8,128)S(1)}, u32[]{:S(2)}, u32[]{:S(2)}) collective-permute-start(f32[2,8,1664]{2,1,0:T(8,128)S(1)} %pad_maximum_fusion.2.refs_9_), channel_id=1, source_target_pairs={{0,192},{16,208},{32,224},{48,240},{64,0},{80,16},{96,32},{112,48}... | collective-permute-start | bytes 319496 | tf_op jit(solution)/shard_map/ppermute | solution.py:271
  32.9 5.8 %collective-permute-start.6 = (f32[2,8,1536]{2,1,0:T(8,128)S(1)}, f32[2,8,1536]{2,1,0:T(8,128)S(1)}, u32[]{:S(2)}, u32[]{:S(2)}) collective-permute-start(f32[2,8,1536]{2,1,0:T(8,128)S(1)} %collective-permute-done.5.refs_7_), channel_id=1, source_target_pairs={{0,1},{1,2},{2,3},{3,4},{4,5},{5,6},{6,7},{7,0},{8,9},{9,10},{10,1... | collective-permute-start | bytes 294920 | tf_op jit(solution)/shard_map/ppermute | solution.py:283
  32.9 7.3 %collective-permute-start.4 = (f32[2,8,1536]{2,1,0:T(8,128)S(1)}, f32[2,8,1536]{2,1,0:T(8,128)S(1)}, u32[]{:S(2)}, u32[]{:S(2)}) collective-permute-start(f32[2,8,1536]{2,1,0:T(8,128)S(1)} %collective-permute-done.2.refs_3_), channel_id=1, source_target_pairs={{0,6},{1,7},{2,0},{3,1},{4,2},{5,3},{6,4},{7,5},{8,14},{9,15},{10,... | collective-permute-start | bytes 294920 | tf_op jit(solution)/shard_map/ppermute | solution.py:283
  36.0 5.4 %collective-permute-start.3 = (f32[2,8,1536]{2,1,0:T(8,128)S(1)}, f32[2,8,1536]{2,1,0:T(8,128)S(1)}, u32[]{:S(2)}, u32[]{:S(2)}) collective-permute-start(f32[2,8,1536]{2,1,0:T(8,128)S(1)} %collective-permute-done.2.refs_3_), channel_id=1, source_target_pairs={{0,7},{1,0},{2,1},{3,2},{4,3},{5,4},{6,5},{7,6},{8,15},{9,8},{10,9... | collective-permute-start | bytes 294920 | tf_op jit(solution)/shard_map/ppermute | solution.py:283
  37.0 5.0 %collective-permute-start.16 = (f32[2,8,1664]{2,1,0:T(8,128)S(1)}, f32[2,8,1664]{2,1,0:T(8,128)S(1)}, u32[]{:S(2)}, u32[]{:S(2)}) collective-permute-start(f32[2,8,1664]{2,1,0:T(8,128)S(1)} %collective-permute-done.12.refs_12_), channel_id=1, source_target_pairs={{0,16},{16,0},{32,48},{48,32},{64,80},{80,64},{96,112},{112,96},{1... | collective-permute-start | bytes 319496 | tf_op jit(solution)/shard_map/ppermute | solution.py:273
  37.0 7.8 %collective-permute-start.15 = (f32[2,8,1664]{2,1,0:T(8,128)S(1)}, f32[2,8,1664]{2,1,0:T(8,128)S(1)}, u32[]{:S(2)}, u32[]{:S(2)}) collective-permute-start(f32[2,8,1664]{2,1,0:T(8,128)S(1)} %collective-permute-done.11.refs_11_), channel_id=1, source_target_pairs={{0,16},{16,0},{32,48},{48,32},{64,80},{80,64},{96,112},{112,96},{1... | collective-permute-start | bytes 319496 | tf_op jit(solution)/shard_map/ppermute | solution.py:273
  38.7 7.0 %collective-permute-start.14 = (f32[2,8,1664]{2,1,0:T(8,128)S(1)}, f32[2,8,1664]{2,1,0:T(8,128)S(1)}, u32[]{:S(2)}, u32[]{:S(2)}) collective-permute-start(f32[2,8,1664]{2,1,0:T(8,128)S(1)} %collective-permute-done.10.refs_10_), channel_id=1, source_target_pairs={{0,16},{16,0},{32,48},{48,32},{64,80},{80,64},{96,112},{112,96},{1... | collective-permute-start | bytes 319496 | tf_op jit(solution)/shard_map/ppermute | solution.py:273
  40.3 25.6 %collective-permute-start.29 = (f32[2,48,512]{2,1,0:T(8,128)S(1)}, f32[2,48,512]{2,1,0:T(8,128)S(1)}, u32[]{:S(2)}, u32[]{:S(2)}) collective-permute-start(f32[2,48,512]{2,1,0:T(8,128)S(1)} %pad_maximum_fusion.refs_0_), channel_id=1, source_target_pairs={{0,16},{16,0},{32,48},{48,32},{64,80},{80,64},{96,112},{112,96},{1... | collective-permute-start | bytes 589832 | tf_op jit(solution)/shard_map/ppermute | solution.py:273
  41.4 18.7 %collective-permute-start.28 = (f32[2,48,512]{2,1,0:T(8,128)S(1)}, f32[2,48,512]{2,1,0:T(8,128)S(1)}, u32[]{:S(2)}, u32[]{:S(2)}) collective-permute-start(f32[2,48,512]{2,1,0:T(8,128)S(1)} %pad_maximum_fusion.refs_0_), channel_id=1, source_target_pairs={{0,64},{16,80},{32,96},{48,112},{64,128},{80,144},{96,160},{112,17... | collective-permute-start | bytes 589832 | tf_op jit(solution)/shard_map/ppermute | solution.py:271
  42.0 18.1 %collective-permute-start.27 = (f32[2,48,512]{2,1,0:T(8,128)S(1)}, f32[2,48,512]{2,1,0:T(8,128)S(1)}, u32[]{:S(2)}, u32[]{:S(2)}) collective-permute-start(f32[2,48,512]{2,1,0:T(8,128)S(1)} %pad_maximum_fusion.refs_0_), channel_id=1, source_target_pairs={{0,128},{16,144},{32,160},{48,176},{64,192},{80,208},{96,224},{112... | collective-permute-start | bytes 589832 | tf_op jit(solution)/shard_map/ppermute | solution.py:271
  44.8 15.8 %collective-permute-start.26 = (f32[2,48,512]{2,1,0:T(8,128)S(1)}, f32[2,48,512]{2,1,0:T(8,128)S(1)}, u32[]{:S(2)}, u32[]{:S(2)}) collective-permute-start(f32[2,48,512]{2,1,0:T(8,128)S(1)} %pad_maximum_fusion.refs_0_), channel_id=1, source_target_pairs={{0,192},{16,208},{32,224},{48,240},{64,0},{80,16},{96,32},{112,48}... | collective-permute-start | bytes 589832 | tf_op jit(solution)/shard_map/ppermute | solution.py:271
  45.8 32.5 %copy-start.1 = (f32[64,256]{1,0:T(8,128)S(1)}, f32[64,256]{1,0:T(8,128)}, u32[]{:S(2)}) copy-start(f32[64,256]{1,0:T(8,128)} %gate_ref.1) | copy-start | bytes 196612
  57.6 27.9 %copy-start = (f32[8,48,64]{2,1,0:T(8,128)S(1)}, f32[8,48,64]{2,1,0:T(8,128)}, u32[]{:S(2)}) copy-start(f32[8,48,64]{2,1,0:T(8,128)} %refs_13_.1) | copy-start | bytes 294916
  57.6 5.9 %collective-permute-start.17 = (f32[48,384]{1,0:T(8,128)S(1)}, f32[48,384]{1,0:T(8,128)S(1)}, u32[]{:S(2)}, u32[]{:S(2)}) collective-permute-start(f32[48,384]{1,0:T(8,128)S(1)} %get-tuple-element.19), channel_id=1, source_target_pairs={{0,8},{1,9},{2,10},{3,11},{4,12},{5,13},{6,14},{7,15},{8,0},{9,1},... | collective-permute-start | bytes 221192 | tf_op jit(solution)/shard_map/ppermute | solution.py:279
  60.1 7.6 %collective-permute-start.32 = (f32[2,48,512]{2,1,0:T(8,128)S(1)}, f32[2,48,512]{2,1,0:T(8,128)S(1)}, u32[]{:S(2)}, u32[]{:S(2)}) collective-permute-start(f32[2,48,512]{2,1,0:T(8,128)S(1)} %collective-permute-done.28.refs_3_), channel_id=1, source_target_pairs={{0,16},{16,0},{32,48},{48,32},{64,80},{80,64},{96,112},{112,96},{1... | collective-permute-start | bytes 589832 | tf_op jit(solution)/shard_map/ppermute | solution.py:273
  60.1 7.6 %collective-permute-start.31 = (f32[2,48,512]{2,1,0:T(8,128)S(1)}, f32[2,48,512]{2,1,0:T(8,128)S(1)}, u32[]{:S(2)}, u32[]{:S(2)}) collective-permute-start(f32[2,48,512]{2,1,0:T(8,128)S(1)} %collective-permute-done.27.refs_2_), channel_id=1, source_target_pairs={{0,16},{16,0},{32,48},{48,32},{64,80},{80,64},{96,112},{112,96},{1... | collective-permute-start | bytes 589832 | tf_op jit(solution)/shard_map/ppermute | solution.py:273
  60.6 16.7 %collective-permute-start.30 = (f32[2,48,512]{2,1,0:T(8,128)S(1)}, f32[2,48,512]{2,1,0:T(8,128)S(1)}, u32[]{:S(2)}, u32[]{:S(2)}) collective-permute-start(f32[2,48,512]{2,1,0:T(8,128)S(1)} %collective-permute-done.26.refs_1_), channel_id=1, source_target_pairs={{0,16},{16,0},{32,48},{48,32},{64,80},{80,64},{96,112},{112,96},{1... | collective-permute-start | bytes 589832 | tf_op jit(solution)/shard_map/ppermute | solution.py:273
  63.5 9.5 %collective-permute-start.22 = (f32[2,48,384]{2,1,0:T(8,128)S(1)}, f32[2,48,384]{2,1,0:T(8,128)S(1)}, u32[]{:S(2)}, u32[]{:S(2)}) collective-permute-start(f32[2,48,384]{2,1,0:T(8,128)S(1)} %pad_maximum_fusion.1.refs_0_), channel_id=1, source_target_pairs={{0,2},{1,3},{2,4},{3,5},{4,6},{5,7},{6,0},{7,1},{8,10},{9,11},{10,... | collective-permute-start | bytes 442376 | tf_op jit(solution)/shard_map/ppermute | solution.py:283
  65.8 8.6 %collective-permute-start.19 = (f32[2,48,384]{2,1,0:T(8,128)S(1)}, f32[2,48,384]{2,1,0:T(8,128)S(1)}, u32[]{:S(2)}, u32[]{:S(2)}) collective-permute-start(f32[2,48,384]{2,1,0:T(8,128)S(1)} %pad_maximum_fusion.1.refs_0_), channel_id=1, source_target_pairs={{0,6},{1,7},{2,0},{3,1},{4,2},{5,3},{6,4},{7,5},{8,14},{9,15},{10,... | collective-permute-start | bytes 442376 | tf_op jit(solution)/shard_map/ppermute | solution.py:283
  67.7 11.2 %collective-permute-start.24 = (f32[2,48,384]{2,1,0:T(8,128)S(1)}, f32[2,48,384]{2,1,0:T(8,128)S(1)}, u32[]{:S(2)}, u32[]{:S(2)}) collective-permute-start(f32[2,48,384]{2,1,0:T(8,128)S(1)} %pad_maximum_fusion.1.refs_0_), channel_id=1, source_target_pairs={{0,1},{1,2},{2,3},{3,4},{4,5},{5,6},{6,7},{7,0},{8,9},{9,10},{10,1... | collective-permute-start | bytes 442376 | tf_op jit(solution)/shard_map/ppermute | solution.py:283
  67.7 11.8 %collective-permute-start.18 = (f32[2,48,384]{2,1,0:T(8,128)S(1)}, f32[2,48,384]{2,1,0:T(8,128)S(1)}, u32[]{:S(2)}, u32[]{:S(2)}) collective-permute-start(f32[2,48,384]{2,1,0:T(8,128)S(1)} %pad_maximum_fusion.1.refs_0_), channel_id=1, source_target_pairs={{0,7},{1,0},{2,1},{3,2},{4,3},{5,4},{6,5},{7,6},{8,15},{9,8},{10,9... | collective-permute-start | bytes 442376 | tf_op jit(solution)/shard_map/ppermute | solution.py:283
  72.9 6.6 %collective-permute-start.23 = (f32[2,48,384]{2,1,0:T(8,128)S(1)}, f32[2,48,384]{2,1,0:T(8,128)S(1)}, u32[]{:S(2)}, u32[]{:S(2)}) collective-permute-start(f32[2,48,384]{2,1,0:T(8,128)S(1)} %collective-permute-done.22.refs_6_), channel_id=1, source_target_pairs={{0,1},{1,2},{2,3},{3,4},{4,5},{5,6},{6,7},{7,0},{8,9},{9,10},{10,1... | collective-permute-start | bytes 442376 | tf_op jit(solution)/shard_map/ppermute | solution.py:283
  74.5 9.6 %collective-permute-start.21 = (f32[2,48,384]{2,1,0:T(8,128)S(1)}, f32[2,48,384]{2,1,0:T(8,128)S(1)}, u32[]{:S(2)}, u32[]{:S(2)}) collective-permute-start(f32[2,48,384]{2,1,0:T(8,128)S(1)} %collective-permute-done.19.refs_2_), channel_id=1, source_target_pairs={{0,6},{1,7},{2,0},{3,1},{4,2},{5,3},{6,4},{7,5},{8,14},{9,15},{10,... | collective-permute-start | bytes 442376 | tf_op jit(solution)/shard_map/ppermute | solution.py:283
  77.3 8.2 %collective-permute-start.20 = (f32[2,48,384]{2,1,0:T(8,128)S(1)}, f32[2,48,384]{2,1,0:T(8,128)S(1)}, u32[]{:S(2)}, u32[]{:S(2)}) collective-permute-start(f32[2,48,384]{2,1,0:T(8,128)S(1)} %collective-permute-done.19.refs_2_), channel_id=1, source_target_pairs={{0,7},{1,0},{2,1},{3,2},{4,3},{5,4},{6,5},{7,6},{8,15},{9,8},{10,9... | collective-permute-start | bytes 442376 | tf_op jit(solution)/shard_map/ppermute | solution.py:283

commit v3 on v2

--- a/solution.py
+++ b/solution.py
@@ -123,11 +123,36 @@
     out_ref[1] = low
 
 
-def outer_rows(left, first_row, res_ref, right_two, mapped_ref, pair_ref, heads_two, seen, pair_out_ref, logits_ref, outer, high_ref, low_ref):
+def right_kernel(head_ref, *refs):
+    right_pieces = refs[:4]
+    right_two, seen, heads_two, right_ref, tall = refs[4:]
+    cols = 48
+    for piece, at in row_places(right_pieces):
+        right_ref[pl.ds(pl.multiple_of(at * 8, 8), 8), :] = piece[...]
+    tall[...] = right_ref[:, : cols * 32].T
+    for b in range(32):
+        high, low = split_two(tall[pl.ds(b, cols, stride=32), :])
+        right_two[b * cols : (b + 1) * cols, :LANES] = high
+        right_two[b * cols : (b + 1) * cols, LANES : 2 * LANES] = low
+        right_two[b * cols : (b + 1) * cols, 2 * LANES :] = high
+    extra = right_ref[:, cols * 32 :]
+    lane = lax.broadcasted_iota(jnp.int32, (LANES, LANES), 1)
+    total = jnp.sum(jnp.where(lane == 64, extra, 0.0))
+    live_cols = extra.T[:cols, :1]
+    seen[0] = jnp.broadcast_to(live_cols * total, (cols, LANES))
+    seen[1] = jnp.broadcast_to((live_cols - 1.0) * 1e9, (cols, LANES))
+    head = jnp.concatenate([head_ref[...], jnp.zeros((LANES - head_ref.shape[0], LANES), f32)], axis=0).T
+    head_high, head_low = split_two(head)
+    heads_two[0, :LANES] = head_high
+    heads_two[0, LANES:] = head_high
+    heads_two[1, :LANES] = head_low
+    heads_two[1, LANES:] = head_low
+
+
+def outer_rows(left, first_row, res_ref, right_two, mapped_ref, pair_ref, heads_two, seen, pair_out_ref, logits_ref, outer, halves_ref):
     cols = 48
     left_high, left_low = split_two(left)
-    both = right_two[...]
-    outer[...] = mxu(both, jnp.concatenate([left_high, left_high], axis=0)) + mxu(both[:, :LANES], left_low)
+    outer[...] = mxu(right_two[...], jnp.concatenate([left_high, left_high, left_low], axis=0))
     for quad in range(ROWS_PER_STEP // 4):
         for four in range(8):
             parts = [
@@ -137,10 +162,10 @@
             for g, part in enumerate(swap_groups(parts)):
                 high, low = split_two(part)
                 at = (quad * 4 + g) * cols
-                high_ref[at : at + cols, four * LANES : (four + 1) * LANES] = high
-                low_ref[at : at + cols, four * LANES : (four + 1) * LANES] = low
-    wide = mxu(high_ref[...], mapped_ref[...])
-    sums = wide[:, :LANES] + wide[:, LANES:] + mxu(low_ref[...], mapped_ref[:, :LANES])
+                halves_ref[at : at + cols, four * LANES : (four + 1) * LANES] = high
+                halves_ref[at : at + cols, 1024 + four * LANES : 1024 + (four + 1) * LANES] = low
+    wide = mxu(halves_ref[:, :1024], mapped_ref[...])
+    sums = wide[:, :LANES] + wide[:, LANES:] + mxu(halves_ref[:, 1024:], mapped_ref[:, :LANES])
     pairs = []
     for i in range(ROWS_PER_STEP):
         live = res_ref[first_row + i].astype(f32)
@@ -163,59 +188,26 @@
 
 def outer_kernel(*refs):
     res_ref = refs[0]
-    left_pieces = refs[1 : 1 + Z_CHIPS]
-    right_pieces = refs[1 + Z_CHIPS : 9 + Z_CHIPS]
-    mapped_ref, head_ref, pair_ref, pair_out_ref, logits_ref, right_two, seen, heads_two = refs[9 + Z_CHIPS : 17 + Z_CHIPS]
-    left_all, right_ref, tall, outer, high_ref, low_ref = refs[17 + Z_CHIPS :]
+    left_pieces = refs[1:3]
+    right_two, seen, heads_two, mapped_ref, pair_ref, pair_out_ref, logits_ref, left_all, outer, halves_ref = refs[3:]
     step = pl.program_id(0)
     cols = 48
 
     @pl.when(step == 0)
     def _():
-        me = lax.axis_index("col")
-        side, place = me // Z_CHIPS, lax.rem(me, Z_CHIPS)
-        for k, piece in enumerate(left_pieces):
-            at = lax.rem(place + k, Z_CHIPS)
-            left_all[pl.ds(pl.multiple_of((side * Z_CHIPS + at) * 8, 8), 8), :] = piece[0]
-            left_all[pl.ds(pl.multiple_of(((1 - side) * Z_CHIPS + at) * 8, 8), 8), :] = piece[1]
-        row = lax.axis_index("row")
-        x, y, core = row // 4, lax.rem(row // 2, 2), lax.rem(row, 2)
-        for k, piece in enumerate(right_pieces):
-            at = lax.rem(x + k % 4, 4) * 4 + (core if k < 4 else 1 - core)
-            right_ref[pl.ds(pl.multiple_of((at + y * 2) * 8, 8), 8), :] = piece[0]
-            right_ref[pl.ds(pl.multiple_of((at + (1 - y) * 2) * 8, 8), 8), :] = piece[1]
-        tall[...] = right_ref[:, : cols * 32].T
-        for b in range(32):
-            high, low = split_two(tall[pl.ds(b, cols, stride=32), :])
-            right_two[b * cols : (b + 1) * cols, :LANES] = high
-            right_two[b * cols : (b + 1) * cols, LANES:] = low
-        extra = right_ref[:, cols * 32 :]
-        lane = lax.broadcasted_iota(jnp.int32, (LANES, LANES), 1)
-        total = jnp.sum(jnp.where(lane == 64, extra, 0.0))
-        live_cols = extra.T[:cols, :1]
-        seen[0] = jnp.broadcast_to(live_cols * total, (cols, LANES))
-        seen[1] = jnp.broadcast_to((live_cols - 1.0) * 1e9, (cols, LANES))
-        head = jnp.concatenate([head_ref[...], jnp.zeros((LANES - head_ref.shape[0], LANES), f32)], axis=0).T
-        head_high, head_low = split_two(head)
-        heads_two[0, :LANES] = head_high
-        heads_two[0, LANES:] = head_high
-        heads_two[1, :LANES] = head_low
-        heads_two[1, LANES:] = head_low
+        for piece, at in col_places(left_pieces):
+            left_all[pl.ds(pl.multiple_of(at * 8, 8), 8), :] = piece[...]
 
     left = left_all[:, pl.ds(pl.multiple_of(step * (ROWS_PER_STEP * 32), LANES), ROWS_PER_STEP * 32)]
-    outer_rows(left, step * ROWS_PER_STEP, res_ref, right_two, mapped_ref, pair_ref, heads_two, seen, pair_out_ref, logits_ref, outer, high_ref, low_ref)
+    outer_rows(left, step * ROWS_PER_STEP, res_ref, right_two, mapped_ref, pair_ref, heads_two, seen, pair_out_ref, logits_ref, outer, halves_ref)
 
 
 def middle_kernel(align_normed_ref, gate_ref, *refs):
-    pieces = refs[:8]
-    turned_high_ref, turned_low_ref, open_ref, held = refs[8:]
-    residues = pieces[0].shape[1]
-    row = lax.axis_index("row")
-    x, y, core = row // 4, lax.rem(row // 2, 2), lax.rem(row, 2)
-    for k, piece in enumerate(pieces):
-        at = lax.rem(x + k % 4, 4) * 4 + (core if k < 4 else 1 - core)
-        held[pl.ds(pl.multiple_of((at + y * 2) * residues, 8), residues), :] = piece[0]
-        held[pl.ds(pl.multiple_of((at + (1 - y) * 2) * residues, 8), residues), :] = piece[1]
+    pieces = refs[:4]
+    turned_high_ref, turned_low_ref, open_ref, held = refs[4:]
+    residues = pieces[0].shape[2]
+    for piece, at in row_places(pieces):
+        held[pl.ds(pl.multiple_of(at * residues, 8), residues), :] = piece[...]
     high, low = split_two(held[...].T)
     turned_high_ref[...] = high
     turned_low_ref[...] = low
@@ -224,18 +216,12 @@
 
 
 def last_kernel(*refs):
-    pieces_in = refs[:Z_CHIPS]
-    turned_high_ref, turned_low_ref, mixed_ref, open_ref, out_weight_ref, align_ref, out_ref, held, averaged = refs[Z_CHIPS:]
+    pieces = refs[:8]
+    turned_high_ref, turned_low_ref, mixed_ref, open_ref, out_weight_ref, align_ref, out_ref, held, averaged = refs[8:]
     heads = mixed_ref.shape[0]
     rows = 48
-    me = lax.axis_index("col")
-    side, place = me // Z_CHIPS, lax.rem(me, Z_CHIPS)
-    for k, piece in enumerate(pieces_in):
-        at = lax.rem(place + k, Z_CHIPS) * rows
-        for other in range(2):
-            half = side if other == 0 else 1 - side
-            start = pl.multiple_of(half * (Z_CHIPS * rows) + at, 8)
-            held[pl.ds(start, rows), :] = piece[other]
+    for piece, at in col_places(pieces):
+        held[pl.ds(pl.multiple_of(at * rows, 8), rows), :] = piece[...]
     logits = held[...]
     top = jnp.max(logits, axis=0, keepdims=True)
     expo = jnp.exp(logits - top)
@@ -264,23 +250,76 @@
     out_ref[...] = align_ref[...] + result.reshape(out_ref.shape)
 
 
-def row_pieces(shard, axis):
-    devices = lax.axis_size(axis)
-    both = jnp.stack([shard, lax.ppermute(shard, axis, [(d, d ^ 2) for d in range(devices)])])
-    pieces = [both] + [
-        lax.ppermute(both, axis, [(d, (d + devices - 4 * k) % devices) for d in range(devices)]) for k in (1, 2, 3)
-    ]
-    return pieces + [lax.ppermute(piece, axis, [(d, d ^ 1) for d in range(devices)]) for piece in pieces]
-
-
-def ring_pieces(shard, axis, *first):
-    devices = lax.axis_size(axis)
+def way(row):
+    return 1 - 2 * (row % 2)
+
+
+def row_pieces(shard, n_row):
+    def further(piece, k):
+        return lax.ppermute(piece, "row", [(r, (r - 4 * k * way(r)) % n_row) for r in range(n_row)])
+
+    both = jnp.stack([shard, lax.ppermute(shard, "row", [(r, r ^ 2) for r in range(n_row)])])
+    even = jnp.stack([both, further(both, 2)])
+    odd = further(even, 1)
+    return [even, odd] + [lax.ppermute(piece, "row", [(r, r ^ 1) for r in range(n_row)]) for piece in (even, odd)]
+
+
+def row_places(pieces):
+    row = lax.axis_index("row")
+    x, y, core = row // 4, lax.rem(row // 2, 2), lax.rem(row, 2)
+    forward = 1 - 2 * core
+    for n, piece in enumerate(pieces):
+        for m in range(2):
+            k = n % 2 + 2 * m
+            at = lax.rem(x + 4 + forward * k, 4) * 4 + core if n < 2 else lax.rem(x + 4 - forward * k, 4) * 4 + 1 - core
+            yield piece.at[m, 0], at + y * 2
+            yield piece.at[m, 1], at + (1 - y) * 2
+
+
+def col_places(pieces):
+    me = lax.axis_index("col")
+    side, place = me // Z_CHIPS, lax.rem(me, Z_CHIPS)
+    forward = 1 - 2 * lax.rem(lax.axis_index("row"), 2)
+    if len(pieces) == 2:
+        views = [(k, piece.at[n]) for piece, places in zip(pieces, ((0, 4, 2, 6), (1, 5, 3, 7))) for n, k in enumerate(places)]
+    else:
+        views = list(enumerate(pieces))
+    for k, view in views:
+        at = lax.rem(place + Z_CHIPS + forward * k, Z_CHIPS)
+        yield view.at[0], side * Z_CHIPS + at
+        yield view.at[1], (1 - side) * Z_CHIPS + at
+
+
+def fewer_pieces(shard, n_row, n_col, *first):
     ring = Z_CHIPS
-    other = lax.ppermute(shard, axis, [(d, (d + ring) % devices) for d in range(devices)])
+
+    def further(piece, k):
+        pairs = [
+            (r * n_col + c, r * n_col + c // ring * ring + (c - k * way(r)) % ring)
+            for r in range(n_row)
+            for c in range(n_col)
+        ]
+        return lax.ppermute(piece, ("row", "col"), pairs)
+
+    other = lax.ppermute(shard, "col", [(c, (c + ring) % n_col) for c in range(n_col)])
+    both = jnp.stack([shard, other])
+    two = after(jnp.stack([both, further(both, 4)]), *first)
+    four = jnp.concatenate([two, further(two, 2)])
+    return [four, further(four, 1)]
+
+
+def ring_pieces(shard, n_row, n_col, *first):
+    ring = Z_CHIPS
+    other = lax.ppermute(shard, "col", [(c, (c + ring) % n_col) for c in range(n_col)])
     both = after(jnp.stack([shard, other]), *first)
 
     def further(piece, k):
-        return lax.ppermute(piece, axis, [(d, d // ring * ring + (d + ring - k) % ring) for d in range(devices)])
+        pairs = [
+            (r * n_col + c, r * n_col + c // ring * ring + (c - k * way(r)) % ring)
+            for r in range(n_row)
+            for c in range(n_col)
+        ]
+        return lax.ppermute(piece, ("row", "col"), pairs)
 
     pieces = {0: both}
     for k in (1, 7, 2, 6):
@@ -350,15 +389,20 @@
         ],
         in_specs=[HBM] * 3,
     )(*[in_hbm(a) for a in (w_outer, value_weight, output_weight.T)])
-    left_pieces = ring_pieces(left, "col", mapped)
-    right_pieces = row_pieces(right_here, "row")
+    left_pieces = fewer_pieces(left, n_row, n_col, mapped)
+    right_pieces = row_pieces(right_here, n_row)
+    right_two, seen, heads_two = call(
+        right_kernel,
+        (shape((cols * 32, 3 * LANES), bf16), shape((2, cols, LANES)), shape((2, 256, LANES), bf16)),
+        16,
+        scratch=[pltpu.VMEM((n_row * seqs, rows * 32 + LANES), f32), pltpu.VMEM((cols * 32, LANES), f32)],
+    )(w_logits.T, *right_pieces)
     steps = rows // ROWS_PER_STEP
     pair_rep = in_hbm(pair_rep)
     pair_block = (ROWS_PER_STEP, cols, pair_width)
     work = [
         pltpu.VMEM((cols * 32, ROWS_PER_STEP * 32), f32),
-        pltpu.VMEM((ROWS_PER_STEP * cols, 1024), bf16),
-        pltpu.VMEM((ROWS_PER_STEP * cols, 1024), bf16),
+        pltpu.VMEM((ROWS_PER_STEP * cols, 2048), bf16),
     ]
     pair_out, logits = pl.pallas_call(
         outer_kernel,
@@ -367,31 +411,26 @@
             shape(pair_rep.shape),
             shape((cols, steps * LANES)),
         ),
-        in_specs=[SMEM] + [VMEM] * 18 + [pl.BlockSpec(pair_block, lambda t: (t, 0, 0))],
+        in_specs=[SMEM] + [VMEM] * 6 + [pl.BlockSpec(pair_block, lambda t: (t, 0, 0))],
         out_specs=[
             pl.BlockSpec(pair_block, lambda t: (t, 0, 0)),
             pl.BlockSpec((cols, LANES), lambda t: (0, t)),
         ],
         scratch_shapes=[
-            pltpu.VMEM((cols * 32, 256), bf16),
-            pltpu.VMEM((2, cols, LANES), f32),
-            pltpu.VMEM((2, 256, LANES), bf16),
             pltpu.VMEM((n_col * seqs, rows * 32), f32),
-            pltpu.VMEM((n_row * seqs, rows * 32 + LANES), f32),
-            pltpu.VMEM((cols * 32, LANES), f32),
         ]
         + work,
         compiler_params=pltpu.CompilerParams(vmem_limit_bytes=32 * 1024 * 1024),
         cost_estimate=pl.CostEstimate(flops=10**10, bytes_accessed=10**7, transcendentals=0),
-    )(res_mask, *left_pieces, *right_pieces, mapped, w_logits.T, pair_rep)
-    normed_pieces = row_pieces(normed, "row")
+    )(res_mask, *left_pieces, right_two, seen, heads_two, mapped, pair_rep)
+    normed_pieces = row_pieces(normed, n_row)
     turned_high, turned_low, opened = call(
         middle_kernel,
         (shape((seqs * width, n_row * rows), bf16), shape((seqs * width, n_row * rows), bf16), shape((seqs * rows, gate_weight.shape[1]))),
         12,
         scratch=[pltpu.VMEM((n_row * rows, seqs * width), f32)],
     )(normed_flat, gate_weight, *normed_pieces)
-    pieces = ring_pieces(logits, "col")
+    pieces = ring_pieces(logits, n_row, n_col)
     alignment_out = call(
         last_kernel,
         shape(alignment.shape),

time: 89.2 us -> 87.5 us (0.981)
  starting transfers between devices: 51.3 us -> 46.4 us
  waiting for transfers between devices: 17 us -> 20.5 us
    ppermute x32 -> x22, starting transfers between devices: 42.2 us -> 37.3 us  [the longest x10 21.9 us: further(): return lax.ppermute(piece, ('row', 'col'), pairs)]
    ppermute x32 -> x22, waiting for transfers between devices: 17 us -> 20.4 us  [the longest x10 14.1 us: further(): return lax.ppermute(piece, ('row', 'col'), pairs)]
    pallas_call x1, Pallas kernels: 11.8 us -> 10.8 us  [per_device(): pl.pallas_call(outer_kernel, grid=(steps,), out_shape=(shape(pair_rep.sha...]
    pallas_call x0 -> x1, Pallas kernels: none -> 0.93 us  [per_device(): call(right_kernel, (shape((cols * 32, 3 * LANES), bf16), shape((2, cols,...]
  transfers between devices with their start and end apart: 33 -> 23, of which waited for: 9 -> 11; matrix products, arithmetic and copies ran while one was open for 0% -> 0% of each run, Pallas kernels for 16% -> 17%
where the time goes in v3:
time: 87.5 us; the launch traced here: 87.3 us
  starting transfers between devices  46.4 us (53%)
  waiting for transfers between devices  20.5 us (23%)
  Pallas kernels  19.5 us (22%)
    ppermute x10, starting transfers between devices, further(): return lax.ppermute(piece, ('row', 'col'), pairs)  21.9 us
    ppermute x10, waiting for transfers between devices, further(): return lax.ppermute(piece, ('row', 'col'), pairs)  14.1 us
    pallas_call x1, Pallas kernels, per_device(): pl.pallas_call(outer_kernel, grid=(steps,), out_shape=(shape(pair_rep.sha...  10.8 us
    ppermute x1, starting transfers between devices, per_device(): right_here = lax.ppermute(right, ('row', 'col'), turn)  9.06 us
    ppermute x4, starting transfers between devices, further(): lax.ppermute(piece, 'row', [(r, (r - 4 * k * way(r)) % n_row) for r in ra...  8.02 us
    ppermute x1, waiting for transfers between devices, ring_pieces(): lax.ppermute(shard, 'col', [(c, (c + ring) % n_col) for c in range(n_col)])  3.48 us
    pallas_call x1, Pallas kernels, per_device(): call(last_kernel, shape(alignment.shape), 24, scratch=[pltpu.VMEM((n_row...  3.35 us
    ppermute x1, starting transfers between devices, fewer_pieces(): lax.ppermute(shard, 'col', [(c, (c + ring) % n_col) for c in range(n_col)])  3.28 us
  transfers between devices with their start and end apart: 23, of which 11 were waited for; matrix products, arithmetic and copies ran while one was open for 0% of the time, Pallas kernels for 17%

profile of v3, /device:TPU:2, one launch (start us, length us, event | category | flops | bytes accessed | tf_op | source)
XLA Modules:
  0.0 87.3 jit_solution(18280099900906375731)
XLA Ops:
  0.6 1.7 %shard_map.122 = (f32[8,1536]{1,0:T(8,128)S(1)}, f32[8,1664]{1,0:T(8,128)S(1)}, f32[48,512]{1,0:T(8,128)S(1)}, f32[384,64]{1,0:T(8,128)S(1)}) custom-call(s32[8]{0:T(128)} %seq_in.1, s32[48]{0:T(128)} %refs_0_.1, f32[8,48,64]{2,1,0:T(8,128)} %refs_13_.1, f32[32,64]{1,0:T(8,128)} %bitcast.34, f32[32,64]{1,0:T(8,128)} %bitcast.35), custom_call_target="tpu_custom_call" | custom-call | tf_op jit(solution)/shard_map/pallas_call | solution.py:364
  2.4 3.3 %collective-permute-start = (f32[8,1536]{1,0:T(8,128)S(1)}, f32[8,1536]{1,0:T(8,128)S(1)}, u32[]{:S(2)}, u32[]{:S(2)}) collective-permute-start(f32[8,1536]{1,0:T(8,128)S(1)} %get-tuple-element.18), channel_id=1, source_target_pairs={{0,8},{1,9},{2,10},{3,11},{4,12},{5,13},{6,14},{7,15},{8,0},{9,1},... | collective-permute-start | bytes 147464 | tf_op jit(solution)/shard_map/ppermute | solution.py:304
  5.7 9.1 %collective-permute-start.4 = (f32[8,1664]{1,0:T(8,128)S(1)}, f32[8,1664]{1,0:T(8,128)S(1)}, u32[]{:S(2)}, u32[]{:S(2)}) collective-permute-start(f32[8,1664]{1,0:T(8,128)S(1)} %get-tuple-element.21), channel_id=1, source_target_pairs={{0,0},{1,16},{2,32},{3,48},{4,64},{5,80},{6,96},{7,112},{8,128},{9... | collective-permute-start | bytes 159752 | tf_op jit(solution)/shard_map/ppermute | solution.py:379
  14.7 0.7 collective-permute-start.18
  15.4 2.1 %shard_map.123 = (bf16[1024,256]{1,0:T(8,128)(2,1)S(1)}, bf16[8,256,256]{2,1,0:T(8,128)(2,1)S(1)}, bf16[2,256,64]{2,1,0:T(8,128)(2,1)S(1)}) custom-call(f32[1024,128]{1,0:T(8,128)} %outer_in.1, f32[64,256]{1,0:T(8,128)} %value_in.1, f32[64,256]{1,0:T(8,128)} %bitcast.30), custom_call_target="tpu_custom_call" | custom-call | tf_op jit(solution)/shard_map/pallas_call | solution.py:380
  17.5 0.0 collective-permute-done
  17.5 2.5 %collective-permute-start.1 = (f32[2,8,1536]{2,1,0:T(8,128)S(1)}, f32[2,8,1536]{2,1,0:T(8,128)S(1)}, u32[]{:S(2)}, u32[]{:S(2)}) collective-permute-start(f32[2,8,1536]{2,1,0:T(8,128)S(1)} %get-tuple-element.39), channel_id=1, source_target_pairs={{0,4},{1,5},{2,6},{3,7},{4,0},{5,1},{6,2},{7,3},{8,12},{9,13},{10,... | collective-permute-start | bytes 294920 | tf_op jit(solution)/shard_map/ppermute | solution.py:302
  20.0 0.0 collective-permute-done.4
  20.0 0.0 collective-permute-start.5
  20.0 0.0 collective-permute-done.18
  20.1 2.5 %collective-permute-start.19 = (f32[2,48,512]{2,1,0:T(8,128)S(1)}, f32[2,48,512]{2,1,0:T(8,128)S(1)}, u32[]{:S(2)}, u32[]{:S(2)}) collective-permute-start(f32[2,48,512]{2,1,0:T(8,128)S(1)} %get-tuple-element.35), channel_id=1, source_target_pairs={{0,128},{16,144},{32,160},{48,176},{64,192},{80,208},{96,224},{112... | collective-permute-start | bytes 589832 | tf_op jit(solution)/shard_map/ppermute | solution.py:259
  22.5 1.6 %collective-permute-done.5 = f32[8,1664]{1,0:T(8,128)S(1)} collective-permute-done((f32[8,1664]{1,0:T(8,128)S(1)}, f32[8,1664]{1,0:T(8,128)S(1)}, u32[]{:S(2)}, u32[]{:S(2)}) %collective-permute-start.5) | collective-permute-done | bytes 53280 | tf_op jit(solution)/shard_map/ppermute | solution.py:261
  24.2 2.3 %collective-permute-start.6 = (f32[2,8,1664]{2,1,0:T(8,128)S(1)}, f32[2,8,1664]{2,1,0:T(8,128)S(1)}, u32[]{:S(2)}, u32[]{:S(2)}) collective-permute-start(f32[2,8,1664]{2,1,0:T(8,128)S(1)} %get-tuple-element.37), channel_id=1, source_target_pairs={{0,128},{16,144},{32,160},{48,176},{64,192},{80,208},{96,224},{112... | collective-permute-start | bytes 319496 | tf_op jit(solution)/shard_map/ppermute | solution.py:259
  26.5 1.3 %collective-permute-done.1 = f32[2,8,1536]{2,1,0:T(8,128)S(1)} collective-permute-done((f32[2,8,1536]{2,1,0:T(8,128)S(1)}, f32[2,8,1536]{2,1,0:T(8,128)S(1)}, u32[]{:S(2)}, u32[]{:S(2)}) %collective-permute-start.1) | collective-permute-done | bytes 98336 | tf_op jit(solution)/shard_map/ppermute | solution.py:302
  27.8 3.1 %collective-permute-start.2 = (f32[2,2,8,1536]{3,2,1,0:T(8,128)S(1)}, f32[2,2,8,1536]{3,2,1,0:T(8,128)S(1)}, u32[]{:S(2)}, u32[]{:S(2)}) collective-permute-start(f32[2,2,8,1536]{3,2,1,0:T(8,128)S(1)} %pad_maximum_fusion.2), channel_id=1, source_target_pairs={{0,6},{1,7},{2,0},{3,1},{4,2},{5,3},{6,4},{7,5},{8,14},{9,15},{10,... | collective-permute-start | bytes 589832 | tf_op jit(solution)/shard_map/ppermute | solution.py:302
  30.9 0.0 collective-permute-done.6
  30.9 0.0 copy-start.3
  30.9 2.4 %collective-permute-start.7 = (f32[2,2,8,1664]{3,2,1,0:T(8,128)S(1)}, f32[2,2,8,1664]{3,2,1,0:T(8,128)S(1)}, u32[]{:S(2)}, u32[]{:S(2)}) collective-permute-start(f32[2,2,8,1664]{3,2,1,0:T(8,128)S(1)} %pad_maximum_fusion.1.refs_0_), channel_id=1, source_target_pairs={{0,192},{16,80},{32,224},{48,112},{64,0},{80,144},{96,32},{112,176... | collective-permute-start | bytes 638984 | tf_op jit(solution)/shard_map/ppermute | solution.py:259
  33.3 0.0 collective-permute-done.19
  33.4 0.9 %collective-permute-start.20 = (f32[2,2,48,512]{3,2,1,0:T(8,128)S(1)}, f32[2,2,48,512]{3,2,1,0:T(8,128)S(1)}, u32[]{:S(2)}, u32[]{:S(2)}) collective-permute-start(f32[2,2,48,512]{3,2,1,0:T(8,128)S(1)} %pad_maximum_fusion.refs_0_), channel_id=1, source_target_pairs={{0,192},{16,80},{32,224},{48,112},{64,0},{80,144},{96,32},{112,176... | collective-permute-start | bytes 1179656 | tf_op jit(solution)/shard_map/ppermute | solution.py:259
  34.2 2.4 %collective-permute-done.2 = f32[2,2,8,1536]{3,2,1,0:T(8,128)S(1)} collective-permute-done((f32[2,2,8,1536]{3,2,1,0:T(8,128)S(1)}, f32[2,2,8,1536]{3,2,1,0:T(8,128)S(1)}, u32[]{:S(2)}, u32[]{:S(2)}) %collective-permute-start.2) | collective-permute-done | bytes 196640 | tf_op jit(solution)/shard_map/ppermute | solution.py:302
  36.6 3.9 %collective-permute-start.3 = (f32[4,2,8,1536]{3,2,1,0:T(8,128)S(1)}, f32[4,2,8,1536]{3,2,1,0:T(8,128)S(1)}, u32[]{:S(2)}, u32[]{:S(2)}) collective-permute-start(f32[4,2,8,1536]{3,2,1,0:T(8,128)S(1)} %constant_dynamic-update-slice_fusion.refs_1_), channel_id=1, source_target_pairs={{0,7},{1,0},{2,1},{3,2},{4,3},{5,4},{6,5},{7,6},{8,15},{9,8},{10,9... | collective-permute-start | bytes 1179656 | tf_op jit(solution)/shard_map/ppermute | solution.py:302
  40.6 0.5 collective-permute-start.9
  41.1 0.0 collective-permute-start.21
  41.1 0.9 %collective-permute-done.8.refs_2_ = f32[2,2,8,1664]{3,2,1,0:T(8,128)S(1)} collective-permute-done((f32[2,2,8,1664]{3,2,1,0:T(8,128)S(1)}, f32[2,2,8,1664]{3,2,1,0:T(8,128)S(1)}, u32[]{:S(2)}, u32[]{:S(2)}) %collective-permute-start.8) | collective-permute-done | bytes 213024 | tf_op jit(solution)/shard_map/ppermute | solution.py:264
  42.0 0.3 collective-permute-done.9.refs_3_
  42.3 0.9 %shard_map.124 = (bf16[1536,384]{1,0:T(8,128)(2,1)S(1)}, f32[2,48,128]{2,1,0:T(8,128)S(1)}, bf16[2,256,128]{2,1,0:T(8,128)(2,1)S(1)}) custom-call(f32[8,128]{1,0:T(8,128)S(1)} %bitcast.24, f32[2,2,8,1664]{3,2,1,0:T(8,128)S(1)} %pad_maximum_fusion.1.refs_0_, f32[2,2,8,1664]{3,2,1,0:T(8,128)S(1)} %collective-permute-done.7.refs_1_, ...), custom_call_target="tpu_custom_call" | custom-call | tf_op jit(solution)/shard_map/pallas_call | solution.py:394
  43.3 0.5 collective-permute-start.22
  43.8 2.1 %collective-permute-done.3.refs_2_ = f32[4,2,8,1536]{3,2,1,0:T(8,128)S(1)} collective-permute-done((f32[4,2,8,1536]{3,2,1,0:T(8,128)S(1)}, f32[4,2,8,1536]{3,2,1,0:T(8,128)S(1)}, u32[]{:S(2)}, u32[]{:S(2)}) %collective-permute-start.3) | collective-permute-done | bytes 393248 | tf_op jit(solution)/shard_map/ppermute | solution.py:302
  45.9 10.8 %shard_map.125 = (f32[48,48,128]{2,1,0:T(8,128)}, f32[48,384]{1,0:T(8,128)S(1)}) custom-call(s32[48]{0:T(128)S(1)} %copy-done.3, f32[4,2,8,1536]{3,2,1,0:T(8,128)S(1)} %constant_dynamic-update-slice_fusion.refs_1_, f32[4,2,8,1536]{3,2,1,0:T(8,128)S(1)} %collective-permute-done.3.refs_2_, bf16[1536,384]{1,0:T(8,128)(2,1)S(1)} %get-tuple-element.22.refs_3_, ...), custom_call_target="tpu_custom_call" | custom-call | flops 10000000000 | bytes 10000000 | tf_op jit(solution)/shard_map/pallas_call | solution.py:407
  56.6 2.5 %collective-permute-start.10 = (f32[48,384]{1,0:T(8,128)S(1)}, f32[48,384]{1,0:T(8,128)S(1)}, u32[]{:S(2)}, u32[]{:S(2)}) collective-permute-start(f32[48,384]{1,0:T(8,128)S(1)} %get-tuple-element.25), channel_id=1, source_target_pairs={{0,8},{1,9},{2,10},{3,11},{4,12},{5,13},{6,14},{7,15},{8,0},{9,1},... | collective-permute-start | bytes 221192 | tf_op jit(solution)/shard_map/ppermute | solution.py:313
  59.1 3.5 %collective-permute-done.10 = f32[48,384]{1,0:T(8,128)S(1)} collective-permute-done((f32[48,384]{1,0:T(8,128)S(1)}, f32[48,384]{1,0:T(8,128)S(1)}, u32[]{:S(2)}, u32[]{:S(2)}) %collective-permute-start.10) | collective-permute-done | bytes 73760 | tf_op jit(solution)/shard_map/ppermute | solution.py:313
  62.6 2.0 %collective-permute-start.15 = (f32[2,48,384]{2,1,0:T(8,128)S(1)}, f32[2,48,384]{2,1,0:T(8,128)S(1)}, u32[]{:S(2)}, u32[]{:S(2)}) collective-permute-start(f32[2,48,384]{2,1,0:T(8,128)S(1)} %pad_maximum_fusion.4.refs_0_), channel_id=1, source_target_pairs={{0,2},{1,3},{2,4},{3,5},{4,6},{5,7},{6,0},{7,1},{8,10},{9,11},{10,... | collective-permute-start | bytes 442376 | tf_op jit(solution)/shard_map/ppermute | solution.py:322
  64.6 2.2 %collective-permute-start.12 = (f32[2,48,384]{2,1,0:T(8,128)S(1)}, f32[2,48,384]{2,1,0:T(8,128)S(1)}, u32[]{:S(2)}, u32[]{:S(2)}) collective-permute-start(f32[2,48,384]{2,1,0:T(8,128)S(1)} %pad_maximum_fusion.4.refs_0_), channel_id=1, source_target_pairs={{0,6},{1,7},{2,0},{3,1},{4,2},{5,3},{6,4},{7,5},{8,14},{9,15},{10,... | collective-permute-start | bytes 442376 | tf_op jit(solution)/shard_map/ppermute | solution.py:322
  66.8 1.1 %collective-permute-start.17 = (f32[2,48,384]{2,1,0:T(8,128)S(1)}, f32[2,48,384]{2,1,0:T(8,128)S(1)}, u32[]{:S(2)}, u32[]{:S(2)}) collective-permute-start(f32[2,48,384]{2,1,0:T(8,128)S(1)} %pad_maximum_fusion.4.refs_0_), channel_id=1, source_target_pairs={{0,1},{1,2},{2,3},{3,4},{4,5},{5,6},{6,7},{7,0},{8,9},{9,10},{10,1... | collective-permute-start | bytes 442376 | tf_op jit(solution)/shard_map/ppermute | solution.py:322
  67.9 2.1 %collective-permute-start.11 = (f32[2,48,384]{2,1,0:T(8,128)S(1)}, f32[2,48,384]{2,1,0:T(8,128)S(1)}, u32[]{:S(2)}, u32[]{:S(2)}) collective-permute-start(f32[2,48,384]{2,1,0:T(8,128)S(1)} %pad_maximum_fusion.4.refs_0_), channel_id=1, source_target_pairs={{0,7},{1,0},{2,1},{3,2},{4,3},{5,4},{6,5},{7,6},{8,15},{9,8},{10,9... | collective-permute-start | bytes 442376 | tf_op jit(solution)/shard_map/ppermute | solution.py:322
  70.0 2.7 %collective-permute-done.15.refs_6_ = f32[2,48,384]{2,1,0:T(8,128)S(1)} collective-permute-done((f32[2,48,384]{2,1,0:T(8,128)S(1)}, f32[2,48,384]{2,1,0:T(8,128)S(1)}, u32[]{:S(2)}, u32[]{:S(2)}) %collective-permute-start.15) | collective-permute-done | bytes 147488 | tf_op jit(solution)/shard_map/ppermute | solution.py:322
  72.7 2.0 %collective-permute-start.16 = (f32[2,48,384]{2,1,0:T(8,128)S(1)}, f32[2,48,384]{2,1,0:T(8,128)S(1)}, u32[]{:S(2)}, u32[]{:S(2)}) collective-permute-start(f32[2,48,384]{2,1,0:T(8,128)S(1)} %collective-permute-done.15.refs_6_), channel_id=1, source_target_pairs={{0,1},{1,2},{2,3},{3,4},{4,5},{5,6},{6,7},{7,0},{8,9},{9,10},{10,1... | collective-permute-start | bytes 442376 | tf_op jit(solution)/shard_map/ppermute | solution.py:322
  74.8 1.0 %collective-permute-start.14 = (f32[2,48,384]{2,1,0:T(8,128)S(1)}, f32[2,48,384]{2,1,0:T(8,128)S(1)}, u32[]{:S(2)}, u32[]{:S(2)}) collective-permute-start(f32[2,48,384]{2,1,0:T(8,128)S(1)} %collective-permute-done.12.refs_2_), channel_id=1, source_target_pairs={{0,6},{1,7},{2,0},{3,1},{4,2},{5,3},{6,4},{7,5},{8,14},{9,15},{10,... | collective-permute-start | bytes 442376 | tf_op jit(solution)/shard_map/ppermute | solution.py:322
  75.7 0.0 collective-permute-done.22.refs_3_
  75.7 1.9 %collective-permute-start.13 = (f32[2,48,384]{2,1,0:T(8,128)S(1)}, f32[2,48,384]{2,1,0:T(8,128)S(1)}, u32[]{:S(2)}, u32[]{:S(2)}) collective-permute-start(f32[2,48,384]{2,1,0:T(8,128)S(1)} %collective-permute-done.12.refs_2_), channel_id=1, source_target_pairs={{0,7},{1,0},{2,1},{3,2},{4,3},{5,4},{6,5},{7,6},{8,15},{9,8},{10,9... | collective-permute-start | bytes 442376 | tf_op jit(solution)/shard_map/ppermute | solution.py:322
  77.7 0.6 shard_map.126
  78.3 0.0 collective-permute-done.17.refs_7_
  78.3 0.0 collective-permute-done.11.refs_1_
  78.3 2.7 %collective-permute-done.16.refs_5_ = f32[2,48,384]{2,1,0:T(8,128)S(1)} collective-permute-done((f32[2,48,384]{2,1,0:T(8,128)S(1)}, f32[2,48,384]{2,1,0:T(8,128)S(1)}, u32[]{:S(2)}, u32[]{:S(2)}) %collective-permute-start.16) | collective-permute-done | bytes 147488 | tf_op jit(solution)/shard_map/ppermute | solution.py:322
  81.0 1.4 %collective-permute-done.14.refs_4_ = f32[2,48,384]{2,1,0:T(8,128)S(1)} collective-permute-done((f32[2,48,384]{2,1,0:T(8,128)S(1)}, f32[2,48,384]{2,1,0:T(8,128)S(1)}, u32[]{:S(2)}, u32[]{:S(2)}) %collective-permute-start.14) | collective-permute-done | bytes 147488 | tf_op jit(solution)/shard_map/ppermute | solution.py:322
  82.5 1.5 %collective-permute-done.13.refs_3_ = f32[2,48,384]{2,1,0:T(8,128)S(1)} collective-permute-done((f32[2,48,384]{2,1,0:T(8,128)S(1)}, f32[2,48,384]{2,1,0:T(8,128)S(1)}, u32[]{:S(2)}, u32[]{:S(2)}) %collective-permute-start.13) | collective-permute-done | bytes 147488 | tf_op jit(solution)/shard_map/ppermute | solution.py:322
  84.0 3.4 %shard_map.127 = f32[8,48,64]{2,1,0:T(8,128)} custom-call(f32[2,48,384]{2,1,0:T(8,128)S(1)} %pad_maximum_fusion.4.refs_0_, f32[2,48,384]{2,1,0:T(8,128)S(1)} %collective-permute-done.11.refs_1_, f32[2,48,384]{2,1,0:T(8,128)S(1)} %collective-permute-done.12.refs_2_, f32[2,48,384]{2,1,0:T(8,128)S(1)} %collective-permute-done.13.refs_3_, ...), custom_call_target="tpu_custom_call" | custom-call | tf_op jit(solution)/shard_map/pallas_call | solution.py:434
  (21 shorter events, 0.2 us)
Async XLA Ops:
  2.4 15.1 %collective-permute-start = (f32[8,1536]{1,0:T(8,128)S(1)}, f32[8,1536]{1,0:T(8,128)S(1)}, u32[]{:S(2)}, u32[]{:S(2)}) collective-permute-start(f32[8,1536]{1,0:T(8,128)S(1)} %get-tuple-element.18), channel_id=1, source_target_pairs={{0,8},{1,9},{2,10},{3,11},{4,12},{5,13},{6,14},{7,15},{8,0},{9,1},... | collective-permute-start | bytes 147464 | tf_op jit(solution)/shard_map/ppermute | solution.py:304
  5.7 14.4 %collective-permute-start.4 = (f32[8,1664]{1,0:T(8,128)S(1)}, f32[8,1664]{1,0:T(8,128)S(1)}, u32[]{:S(2)}, u32[]{:S(2)}) collective-permute-start(f32[8,1664]{1,0:T(8,128)S(1)} %get-tuple-element.21), channel_id=1, source_target_pairs={{0,0},{1,16},{2,32},{3,48},{4,64},{5,80},{6,96},{7,112},{8,128},{9... | collective-permute-start | bytes 159752 | tf_op jit(solution)/shard_map/ppermute | solution.py:379
  14.7 5.3 %collective-permute-start.18 = (f32[48,512]{1,0:T(8,128)S(1)}, f32[48,512]{1,0:T(8,128)S(1)}, u32[]{:S(2)}, u32[]{:S(2)}) collective-permute-start(f32[48,512]{1,0:T(8,128)S(1)} %get-tuple-element.27), channel_id=1, source_target_pairs={{0,32},{16,48},{32,0},{48,16},{64,96},{80,112},{96,64},{112,80},{1... | collective-permute-start | bytes 294920 | tf_op jit(solution)/shard_map/ppermute | solution.py:261
  17.5 10.2 %collective-permute-start.1 = (f32[2,8,1536]{2,1,0:T(8,128)S(1)}, f32[2,8,1536]{2,1,0:T(8,128)S(1)}, u32[]{:S(2)}, u32[]{:S(2)}) collective-permute-start(f32[2,8,1536]{2,1,0:T(8,128)S(1)} %get-tuple-element.39), channel_id=1, source_target_pairs={{0,4},{1,5},{2,6},{3,7},{4,0},{5,1},{6,2},{7,3},{8,12},{9,13},{10,... | collective-permute-start | bytes 294920 | tf_op jit(solution)/shard_map/ppermute | solution.py:302
  20.0 4.1 %collective-permute-start.5 = (f32[8,1664]{1,0:T(8,128)S(1)}, f32[8,1664]{1,0:T(8,128)S(1)}, u32[]{:S(2)}, u32[]{:S(2)}) collective-permute-start(f32[8,1664]{1,0:T(8,128)S(1)} %collective-permute-done.4), channel_id=1, source_target_pairs={{0,32},{16,48},{32,0},{48,16},{64,96},{80,112},{96,64},{112,80},{1... | collective-permute-start | bytes 159752 | tf_op jit(solution)/shard_map/ppermute | solution.py:261
  20.1 13.3 %collective-permute-start.19 = (f32[2,48,512]{2,1,0:T(8,128)S(1)}, f32[2,48,512]{2,1,0:T(8,128)S(1)}, u32[]{:S(2)}, u32[]{:S(2)}) collective-permute-start(f32[2,48,512]{2,1,0:T(8,128)S(1)} %get-tuple-element.35), channel_id=1, source_target_pairs={{0,128},{16,144},{32,160},{48,176},{64,192},{80,208},{96,224},{112... | collective-permute-start | bytes 589832 | tf_op jit(solution)/shard_map/ppermute | solution.py:259
  24.2 6.7 %collective-permute-start.6 = (f32[2,8,1664]{2,1,0:T(8,128)S(1)}, f32[2,8,1664]{2,1,0:T(8,128)S(1)}, u32[]{:S(2)}, u32[]{:S(2)}) collective-permute-start(f32[2,8,1664]{2,1,0:T(8,128)S(1)} %get-tuple-element.37), channel_id=1, source_target_pairs={{0,128},{16,144},{32,160},{48,176},{64,192},{80,208},{96,224},{112... | collective-permute-start | bytes 319496 | tf_op jit(solution)/shard_map/ppermute | solution.py:259
  27.7 14.6 %copy-start.2 = (f32[128,8]{0,1:T(8,128)S(1)}, f32[128,8]{0,1:T(8,128)}, u32[]{:S(2)}) copy-start(f32[128,8]{0,1:T(8,128)} %param.18) | copy-start | bytes 12292
  27.8 8.9 %collective-permute-start.2 = (f32[2,2,8,1536]{3,2,1,0:T(8,128)S(1)}, f32[2,2,8,1536]{3,2,1,0:T(8,128)S(1)}, u32[]{:S(2)}, u32[]{:S(2)}) collective-permute-start(f32[2,2,8,1536]{3,2,1,0:T(8,128)S(1)} %pad_maximum_fusion.2), channel_id=1, source_target_pairs={{0,6},{1,7},{2,0},{3,1},{4,2},{5,3},{6,4},{7,5},{8,14},{9,15},{10,... | collective-permute-start | bytes 589832 | tf_op jit(solution)/shard_map/ppermute | solution.py:302
  30.9 15.0 %copy-start.3 = (s32[48]{0:T(128)S(1)}, s32[48]{0:T(128)}, u32[]{:S(2)}) copy-start(s32[48]{0:T(128)} %refs_0_.1) | copy-start | bytes 580
  30.9 9.6 %collective-permute-start.7 = (f32[2,2,8,1664]{3,2,1,0:T(8,128)S(1)}, f32[2,2,8,1664]{3,2,1,0:T(8,128)S(1)}, u32[]{:S(2)}, u32[]{:S(2)}) collective-permute-start(f32[2,2,8,1664]{3,2,1,0:T(8,128)S(1)} %pad_maximum_fusion.1.refs_0_), channel_id=1, source_target_pairs={{0,192},{16,80},{32,224},{48,112},{64,0},{80,144},{96,32},{112,176... | collective-permute-start | bytes 638984 | tf_op jit(solution)/shard_map/ppermute | solution.py:259
  33.4 9.9 %collective-permute-start.20 = (f32[2,2,48,512]{3,2,1,0:T(8,128)S(1)}, f32[2,2,48,512]{3,2,1,0:T(8,128)S(1)}, u32[]{:S(2)}, u32[]{:S(2)}) collective-permute-start(f32[2,2,48,512]{3,2,1,0:T(8,128)S(1)} %pad_maximum_fusion.refs_0_), channel_id=1, source_target_pairs={{0,192},{16,80},{32,224},{48,112},{64,0},{80,144},{96,32},{112,176... | collective-permute-start | bytes 1179656 | tf_op jit(solution)/shard_map/ppermute | solution.py:259
  36.6 9.2 %collective-permute-start.3 = (f32[4,2,8,1536]{3,2,1,0:T(8,128)S(1)}, f32[4,2,8,1536]{3,2,1,0:T(8,128)S(1)}, u32[]{:S(2)}, u32[]{:S(2)}) collective-permute-start(f32[4,2,8,1536]{3,2,1,0:T(8,128)S(1)} %constant_dynamic-update-slice_fusion.refs_1_), channel_id=1, source_target_pairs={{0,7},{1,0},{2,1},{3,2},{4,3},{5,4},{6,5},{7,6},{8,15},{9,8},{10,9... | collective-permute-start | bytes 1179656 | tf_op jit(solution)/shard_map/ppermute | solution.py:302
  40.6 1.5 %collective-permute-start.8 = (f32[2,2,8,1664]{3,2,1,0:T(8,128)S(1)}, f32[2,2,8,1664]{3,2,1,0:T(8,128)S(1)}, u32[]{:S(2)}, u32[]{:S(2)}) collective-permute-start(f32[2,2,8,1664]{3,2,1,0:T(8,128)S(1)} %pad_maximum_fusion.1.refs_0_), channel_id=1, source_target_pairs={{0,16},{16,0},{32,48},{48,32},{64,80},{80,64},{96,112},{112,96},{1... | collective-permute-start | bytes 638984 | tf_op jit(solution)/shard_map/ppermute | solution.py:264
  40.6 1.8 %collective-permute-start.9 = (f32[2,2,8,1664]{3,2,1,0:T(8,128)S(1)}, f32[2,2,8,1664]{3,2,1,0:T(8,128)S(1)}, u32[]{:S(2)}, u32[]{:S(2)}) collective-permute-start(f32[2,2,8,1664]{3,2,1,0:T(8,128)S(1)} %collective-permute-done.7.refs_1_), channel_id=1, source_target_pairs={{0,16},{16,0},{32,48},{48,32},{64,80},{80,64},{96,112},{112,96},{1... | collective-permute-start | bytes 638984 | tf_op jit(solution)/shard_map/ppermute | solution.py:264
  41.1 26.8 %collective-permute-start.21 = (f32[2,2,48,512]{3,2,1,0:T(8,128)S(1)}, f32[2,2,48,512]{3,2,1,0:T(8,128)S(1)}, u32[]{:S(2)}, u32[]{:S(2)}) collective-permute-start(f32[2,2,48,512]{3,2,1,0:T(8,128)S(1)} %pad_maximum_fusion.refs_0_), channel_id=1, source_target_pairs={{0,16},{16,0},{32,48},{48,32},{64,80},{80,64},{96,112},{112,96},{1... | collective-permute-start | bytes 1179656 | tf_op jit(solution)/shard_map/ppermute | solution.py:264
  43.3 32.5 %collective-permute-start.22 = (f32[2,2,48,512]{3,2,1,0:T(8,128)S(1)}, f32[2,2,48,512]{3,2,1,0:T(8,128)S(1)}, u32[]{:S(2)}, u32[]{:S(2)}) collective-permute-start(f32[2,2,48,512]{3,2,1,0:T(8,128)S(1)} %collective-permute-done.20.refs_1_), channel_id=1, source_target_pairs={{0,16},{16,0},{32,48},{48,32},{64,80},{80,64},{96,112},{112,96},{1... | collective-permute-start | bytes 1179656 | tf_op jit(solution)/shard_map/ppermute | solution.py:264
  45.9 31.8 %copy-start.1 = (f32[64,256]{1,0:T(8,128)S(1)}, f32[64,256]{1,0:T(8,128)}, u32[]{:S(2)}) copy-start(f32[64,256]{1,0:T(8,128)} %gate_ref.1) | copy-start | bytes 196612
  56.6 27.3 %copy-start = (f32[8,48,64]{2,1,0:T(8,128)S(1)}, f32[8,48,64]{2,1,0:T(8,128)}, u32[]{:S(2)}) copy-start(f32[8,48,64]{2,1,0:T(8,128)} %refs_13_.1) | copy-start | bytes 294916
  56.6 5.9 %collective-permute-start.10 = (f32[48,384]{1,0:T(8,128)S(1)}, f32[48,384]{1,0:T(8,128)S(1)}, u32[]{:S(2)}, u32[]{:S(2)}) collective-permute-start(f32[48,384]{1,0:T(8,128)S(1)} %get-tuple-element.25), channel_id=1, source_target_pairs={{0,8},{1,9},{2,10},{3,11},{4,12},{5,13},{6,14},{7,15},{8,0},{9,1},... | collective-permute-start | bytes 221192 | tf_op jit(solution)/shard_map/ppermute | solution.py:313
  62.6 10.2 %collective-permute-start.15 = (f32[2,48,384]{2,1,0:T(8,128)S(1)}, f32[2,48,384]{2,1,0:T(8,128)S(1)}, u32[]{:S(2)}, u32[]{:S(2)}) collective-permute-start(f32[2,48,384]{2,1,0:T(8,128)S(1)} %pad_maximum_fusion.4.refs_0_), channel_id=1, source_target_pairs={{0,2},{1,3},{2,4},{3,5},{4,6},{5,7},{6,0},{7,1},{8,10},{9,11},{10,... | collective-permute-start | bytes 442376 | tf_op jit(solution)/shard_map/ppermute | solution.py:322
  64.6 10.1 %collective-permute-start.12 = (f32[2,48,384]{2,1,0:T(8,128)S(1)}, f32[2,48,384]{2,1,0:T(8,128)S(1)}, u32[]{:S(2)}, u32[]{:S(2)}) collective-permute-start(f32[2,48,384]{2,1,0:T(8,128)S(1)} %pad_maximum_fusion.4.refs_0_), channel_id=1, source_target_pairs={{0,6},{1,7},{2,0},{3,1},{4,2},{5,3},{6,4},{7,5},{8,14},{9,15},{10,... | collective-permute-start | bytes 442376 | tf_op jit(solution)/shard_map/ppermute | solution.py:322
  66.8 11.5 %collective-permute-start.17 = (f32[2,48,384]{2,1,0:T(8,128)S(1)}, f32[2,48,384]{2,1,0:T(8,128)S(1)}, u32[]{:S(2)}, u32[]{:S(2)}) collective-permute-start(f32[2,48,384]{2,1,0:T(8,128)S(1)} %pad_maximum_fusion.4.refs_0_), channel_id=1, source_target_pairs={{0,1},{1,2},{2,3},{3,4},{4,5},{5,6},{6,7},{7,0},{8,9},{9,10},{10,1... | collective-permute-start | bytes 442376 | tf_op jit(solution)/shard_map/ppermute | solution.py:322
  67.9 10.4 %collective-permute-start.11 = (f32[2,48,384]{2,1,0:T(8,128)S(1)}, f32[2,48,384]{2,1,0:T(8,128)S(1)}, u32[]{:S(2)}, u32[]{:S(2)}) collective-permute-start(f32[2,48,384]{2,1,0:T(8,128)S(1)} %pad_maximum_fusion.4.refs_0_), channel_id=1, source_target_pairs={{0,7},{1,0},{2,1},{3,2},{4,3},{5,4},{6,5},{7,6},{8,15},{9,8},{10,9... | collective-permute-start | bytes 442376 | tf_op jit(solution)/shard_map/ppermute | solution.py:322
  72.7 8.3 %collective-permute-start.16 = (f32[2,48,384]{2,1,0:T(8,128)S(1)}, f32[2,48,384]{2,1,0:T(8,128)S(1)}, u32[]{:S(2)}, u32[]{:S(2)}) collective-permute-start(f32[2,48,384]{2,1,0:T(8,128)S(1)} %collective-permute-done.15.refs_6_), channel_id=1, source_target_pairs={{0,1},{1,2},{2,3},{3,4},{4,5},{5,6},{6,7},{7,0},{8,9},{9,10},{10,1... | collective-permute-start | bytes 442376 | tf_op jit(solution)/shard_map/ppermute | solution.py:322
  74.8 7.7 %collective-permute-start.14 = (f32[2,48,384]{2,1,0:T(8,128)S(1)}, f32[2,48,384]{2,1,0:T(8,128)S(1)}, u32[]{:S(2)}, u32[]{:S(2)}) collective-permute-start(f32[2,48,384]{2,1,0:T(8,128)S(1)} %collective-permute-done.12.refs_2_), channel_id=1, source_target_pairs={{0,6},{1,7},{2,0},{3,1},{4,2},{5,3},{6,4},{7,5},{8,14},{9,15},{10,... | collective-permute-start | bytes 442376 | tf_op jit(solution)/shard_map/ppermute | solution.py:322
  75.7 8.2 %collective-permute-start.13 = (f32[2,48,384]{2,1,0:T(8,128)S(1)}, f32[2,48,384]{2,1,0:T(8,128)S(1)}, u32[]{:S(2)}, u32[]{:S(2)}) collective-permute-start(f32[2,48,384]{2,1,0:T(8,128)S(1)} %collective-permute-done.12.refs_2_), channel_id=1, source_target_pairs={{0,7},{1,0},{2,1},{3,2},{4,3},{5,4},{6,5},{7,6},{8,15},{9,8},{10,9... | collective-permute-start | bytes 442376 | tf_op jit(solution)/shard_map/ppermute | solution.py:322

commit v4 on v3

--- a/solution.py
+++ b/solution.py
@@ -254,11 +254,11 @@
     return 1 - 2 * (row % 2)
 
 
-def row_pieces(shard, n_row):
+def row_pieces(shard, n_row, *first):
     def further(piece, k):
         return lax.ppermute(piece, "row", [(r, (r - 4 * k * way(r)) % n_row) for r in range(n_row)])
 
-    both = jnp.stack([shard, lax.ppermute(shard, "row", [(r, r ^ 2) for r in range(n_row)])])
+    both = after(jnp.stack([shard, lax.ppermute(shard, "row", [(r, r ^ 2) for r in range(n_row)])]), *first)
     even = jnp.stack([both, further(both, 2)])
     odd = further(even, 1)
     return [even, odd] + [lax.ppermute(piece, "row", [(r, r ^ 1) for r in range(n_row)]) for piece in (even, odd)]
@@ -389,8 +389,8 @@
         ],
         in_specs=[HBM] * 3,
     )(*[in_hbm(a) for a in (w_outer, value_weight, output_weight.T)])
-    left_pieces = fewer_pieces(left, n_row, n_col, mapped)
-    right_pieces = row_pieces(right_here, n_row)
+    right_pieces = row_pieces(right_here, n_row, mapped)
+    left_pieces = fewer_pieces(left, n_row, n_col)
     right_two, seen, heads_two = call(
         right_kernel,
         (shape((cols * 32, 3 * LANES), bf16), shape((2, cols, LANES)), shape((2, 256, LANES), bf16)),

time: 87.5 us -> 87.5 us (level)
  no operation moved by 1% of the time
where the time goes in v4:
time: 87.5 us; the launch traced here: 87.3 us
  starting transfers between devices  46.4 us (53%)
  waiting for transfers between devices  20.4 us (23%)
  Pallas kernels  19.5 us (22%)
    ppermute x10, starting transfers between devices, further(): return lax.ppermute(piece, ('row', 'col'), pairs)  21.9 us
    ppermute x10, waiting for transfers between devices, further(): return lax.ppermute(piece, ('row', 'col'), pairs)  14 us
    pallas_call x1, Pallas kernels, per_device(): pl.pallas_call(outer_kernel, grid=(steps,), out_shape=(shape(pair_rep.sha...  10.8 us
    ppermute x1, starting transfers between devices, per_device(): right_here = lax.ppermute(right, ('row', 'col'), turn)  9.06 us
    ppermute x4, starting transfers between devices, further(): lax.ppermute(piece, 'row', [(r, (r - 4 * k * way(r)) % n_row) for r in ra...  8.05 us
    ppermute x1, waiting for transfers between devices, ring_pieces(): lax.ppermute(shard, 'col', [(c, (c + ring) % n_col) for c in range(n_col)])  3.49 us
    pallas_call x1, Pallas kernels, per_device(): call(last_kernel, shape(alignment.shape), 24, scratch=[pltpu.VMEM((n_row...  3.35 us
    ppermute x1, starting transfers between devices, fewer_pieces(): lax.ppermute(shard, 'col', [(c, (c + ring) % n_col) for c in range(n_col)])  3.28 us
  transfers between devices with their start and end apart: 23, of which 11 were waited for; matrix products, arithmetic and copies ran while one was open for 0% of the time, Pallas kernels for 17%

profile of v4, /device:TPU:2, one launch (start us, length us, event | category | flops | bytes accessed | tf_op | source)
XLA Modules:
  0.0 87.3 jit_solution(3926029599487015149)
XLA Ops:
  0.6 1.7 %shard_map.122 = (f32[8,1536]{1,0:T(8,128)S(1)}, f32[8,1664]{1,0:T(8,128)S(1)}, f32[48,512]{1,0:T(8,128)S(1)}, f32[384,64]{1,0:T(8,128)S(1)}) custom-call(s32[8]{0:T(128)} %seq_in.1, s32[48]{0:T(128)} %refs_0_.1, f32[8,48,64]{2,1,0:T(8,128)} %refs_13_.1, f32[32,64]{1,0:T(8,128)} %bitcast.34, f32[32,64]{1,0:T(8,128)} %bitcast.35), custom_call_target="tpu_custom_call" | custom-call | tf_op jit(solution)/shard_map/pallas_call | solution.py:364
  2.4 3.3 %collective-permute-start = (f32[8,1536]{1,0:T(8,128)S(1)}, f32[8,1536]{1,0:T(8,128)S(1)}, u32[]{:S(2)}, u32[]{:S(2)}) collective-permute-start(f32[8,1536]{1,0:T(8,128)S(1)} %get-tuple-element.18), channel_id=1, source_target_pairs={{0,8},{1,9},{2,10},{3,11},{4,12},{5,13},{6,14},{7,15},{8,0},{9,1},... | collective-permute-start | bytes 147464 | tf_op jit(solution)/shard_map/ppermute | solution.py:304
  5.7 9.1 %collective-permute-start.4 = (f32[8,1664]{1,0:T(8,128)S(1)}, f32[8,1664]{1,0:T(8,128)S(1)}, u32[]{:S(2)}, u32[]{:S(2)}) collective-permute-start(f32[8,1664]{1,0:T(8,128)S(1)} %get-tuple-element.19), channel_id=1, source_target_pairs={{0,0},{1,16},{2,32},{3,48},{4,64},{5,80},{6,96},{7,112},{8,128},{9... | collective-permute-start | bytes 159752 | tf_op jit(solution)/shard_map/ppermute | solution.py:379
  14.7 0.7 collective-permute-start.18
  15.4 2.1 %shard_map.123 = (bf16[1024,256]{1,0:T(8,128)(2,1)S(1)}, bf16[8,256,256]{2,1,0:T(8,128)(2,1)S(1)}, bf16[2,256,64]{2,1,0:T(8,128)(2,1)S(1)}) custom-call(f32[1024,128]{1,0:T(8,128)} %outer_in.1, f32[64,256]{1,0:T(8,128)} %value_in.1, f32[64,256]{1,0:T(8,128)} %bitcast.30), custom_call_target="tpu_custom_call" | custom-call | tf_op jit(solution)/shard_map/pallas_call | solution.py:380
  17.5 0.0 collective-permute-done
  17.5 2.5 %collective-permute-start.1 = (f32[2,8,1536]{2,1,0:T(8,128)S(1)}, f32[2,8,1536]{2,1,0:T(8,128)S(1)}, u32[]{:S(2)}, u32[]{:S(2)}) collective-permute-start(f32[2,8,1536]{2,1,0:T(8,128)S(1)} %get-tuple-element.35), channel_id=1, source_target_pairs={{0,4},{1,5},{2,6},{3,7},{4,0},{5,1},{6,2},{7,3},{8,12},{9,13},{10,... | collective-permute-start | bytes 294920 | tf_op jit(solution)/shard_map/ppermute | solution.py:302
  20.0 0.0 collective-permute-done.4
  20.0 0.0 collective-permute-start.5
  20.0 0.0 collective-permute-done.18
  20.1 2.5 %collective-permute-start.19 = (f32[2,48,512]{2,1,0:T(8,128)S(1)}, f32[2,48,512]{2,1,0:T(8,128)S(1)}, u32[]{:S(2)}, u32[]{:S(2)}) collective-permute-start(f32[2,48,512]{2,1,0:T(8,128)S(1)} %pad_maximum_fusion.4), channel_id=1, source_target_pairs={{0,128},{16,144},{32,160},{48,176},{64,192},{80,208},{96,224},{112... | collective-permute-start | bytes 589832 | tf_op jit(solution)/shard_map/ppermute | solution.py:259
  22.5 1.6 %collective-permute-done.5 = f32[8,1664]{1,0:T(8,128)S(1)} collective-permute-done((f32[8,1664]{1,0:T(8,128)S(1)}, f32[8,1664]{1,0:T(8,128)S(1)}, u32[]{:S(2)}, u32[]{:S(2)}) %collective-permute-start.5) | collective-permute-done | bytes 53280 | tf_op jit(solution)/shard_map/ppermute | solution.py:261
  24.2 2.3 %collective-permute-start.6 = (f32[2,8,1664]{2,1,0:T(8,128)S(1)}, f32[2,8,1664]{2,1,0:T(8,128)S(1)}, u32[]{:S(2)}, u32[]{:S(2)}) collective-permute-start(f32[2,8,1664]{2,1,0:T(8,128)S(1)} %pad_maximum_fusion.6), channel_id=1, source_target_pairs={{0,128},{16,144},{32,160},{48,176},{64,192},{80,208},{96,224},{112... | collective-permute-start | bytes 319496 | tf_op jit(solution)/shard_map/ppermute | solution.py:259
  26.5 1.3 %collective-permute-done.1 = f32[2,8,1536]{2,1,0:T(8,128)S(1)} collective-permute-done((f32[2,8,1536]{2,1,0:T(8,128)S(1)}, f32[2,8,1536]{2,1,0:T(8,128)S(1)}, u32[]{:S(2)}, u32[]{:S(2)}) %collective-permute-start.1) | collective-permute-done | bytes 98336 | tf_op jit(solution)/shard_map/ppermute | solution.py:302
  27.8 3.1 %collective-permute-start.2 = (f32[2,2,8,1536]{3,2,1,0:T(8,128)S(1)}, f32[2,2,8,1536]{3,2,1,0:T(8,128)S(1)}, u32[]{:S(2)}, u32[]{:S(2)}) collective-permute-start(f32[2,2,8,1536]{3,2,1,0:T(8,128)S(1)} %pad_maximum_fusion.3), channel_id=1, source_target_pairs={{0,6},{1,7},{2,0},{3,1},{4,2},{5,3},{6,4},{7,5},{8,14},{9,15},{10,... | collective-permute-start | bytes 589832 | tf_op jit(solution)/shard_map/ppermute | solution.py:302
  30.9 0.0 collective-permute-done.6
  30.9 2.4 %collective-permute-start.7 = (f32[2,2,8,1664]{3,2,1,0:T(8,128)S(1)}, f32[2,2,8,1664]{3,2,1,0:T(8,128)S(1)}, u32[]{:S(2)}, u32[]{:S(2)}) collective-permute-start(f32[2,2,8,1664]{3,2,1,0:T(8,128)S(1)} %pad_maximum_fusion.2.refs_0_), channel_id=1, source_target_pairs={{0,192},{16,80},{32,224},{48,112},{64,0},{80,144},{96,32},{112,176... | collective-permute-start | bytes 638984 | tf_op jit(solution)/shard_map/ppermute | solution.py:259
  33.3 0.0 collective-permute-done.19
  33.3 0.9 %collective-permute-start.20 = (f32[2,2,48,512]{3,2,1,0:T(8,128)S(1)}, f32[2,2,48,512]{3,2,1,0:T(8,128)S(1)}, u32[]{:S(2)}, u32[]{:S(2)}) collective-permute-start(f32[2,2,48,512]{3,2,1,0:T(8,128)S(1)} %pad_maximum_fusion.1.refs_0_), channel_id=1, source_target_pairs={{0,192},{16,80},{32,224},{48,112},{64,0},{80,144},{96,32},{112,176... | collective-permute-start | bytes 1179656 | tf_op jit(solution)/shard_map/ppermute | solution.py:259
  34.2 2.4 %collective-permute-done.2 = f32[2,2,8,1536]{3,2,1,0:T(8,128)S(1)} collective-permute-done((f32[2,2,8,1536]{3,2,1,0:T(8,128)S(1)}, f32[2,2,8,1536]{3,2,1,0:T(8,128)S(1)}, u32[]{:S(2)}, u32[]{:S(2)}) %collective-permute-start.2) | collective-permute-done | bytes 196640 | tf_op jit(solution)/shard_map/ppermute | solution.py:302
  36.6 3.9 %collective-permute-start.3 = (f32[4,2,8,1536]{3,2,1,0:T(8,128)S(1)}, f32[4,2,8,1536]{3,2,1,0:T(8,128)S(1)}, u32[]{:S(2)}, u32[]{:S(2)}) collective-permute-start(f32[4,2,8,1536]{3,2,1,0:T(8,128)S(1)} %pad_maximum_fusion.refs_1_), channel_id=1, source_target_pairs={{0,7},{1,0},{2,1},{3,2},{4,3},{5,4},{6,5},{7,6},{8,15},{9,8},{10,9... | collective-permute-start | bytes 1179656 | tf_op jit(solution)/shard_map/ppermute | solution.py:302
  40.6 0.0 collective-permute-done.7.refs_1_
  40.6 0.5 collective-permute-start.9
  41.1 0.0 collective-permute-start.21
  41.1 0.9 %collective-permute-done.8.refs_2_ = f32[2,2,8,1664]{3,2,1,0:T(8,128)S(1)} collective-permute-done((f32[2,2,8,1664]{3,2,1,0:T(8,128)S(1)}, f32[2,2,8,1664]{3,2,1,0:T(8,128)S(1)}, u32[]{:S(2)}, u32[]{:S(2)}) %collective-permute-start.8) | collective-permute-done | bytes 213024 | tf_op jit(solution)/shard_map/ppermute | solution.py:264
  42.0 0.3 collective-permute-done.9.refs_3_
  42.3 0.9 %shard_map.124 = (bf16[1536,384]{1,0:T(8,128)(2,1)S(1)}, f32[2,48,128]{2,1,0:T(8,128)S(1)}, bf16[2,256,128]{2,1,0:T(8,128)(2,1)S(1)}) custom-call(f32[8,128]{1,0:T(8,128)S(1)} %bitcast.22, f32[2,2,8,1664]{3,2,1,0:T(8,128)S(1)} %pad_maximum_fusion.2.refs_0_, f32[2,2,8,1664]{3,2,1,0:T(8,128)S(1)} %collective-permute-done.7.refs_1_, ...), custom_call_target="tpu_custom_call" | custom-call | tf_op jit(solution)/shard_map/pallas_call | solution.py:394
  43.3 0.5 collective-permute-start.22
  43.8 2.1 %collective-permute-done.3.refs_2_ = f32[4,2,8,1536]{3,2,1,0:T(8,128)S(1)} collective-permute-done((f32[4,2,8,1536]{3,2,1,0:T(8,128)S(1)}, f32[4,2,8,1536]{3,2,1,0:T(8,128)S(1)}, u32[]{:S(2)}, u32[]{:S(2)}) %collective-permute-start.3) | collective-permute-done | bytes 393248 | tf_op jit(solution)/shard_map/ppermute | solution.py:302
  45.9 10.8 %shard_map.125 = (f32[48,48,128]{2,1,0:T(8,128)}, f32[48,384]{1,0:T(8,128)S(1)}) custom-call(s32[48]{0:T(128)S(1)} %copy-done.3, f32[4,2,8,1536]{3,2,1,0:T(8,128)S(1)} %pad_maximum_fusion.refs_1_, f32[4,2,8,1536]{3,2,1,0:T(8,128)S(1)} %collective-permute-done.3.refs_2_, bf16[1536,384]{1,0:T(8,128)(2,1)S(1)} %get-tuple-element.22.refs_3_, ...), custom_call_target="tpu_custom_call" | custom-call | flops 10000000000 | bytes 10000000 | tf_op jit(solution)/shard_map/pallas_call | solution.py:407
  56.6 2.4 %collective-permute-start.10 = (f32[48,384]{1,0:T(8,128)S(1)}, f32[48,384]{1,0:T(8,128)S(1)}, u32[]{:S(2)}, u32[]{:S(2)}) collective-permute-start(f32[48,384]{1,0:T(8,128)S(1)} %get-tuple-element.25), channel_id=1, source_target_pairs={{0,8},{1,9},{2,10},{3,11},{4,12},{5,13},{6,14},{7,15},{8,0},{9,1},... | collective-permute-start | bytes 221192 | tf_op jit(solution)/shard_map/ppermute | solution.py:313
  59.1 3.5 %collective-permute-done.10 = f32[48,384]{1,0:T(8,128)S(1)} collective-permute-done((f32[48,384]{1,0:T(8,128)S(1)}, f32[48,384]{1,0:T(8,128)S(1)}, u32[]{:S(2)}, u32[]{:S(2)}) %collective-permute-start.10) | collective-permute-done | bytes 73760 | tf_op jit(solution)/shard_map/ppermute | solution.py:313
  62.6 2.0 %collective-permute-start.15 = (f32[2,48,384]{2,1,0:T(8,128)S(1)}, f32[2,48,384]{2,1,0:T(8,128)S(1)}, u32[]{:S(2)}, u32[]{:S(2)}) collective-permute-start(f32[2,48,384]{2,1,0:T(8,128)S(1)} %pad_maximum_fusion.5.refs_0_), channel_id=1, source_target_pairs={{0,2},{1,3},{2,4},{3,5},{4,6},{5,7},{6,0},{7,1},{8,10},{9,11},{10,... | collective-permute-start | bytes 442376 | tf_op jit(solution)/shard_map/ppermute | solution.py:322
  64.6 2.2 %collective-permute-start.12 = (f32[2,48,384]{2,1,0:T(8,128)S(1)}, f32[2,48,384]{2,1,0:T(8,128)S(1)}, u32[]{:S(2)}, u32[]{:S(2)}) collective-permute-start(f32[2,48,384]{2,1,0:T(8,128)S(1)} %pad_maximum_fusion.5.refs_0_), channel_id=1, source_target_pairs={{0,6},{1,7},{2,0},{3,1},{4,2},{5,3},{6,4},{7,5},{8,14},{9,15},{10,... | collective-permute-start | bytes 442376 | tf_op jit(solution)/shard_map/ppermute | solution.py:322
  66.8 1.1 %collective-permute-start.17 = (f32[2,48,384]{2,1,0:T(8,128)S(1)}, f32[2,48,384]{2,1,0:T(8,128)S(1)}, u32[]{:S(2)}, u32[]{:S(2)}) collective-permute-start(f32[2,48,384]{2,1,0:T(8,128)S(1)} %pad_maximum_fusion.5.refs_0_), channel_id=1, source_target_pairs={{0,1},{1,2},{2,3},{3,4},{4,5},{5,6},{6,7},{7,0},{8,9},{9,10},{10,1... | collective-permute-start | bytes 442376 | tf_op jit(solution)/shard_map/ppermute | solution.py:322
  67.9 2.1 %collective-permute-start.11 = (f32[2,48,384]{2,1,0:T(8,128)S(1)}, f32[2,48,384]{2,1,0:T(8,128)S(1)}, u32[]{:S(2)}, u32[]{:S(2)}) collective-permute-start(f32[2,48,384]{2,1,0:T(8,128)S(1)} %pad_maximum_fusion.5.refs_0_), channel_id=1, source_target_pairs={{0,7},{1,0},{2,1},{3,2},{4,3},{5,4},{6,5},{7,6},{8,15},{9,8},{10,9... | collective-permute-start | bytes 442376 | tf_op jit(solution)/shard_map/ppermute | solution.py:322
  70.0 2.6 %collective-permute-done.15.refs_6_ = f32[2,48,384]{2,1,0:T(8,128)S(1)} collective-permute-done((f32[2,48,384]{2,1,0:T(8,128)S(1)}, f32[2,48,384]{2,1,0:T(8,128)S(1)}, u32[]{:S(2)}, u32[]{:S(2)}) %collective-permute-start.15) | collective-permute-done | bytes 147488 | tf_op jit(solution)/shard_map/ppermute | solution.py:322
  72.7 2.1 %collective-permute-start.16 = (f32[2,48,384]{2,1,0:T(8,128)S(1)}, f32[2,48,384]{2,1,0:T(8,128)S(1)}, u32[]{:S(2)}, u32[]{:S(2)}) collective-permute-start(f32[2,48,384]{2,1,0:T(8,128)S(1)} %collective-permute-done.15.refs_6_), channel_id=1, source_target_pairs={{0,1},{1,2},{2,3},{3,4},{4,5},{5,6},{6,7},{7,0},{8,9},{9,10},{10,1... | collective-permute-start | bytes 442376 | tf_op jit(solution)/shard_map/ppermute | solution.py:322
  74.8 0.0 collective-permute-done.12.refs_2_
  74.8 1.0 %collective-permute-start.14 = (f32[2,48,384]{2,1,0:T(8,128)S(1)}, f32[2,48,384]{2,1,0:T(8,128)S(1)}, u32[]{:S(2)}, u32[]{:S(2)}) collective-permute-start(f32[2,48,384]{2,1,0:T(8,128)S(1)} %collective-permute-done.12.refs_2_), channel_id=1, source_target_pairs={{0,6},{1,7},{2,0},{3,1},{4,2},{5,3},{6,4},{7,5},{8,14},{9,15},{10,... | collective-permute-start | bytes 442376 | tf_op jit(solution)/shard_map/ppermute | solution.py:322
  75.7 0.0 collective-permute-done.22.refs_3_
  75.7 1.9 %collective-permute-start.13 = (f32[2,48,384]{2,1,0:T(8,128)S(1)}, f32[2,48,384]{2,1,0:T(8,128)S(1)}, u32[]{:S(2)}, u32[]{:S(2)}) collective-permute-start(f32[2,48,384]{2,1,0:T(8,128)S(1)} %collective-permute-done.12.refs_2_), channel_id=1, source_target_pairs={{0,7},{1,0},{2,1},{3,2},{4,3},{5,4},{6,5},{7,6},{8,15},{9,8},{10,9... | collective-permute-start | bytes 442376 | tf_op jit(solution)/shard_map/ppermute | solution.py:322
  77.7 0.6 shard_map.126
  78.3 0.0 collective-permute-done.11.refs_1_
  78.3 2.7 %collective-permute-done.16.refs_5_ = f32[2,48,384]{2,1,0:T(8,128)S(1)} collective-permute-done((f32[2,48,384]{2,1,0:T(8,128)S(1)}, f32[2,48,384]{2,1,0:T(8,128)S(1)}, u32[]{:S(2)}, u32[]{:S(2)}) %collective-permute-start.16) | collective-permute-done | bytes 147488 | tf_op jit(solution)/shard_map/ppermute | solution.py:322
  81.0 1.4 %collective-permute-done.14.refs_4_ = f32[2,48,384]{2,1,0:T(8,128)S(1)} collective-permute-done((f32[2,48,384]{2,1,0:T(8,128)S(1)}, f32[2,48,384]{2,1,0:T(8,128)S(1)}, u32[]{:S(2)}, u32[]{:S(2)}) %collective-permute-start.14) | collective-permute-done | bytes 147488 | tf_op jit(solution)/shard_map/ppermute | solution.py:322
  82.5 1.5 %collective-permute-done.13.refs_3_ = f32[2,48,384]{2,1,0:T(8,128)S(1)} collective-permute-done((f32[2,48,384]{2,1,0:T(8,128)S(1)}, f32[2,48,384]{2,1,0:T(8,128)S(1)}, u32[]{:S(2)}, u32[]{:S(2)}) %collective-permute-start.13) | collective-permute-done | bytes 147488 | tf_op jit(solution)/shard_map/ppermute | solution.py:322
  84.0 3.4 %shard_map.127 = f32[8,48,64]{2,1,0:T(8,128)} custom-call(f32[2,48,384]{2,1,0:T(8,128)S(1)} %pad_maximum_fusion.5.refs_0_, f32[2,48,384]{2,1,0:T(8,128)S(1)} %collective-permute-done.11.refs_1_, f32[2,48,384]{2,1,0:T(8,128)S(1)} %collective-permute-done.12.refs_2_, f32[2,48,384]{2,1,0:T(8,128)S(1)} %collective-permute-done.13.refs_3_, ...), custom_call_target="tpu_custom_call" | custom-call | tf_op jit(solution)/shard_map/pallas_call | solution.py:434
  (20 shorter events, 0.2 us)
Async XLA Ops:
  2.4 15.1 %collective-permute-start = (f32[8,1536]{1,0:T(8,128)S(1)}, f32[8,1536]{1,0:T(8,128)S(1)}, u32[]{:S(2)}, u32[]{:S(2)}) collective-permute-start(f32[8,1536]{1,0:T(8,128)S(1)} %get-tuple-element.18), channel_id=1, source_target_pairs={{0,8},{1,9},{2,10},{3,11},{4,12},{5,13},{6,14},{7,15},{8,0},{9,1},... | collective-permute-start | bytes 147464 | tf_op jit(solution)/shard_map/ppermute | solution.py:304
  5.7 14.4 %collective-permute-start.4 = (f32[8,1664]{1,0:T(8,128)S(1)}, f32[8,1664]{1,0:T(8,128)S(1)}, u32[]{:S(2)}, u32[]{:S(2)}) collective-permute-start(f32[8,1664]{1,0:T(8,128)S(1)} %get-tuple-element.19), channel_id=1, source_target_pairs={{0,0},{1,16},{2,32},{3,48},{4,64},{5,80},{6,96},{7,112},{8,128},{9... | collective-permute-start | bytes 159752 | tf_op jit(solution)/shard_map/ppermute | solution.py:379
  14.7 5.3 %collective-permute-start.18 = (f32[48,512]{1,0:T(8,128)S(1)}, f32[48,512]{1,0:T(8,128)S(1)}, u32[]{:S(2)}, u32[]{:S(2)}) collective-permute-start(f32[48,512]{1,0:T(8,128)S(1)} %get-tuple-element.27), channel_id=1, source_target_pairs={{0,32},{16,48},{32,0},{48,16},{64,96},{80,112},{96,64},{112,80},{1... | collective-permute-start | bytes 294920 | tf_op jit(solution)/shard_map/ppermute | solution.py:261
  17.5 10.2 %collective-permute-start.1 = (f32[2,8,1536]{2,1,0:T(8,128)S(1)}, f32[2,8,1536]{2,1,0:T(8,128)S(1)}, u32[]{:S(2)}, u32[]{:S(2)}) collective-permute-start(f32[2,8,1536]{2,1,0:T(8,128)S(1)} %get-tuple-element.35), channel_id=1, source_target_pairs={{0,4},{1,5},{2,6},{3,7},{4,0},{5,1},{6,2},{7,3},{8,12},{9,13},{10,... | collective-permute-start | bytes 294920 | tf_op jit(solution)/shard_map/ppermute | solution.py:302
  20.0 4.1 %collective-permute-start.5 = (f32[8,1664]{1,0:T(8,128)S(1)}, f32[8,1664]{1,0:T(8,128)S(1)}, u32[]{:S(2)}, u32[]{:S(2)}) collective-permute-start(f32[8,1664]{1,0:T(8,128)S(1)} %collective-permute-done.4), channel_id=1, source_target_pairs={{0,32},{16,48},{32,0},{48,16},{64,96},{80,112},{96,64},{112,80},{1... | collective-permute-start | bytes 159752 | tf_op jit(solution)/shard_map/ppermute | solution.py:261
  20.1 13.2 %collective-permute-start.19 = (f32[2,48,512]{2,1,0:T(8,128)S(1)}, f32[2,48,512]{2,1,0:T(8,128)S(1)}, u32[]{:S(2)}, u32[]{:S(2)}) collective-permute-start(f32[2,48,512]{2,1,0:T(8,128)S(1)} %pad_maximum_fusion.4), channel_id=1, source_target_pairs={{0,128},{16,144},{32,160},{48,176},{64,192},{80,208},{96,224},{112... | collective-permute-start | bytes 589832 | tf_op jit(solution)/shard_map/ppermute | solution.py:259
  24.2 6.7 %collective-permute-start.6 = (f32[2,8,1664]{2,1,0:T(8,128)S(1)}, f32[2,8,1664]{2,1,0:T(8,128)S(1)}, u32[]{:S(2)}, u32[]{:S(2)}) collective-permute-start(f32[2,8,1664]{2,1,0:T(8,128)S(1)} %pad_maximum_fusion.6), channel_id=1, source_target_pairs={{0,128},{16,144},{32,160},{48,176},{64,192},{80,208},{96,224},{112... | collective-permute-start | bytes 319496 | tf_op jit(solution)/shard_map/ppermute | solution.py:259
  27.7 14.6 %copy-start.2 = (f32[128,8]{0,1:T(8,128)S(1)}, f32[128,8]{0,1:T(8,128)}, u32[]{:S(2)}) copy-start(f32[128,8]{0,1:T(8,128)} %param.18) | copy-start | bytes 12292
  27.8 8.9 %collective-permute-start.2 = (f32[2,2,8,1536]{3,2,1,0:T(8,128)S(1)}, f32[2,2,8,1536]{3,2,1,0:T(8,128)S(1)}, u32[]{:S(2)}, u32[]{:S(2)}) collective-permute-start(f32[2,2,8,1536]{3,2,1,0:T(8,128)S(1)} %pad_maximum_fusion.3), channel_id=1, source_target_pairs={{0,6},{1,7},{2,0},{3,1},{4,2},{5,3},{6,4},{7,5},{8,14},{9,15},{10,... | collective-permute-start | bytes 589832 | tf_op jit(solution)/shard_map/ppermute | solution.py:302
  30.9 9.7 %collective-permute-start.7 = (f32[2,2,8,1664]{3,2,1,0:T(8,128)S(1)}, f32[2,2,8,1664]{3,2,1,0:T(8,128)S(1)}, u32[]{:S(2)}, u32[]{:S(2)}) collective-permute-start(f32[2,2,8,1664]{3,2,1,0:T(8,128)S(1)} %pad_maximum_fusion.2.refs_0_), channel_id=1, source_target_pairs={{0,192},{16,80},{32,224},{48,112},{64,0},{80,144},{96,32},{112,176... | collective-permute-start | bytes 638984 | tf_op jit(solution)/shard_map/ppermute | solution.py:259
  33.3 12.6 %copy-start.3 = (s32[48]{0:T(128)S(1)}, s32[48]{0:T(128)}, u32[]{:S(2)}) copy-start(s32[48]{0:T(128)} %refs_0_.1) | copy-start | bytes 580
  33.3 10.0 %collective-permute-start.20 = (f32[2,2,48,512]{3,2,1,0:T(8,128)S(1)}, f32[2,2,48,512]{3,2,1,0:T(8,128)S(1)}, u32[]{:S(2)}, u32[]{:S(2)}) collective-permute-start(f32[2,2,48,512]{3,2,1,0:T(8,128)S(1)} %pad_maximum_fusion.1.refs_0_), channel_id=1, source_target_pairs={{0,192},{16,80},{32,224},{48,112},{64,0},{80,144},{96,32},{112,176... | collective-permute-start | bytes 1179656 | tf_op jit(solution)/shard_map/ppermute | solution.py:259
  36.6 9.2 %collective-permute-start.3 = (f32[4,2,8,1536]{3,2,1,0:T(8,128)S(1)}, f32[4,2,8,1536]{3,2,1,0:T(8,128)S(1)}, u32[]{:S(2)}, u32[]{:S(2)}) collective-permute-start(f32[4,2,8,1536]{3,2,1,0:T(8,128)S(1)} %pad_maximum_fusion.refs_1_), channel_id=1, source_target_pairs={{0,7},{1,0},{2,1},{3,2},{4,3},{5,4},{6,5},{7,6},{8,15},{9,8},{10,9... | collective-permute-start | bytes 1179656 | tf_op jit(solution)/shard_map/ppermute | solution.py:302
  40.6 1.5 %collective-permute-start.8 = (f32[2,2,8,1664]{3,2,1,0:T(8,128)S(1)}, f32[2,2,8,1664]{3,2,1,0:T(8,128)S(1)}, u32[]{:S(2)}, u32[]{:S(2)}) collective-permute-start(f32[2,2,8,1664]{3,2,1,0:T(8,128)S(1)} %pad_maximum_fusion.2.refs_0_), channel_id=1, source_target_pairs={{0,16},{16,0},{32,48},{48,32},{64,80},{80,64},{96,112},{112,96},{1... | collective-permute-start | bytes 638984 | tf_op jit(solution)/shard_map/ppermute | solution.py:264
  40.6 1.8 %collective-permute-start.9 = (f32[2,2,8,1664]{3,2,1,0:T(8,128)S(1)}, f32[2,2,8,1664]{3,2,1,0:T(8,128)S(1)}, u32[]{:S(2)}, u32[]{:S(2)}) collective-permute-start(f32[2,2,8,1664]{3,2,1,0:T(8,128)S(1)} %collective-permute-done.7.refs_1_), channel_id=1, source_target_pairs={{0,16},{16,0},{32,48},{48,32},{64,80},{80,64},{96,112},{112,96},{1... | collective-permute-start | bytes 638984 | tf_op jit(solution)/shard_map/ppermute | solution.py:264
  41.1 26.8 %collective-permute-start.21 = (f32[2,2,48,512]{3,2,1,0:T(8,128)S(1)}, f32[2,2,48,512]{3,2,1,0:T(8,128)S(1)}, u32[]{:S(2)}, u32[]{:S(2)}) collective-permute-start(f32[2,2,48,512]{3,2,1,0:T(8,128)S(1)} %pad_maximum_fusion.1.refs_0_), channel_id=1, source_target_pairs={{0,16},{16,0},{32,48},{48,32},{64,80},{80,64},{96,112},{112,96},{1... | collective-permute-start | bytes 1179656 | tf_op jit(solution)/shard_map/ppermute | solution.py:264
  43.3 32.4 %collective-permute-start.22 = (f32[2,2,48,512]{3,2,1,0:T(8,128)S(1)}, f32[2,2,48,512]{3,2,1,0:T(8,128)S(1)}, u32[]{:S(2)}, u32[]{:S(2)}) collective-permute-start(f32[2,2,48,512]{3,2,1,0:T(8,128)S(1)} %collective-permute-done.20.refs_1_), channel_id=1, source_target_pairs={{0,16},{16,0},{32,48},{48,32},{64,80},{80,64},{96,112},{112,96},{1... | collective-permute-start | bytes 1179656 | tf_op jit(solution)/shard_map/ppermute | solution.py:264
  45.9 31.8 %copy-start.1 = (f32[64,256]{1,0:T(8,128)S(1)}, f32[64,256]{1,0:T(8,128)}, u32[]{:S(2)}) copy-start(f32[64,256]{1,0:T(8,128)} %gate_ref.1) | copy-start | bytes 196612
  56.6 27.3 %copy-start = (f32[8,48,64]{2,1,0:T(8,128)S(1)}, f32[8,48,64]{2,1,0:T(8,128)}, u32[]{:S(2)}) copy-start(f32[8,48,64]{2,1,0:T(8,128)} %refs_13_.1) | copy-start | bytes 294916
  56.6 5.9 %collective-permute-start.10 = (f32[48,384]{1,0:T(8,128)S(1)}, f32[48,384]{1,0:T(8,128)S(1)}, u32[]{:S(2)}, u32[]{:S(2)}) collective-permute-start(f32[48,384]{1,0:T(8,128)S(1)} %get-tuple-element.25), channel_id=1, source_target_pairs={{0,8},{1,9},{2,10},{3,11},{4,12},{5,13},{6,14},{7,15},{8,0},{9,1},... | collective-permute-start | bytes 221192 | tf_op jit(solution)/shard_map/ppermute | solution.py:313
  62.6 10.1 %collective-permute-start.15 = (f32[2,48,384]{2,1,0:T(8,128)S(1)}, f32[2,48,384]{2,1,0:T(8,128)S(1)}, u32[]{:S(2)}, u32[]{:S(2)}) collective-permute-start(f32[2,48,384]{2,1,0:T(8,128)S(1)} %pad_maximum_fusion.5.refs_0_), channel_id=1, source_target_pairs={{0,2},{1,3},{2,4},{3,5},{4,6},{5,7},{6,0},{7,1},{8,10},{9,11},{10,... | collective-permute-start | bytes 442376 | tf_op jit(solution)/shard_map/ppermute | solution.py:322
  64.6 10.1 %collective-permute-start.12 = (f32[2,48,384]{2,1,0:T(8,128)S(1)}, f32[2,48,384]{2,1,0:T(8,128)S(1)}, u32[]{:S(2)}, u32[]{:S(2)}) collective-permute-start(f32[2,48,384]{2,1,0:T(8,128)S(1)} %pad_maximum_fusion.5.refs_0_), channel_id=1, source_target_pairs={{0,6},{1,7},{2,0},{3,1},{4,2},{5,3},{6,4},{7,5},{8,14},{9,15},{10,... | collective-permute-start | bytes 442376 | tf_op jit(solution)/shard_map/ppermute | solution.py:322
  66.8 11.5 %collective-permute-start.17 = (f32[2,48,384]{2,1,0:T(8,128)S(1)}, f32[2,48,384]{2,1,0:T(8,128)S(1)}, u32[]{:S(2)}, u32[]{:S(2)}) collective-permute-start(f32[2,48,384]{2,1,0:T(8,128)S(1)} %pad_maximum_fusion.5.refs_0_), channel_id=1, source_target_pairs={{0,1},{1,2},{2,3},{3,4},{4,5},{5,6},{6,7},{7,0},{8,9},{9,10},{10,1... | collective-permute-start | bytes 442376 | tf_op jit(solution)/shard_map/ppermute | solution.py:322
  67.9 10.4 %collective-permute-start.11 = (f32[2,48,384]{2,1,0:T(8,128)S(1)}, f32[2,48,384]{2,1,0:T(8,128)S(1)}, u32[]{:S(2)}, u32[]{:S(2)}) collective-permute-start(f32[2,48,384]{2,1,0:T(8,128)S(1)} %pad_maximum_fusion.5.refs_0_), channel_id=1, source_target_pairs={{0,7},{1,0},{2,1},{3,2},{4,3},{5,4},{6,5},{7,6},{8,15},{9,8},{10,9... | collective-permute-start | bytes 442376 | tf_op jit(solution)/shard_map/ppermute | solution.py:322
  72.7 8.3 %collective-permute-start.16 = (f32[2,48,384]{2,1,0:T(8,128)S(1)}, f32[2,48,384]{2,1,0:T(8,128)S(1)}, u32[]{:S(2)}, u32[]{:S(2)}) collective-permute-start(f32[2,48,384]{2,1,0:T(8,128)S(1)} %collective-permute-done.15.refs_6_), channel_id=1, source_target_pairs={{0,1},{1,2},{2,3},{3,4},{4,5},{5,6},{6,7},{7,0},{8,9},{9,10},{10,1... | collective-permute-start | bytes 442376 | tf_op jit(solution)/shard_map/ppermute | solution.py:322
  74.8 7.7 %collective-permute-start.14 = (f32[2,48,384]{2,1,0:T(8,128)S(1)}, f32[2,48,384]{2,1,0:T(8,128)S(1)}, u32[]{:S(2)}, u32[]{:S(2)}) collective-permute-start(f32[2,48,384]{2,1,0:T(8,128)S(1)} %collective-permute-done.12.refs_2_), channel_id=1, source_target_pairs={{0,6},{1,7},{2,0},{3,1},{4,2},{5,3},{6,4},{7,5},{8,14},{9,15},{10,... | collective-permute-start | bytes 442376 | tf_op jit(solution)/shard_map/ppermute | solution.py:322
  75.7 8.2 %collective-permute-start.13 = (f32[2,48,384]{2,1,0:T(8,128)S(1)}, f32[2,48,384]{2,1,0:T(8,128)S(1)}, u32[]{:S(2)}, u32[]{:S(2)}) collective-permute-start(f32[2,48,384]{2,1,0:T(8,128)S(1)} %collective-permute-done.12.refs_2_), channel_id=1, source_target_pairs={{0,7},{1,0},{2,1},{3,2},{4,3},{5,4},{6,5},{7,6},{8,15},{9,8},{10,9... | collective-permute-start | bytes 442376 | tf_op jit(solution)/shard_map/ppermute | solution.py:322
